TPU v7x, 256 devices: a whole 4x4x8 slice. The times are simulated.
256 devices in a mesh: brick: 32 (over z, x), scene: 8 (over y, core).
Axes of the slice: x: 4, y: 4, z: 8, core: 2. Of those that a mesh axis runs over, the one named last changes fastest.
Arguments:
- features: float32 [8, 128, 64, 512], P('scene', 'brick'), may hold values from -6 to 6
- cotangent: float32 [8, 128, 64, 512], P('scene', 'brick'), may hold values from -6 to 6
- first_kernel: float32 [27, 64, 64], replicated, may hold values from -0.15625 to 0.15625
- second_kernel: float32 [27, 64, 64], replicated, may hold values from -0.15625 to 0.15625
- counts: int32 [32], P('brick'), may hold values from 1 to 4, as said below
- neighbours: int32 [128, 26], P('brick'), may hold values from -1 to 127, as said below
Outputs:
- out_features: float32 [8, 128, 64, 512], P('scene', 'brick')
- feature_grad: float32 [8, 128, 64, 512], P('scene', 'brick')
- first_grad: float32 [27, 64, 64], replicated
- second_grad: float32 [27, 64, 64], replicated
Inputs may be any that keep to these rules, and one draw needn't show every extreme that they name: Index d of brick owns counts[d] bricks in its slots 0 to counts[d] - 1; some index owns 4. `neighbours`: entries name occupied slots; the relation is symmetric (if slot t is the neighbour of s in direction (a, b, c), s is the neighbour of t in (-a, -b, -c)); unoccupied slots have only -1. A neighbour in a direction with c = 0 is owned by the same index of brick, with c = 1 by the same or the next index, with c = -1 by the same or the previous index.
All inputs are finite; a program needn't handle non-finite values.
Results may differ from a plain program's by a relative error of at most 0.0057.
Values may be sent and summed in bfloat16 or wider, within the bound.
No kernel may reach another device: no remote copies, remote signals or barrier semaphores. Data moves between devices by JAX's collectives and lax.ppermute only.
A program may use at most 128 MiB of HBM per device.

v0:
```python
import jax
import jax.numpy as jnp
from jax import lax
from jax.sharding import PartitionSpec as P

E = 8


offsets = [(a, b, c) for a in (-1, 0, 1) for b in (-1, 0, 1) for c in (-1, 0, 1)]
directions = [item for item in offsets if item != (0, 0, 0)]


def with_halo(shard, sides, width):
    for axis, dim in sides:
        devices, length = (lax.axis_size(axis), shard.shape[dim])
        up = [(i, (i + 1) % devices) for i in range(devices - 1)]
        down = [(j, i) for i, j in up]
        last = lax.slice_in_dim(shard, length - width, length, axis=dim)
        first = lax.slice_in_dim(shard, 0, width, axis=dim)
        before = lax.ppermute(last, axis, up)
        after = lax.ppermute(first, axis, down)
        shard = jnp.concatenate([before, shard, after], axis=dim)
    return shard


def source_range(offset, edge_cells):
    if offset < 0:
        return (edge_cells - 1, edge_cells)
    if offset == 0:
        return (0, edge_cells)
    return (0, 1)


def assemble(center, sources, indices, present, edge_cells):
    pieces = {}
    pieces[0, 0, 0] = center
    for number, (a, b, c) in enumerate(directions):
        source = sources[c + 1]
        range_i = source_range(a, edge_cells)
        range_j = source_range(b, edge_cells)
        depth_range = source_range(c, edge_cells) if c == 0 else (0, 1)
        slab_part = source[
            :, :, range_i[0] : range_i[1], range_j[0] : range_j[1], depth_range[0] : depth_range[1]
        ]
        last_row = source.shape[0] - 1
        chosen_rows = jnp.clip(indices[c + 1][:, number], 0, last_row).astype(jnp.int32)
        picked = jnp.take(slab_part, chosen_rows, axis=0)
        pieces[a, b, c] = jnp.where(
            present[:, number][:, None, None, None, None], picked, jnp.zeros_like(picked)
        )
    planes = []
    for a in (-1, 0, 1):
        lines = []
        for b in (-1, 0, 1):
            lines.append(jnp.concatenate([pieces[a, b, c] for c in (-1, 0, 1)], axis=4))
        planes.append(jnp.concatenate(lines, axis=3))
    return jnp.concatenate(planes, axis=2)


def columns_of(padded):
    lead_shape = padded.shape[:3]
    stacked = []
    for number in range(27):
        a, b, c = offsets[number]
        part = padded[..., 1 + a : 1 + a + E, 1 + b : 1 + b + E, 1 + c : 1 + c + E]
        stacked.append(part.reshape(lead_shape + (E * E * E,)))
    joined = jnp.stack(stacked, axis=2)
    return joined.reshape((lead_shape[0], lead_shape[1], 27 * lead_shape[2], E * E * E))


def apply_flat(columns, weight_flat):
    return jnp.einsum("ko,nskp->nsop", weight_flat, columns, preferred_element_type=jnp.float32)


def kernel_terms(columns, errors_b):
    total = jnp.einsum("nskp,nsop->ko", columns, errors_b, preferred_element_type=jnp.float32)
    return total.reshape(27, errors_b.shape[2], errors_b.shape[2])


def slope(values):
    sig = jax.nn.sigmoid(values)
    return sig * (1.0 + values * (1.0 - sig))


def body(features, cotangent, first_kernel, second_kernel, counts, neighbours):
    scenes_here, slots_here, channels, voxels = features.shape
    device_row = lax.axis_index("brick")
    occupied = (jnp.arange(slots_here, dtype=jnp.int32) < counts[0]).astype(jnp.float32)[
        None, :, None, None
    ]
    inputs = features * occupied
    upstream = cotangent * occupied
    present = neighbours >= 0
    index_mid = neighbours - device_row * slots_here
    index_low = index_mid + slots_here
    indices = (index_low, index_mid, index_mid)
    first_b = first_kernel.astype(jnp.bfloat16)
    second_b = second_kernel.astype(jnp.bfloat16)
    first_fwd = first_b.reshape(27 * channels, channels)
    second_fwd = second_b.reshape(27 * channels, channels)
    first_back = jnp.transpose(first_b[::-1], (0, 2, 1)).reshape(27 * channels, channels)
    second_back = jnp.transpose(second_b[::-1], (0, 2, 1)).reshape(27 * channels, channels)
    cube_shape = (scenes_here, slots_here, channels, E, E, E)

    def padded_of(values):
        rounded = values.astype(jnp.bfloat16)
        cubes = rounded.reshape(cube_shape)
        extended = with_halo(rounded, (("brick", 1),), slots_here)
        below = extended[:, :slots_here].reshape(cube_shape)[..., E - 1 : E]
        above = extended[:, 2 * slots_here :].reshape(cube_shape)[..., 0:1]
        pool_low = jnp.concatenate([below, cubes[..., E - 1 : E]], axis=1)
        pool_high = jnp.concatenate([cubes[..., 0:1], above], axis=1)

        def build(centre, lower_pool, upper_pool):
            return assemble(centre, (lower_pool, centre, upper_pool), indices, present, E)

        return columns_of(jax.vmap(build)(cubes, pool_low, pool_high))

    columns_in = padded_of(inputs)
    first_pre = apply_flat(columns_in, first_fwd)
    hidden = inputs + jax.nn.silu(first_pre)
    columns_hidden = padded_of(hidden)
    second_pre = apply_flat(columns_hidden, second_fwd)
    outputs = hidden + jax.nn.silu(second_pre)
    second_err = upstream * slope(second_pre)
    hidden_grad = upstream + apply_flat(padded_of(second_err), second_back)
    second_local = kernel_terms(columns_hidden, second_err.astype(jnp.bfloat16))
    first_err = hidden_grad * slope(first_pre)
    input_grad = hidden_grad + apply_flat(padded_of(first_err), first_back)
    first_local = kernel_terms(columns_in, first_err.astype(jnp.bfloat16))
    first_total, second_total = lax.psum((first_local, second_local), ("brick", "scene"))
    total_slots = (
        lax.axis_size("brick") * lax.axis_size("scene") * scenes_here * slots_here * voxels
    )
    scale = 1.0 / jnp.sqrt(jnp.float32(total_slots))
    return (outputs, input_grad, first_total * scale, second_total * scale)


def solution(mesh):
    return jax.shard_map(
        body,
        mesh=mesh,
        in_specs=(
            P("scene", "brick", None, None),
            P("scene", "brick", None, None),
            P(),
            P(),
            P("brick"),
            P("brick", None),
        ),
        out_specs=(P("scene", "brick", None, None), P("scene", "brick", None, None), P(), P()),
        check_vma=False,
    )
```

profile of v0, /device:TPU:1, one launch (start us, length us, event | category | flops | bytes accessed | tf_op | source)
XLA Modules:
  0.0 655.3 jit_solution(11767349416236179653)
XLA Ops:
  10.5 5.3 collective-permute-start
  68.7 2.7 maximum_maximum_fusion.5
  72.8 2.0 maximum_maximum_fusion
  76.1 2.0 copy.455
  78.0 2.0 copy.454
  80.9 3.3 fusion.271
  88.9 2.5 fusion.263
  91.5 2.0 copy.447
  93.5 2.0 copy.446
  105.9 2.3 fusion.262
  127.3 2.2 copy-done
  129.6 3.3 fusion.254
  134.3 4.2 collective-permute-start.2
  166.2 2.5 maximum_maximum_fusion.7
  170.0 2.4 maximum_maximum_fusion.1
  178.5 3.3 fusion.269
  181.8 2.0 copy.521
  186.6 2.5 fusion.261
  189.1 2.0 copy.518
  203.5 2.3 fusion.260
  225.3 3.9 multiply_convert_fusion.1
  229.2 3.8 fusion.4
  234.4 4.2 collective-permute-start.4
  266.2 2.5 maximum_maximum_fusion.9
  270.1 2.2 maximum_maximum_fusion.2
  278.4 3.3 fusion.267
  283.7 2.0 copy.591
  286.5 2.5 fusion.259
  289.1 2.0 copy.589
  303.5 2.3 fusion.258
  342.9 3.7 copy.607
  346.6 3.4 multiply_convert_fusion
  350.1 2.9 fusion.7
  354.3 4.9 collective-permute-start.6
  386.4 2.5 maximum_maximum_fusion.11
  390.2 2.0 maximum_maximum_fusion.3
  398.4 3.4 fusion.265
  403.8 2.0 copy.662
  406.7 2.6 fusion.257
  409.3 2.0 copy.660
  411.3 2.0 copy.659
  415.2 2.0 copy.657
  423.8 2.4 fusion.256
  430.7 2.0 copy.674
  445.3 3.2 fusion.11
  448.5 195.2 %all-reduce.3.cloned.1.call-done = (f32[27,64,64]{2,1,0:T(8,128)}, f32[27,64,64]{2,1,0:T(8,128)}) async-done(((f32[27,64,64]{2,1,0:T(8,128)}, f32[27,64,64]{2,1,0:T(8,128)}), (f32[27,64,64]{2,1,0:T(8,128)}, f32[27,64,64]{2,1,0:T(8,128)})) %all-reduce.3.cloned.1.call-update) | async-done | bytes 884752 | tf_op jit(solution)/shard_map/psum | solution.py:131
  643.7 2.2 broadcast_multiply_fusion.1
  645.9 2.2 broadcast_multiply_fusion
  (1395 shorter events, 311.3 us)
Async XLA Ops:
  7.2 26.1 %copy-start.98 = (f32[27,64,64]{2,1,0:T(8,128)S(1)}, f32[27,64,64]{2,1,0:T(8,128)}, u32[]{:S(2)}) copy-start(f32[27,64,64]{2,1,0:T(8,128)} %param.22) | copy-start | bytes 1327108
  7.2 26.2 %copy-start.99 = (f32[27,64,64]{2,1,0:T(8,128)S(1)}, f32[27,64,64]{2,1,0:T(8,128)}, u32[]{:S(2)}) copy-start(f32[27,64,64]{2,1,0:T(8,128)} %param.23) | copy-start | bytes 1327108
  7.2 636.5 %all-reduce.3.cloned.1.call-start = ((), (), s32[]{:S(2)}) async-start(), calls=%async_computation | async-start | bytes 3538944 | tf_op jit(solution)/shard_map/psum | solution.py:131
  9.2 40.8 %collective-permute-start.1 = (bf16[1,4,64,512]{3,2,1,0:T(8,128)(2,1)S(1)}, bf16[1,4,64,512]{3,2,1,0:T(8,128)(2,1)}, u32[]{:S(2)}, u32[]{:S(2)}) collective-permute-start(bf16[1,4,64,512]{3,2,1,0:T(8,128)(2,1)S(1)} %multiply_convert_fusion.2), channel_id=1, source_target_pairs={{8,0},{16,8},{24,16},{32,24},{40,32},{48,40},{56,48},{64,56},{72,6... | collective-permute-start | bytes 786440 | tf_op jit(solution)/shard_map/ppermute | solution.py:21
  10.5 37.6 %collective-permute-start = (bf16[1,4,64,512]{3,2,1,0:T(8,128)(2,1)S(1)}, bf16[1,4,64,512]{3,2,1,0:T(8,128)(2,1)}, u32[]{:S(2)}, u32[]{:S(2)}) collective-permute-start(bf16[1,4,64,512]{3,2,1,0:T(8,128)(2,1)S(1)} %multiply_convert_fusion.2), channel_id=1, source_target_pairs={{0,8},{8,16},{16,24},{24,32},{32,40},{40,48},{48,56},{56,64},{64,7... | collective-permute-start | bytes 786440 | tf_op jit(solution)/shard_map/ppermute | solution.py:20
  19.7 37.3 %copy-start.233 = (pred[4]{0:T(512)(128)(4,1)}, pred[4]{0:T(512)(128)(4,1)S(1)}, u32[]{:S(2)}) copy-start(pred[4]{0:T(512)(128)(4,1)S(1)} %get-tuple-element.336) | copy-start | bytes 16
  20.8 21.8 %copy-start.329 = (pred[4]{0:T(512)(128)(4,1)}, pred[4]{0:T(512)(128)(4,1)S(1)}, u32[]{:S(2)}) copy-start(pred[4]{0:T(512)(128)(4,1)S(1)} %compare_and_fusion.24) | copy-start | bytes 16
  21.3 19.8 %copy-start.253 = (pred[4]{0:T(512)(128)(4,1)}, pred[4]{0:T(512)(128)(4,1)S(1)}, u32[]{:S(2)}) copy-start(pred[4]{0:T(512)(128)(4,1)S(1)} %get-tuple-element.310) | copy-start | bytes 16
  21.9 20.1 %copy-start.249 = (pred[4]{0:T(512)(128)(4,1)}, pred[4]{0:T(512)(128)(4,1)S(1)}, u32[]{:S(2)}) copy-start(pred[4]{0:T(512)(128)(4,1)S(1)} %get-tuple-element.306) | copy-start | bytes 16
  22.4 21.1 %copy-start.153 = (pred[4]{0:T(512)(128)(4,1)}, pred[4]{0:T(512)(128)(4,1)S(1)}, u32[]{:S(2)}) copy-start(pred[4]{0:T(512)(128)(4,1)S(1)} %get-tuple-element.308) | copy-start | bytes 16
  23.0 20.4 %copy-start.157 = (pred[4]{0:T(512)(128)(4,1)}, pred[4]{0:T(512)(128)(4,1)S(1)}, u32[]{:S(2)}) copy-start(pred[4]{0:T(512)(128)(4,1)S(1)} %get-tuple-element.312) | copy-start | bytes 16
  24.2 19.1 %copy-start.165 = (pred[4]{0:T(512)(128)(4,1)}, pred[4]{0:T(512)(128)(4,1)S(1)}, u32[]{:S(2)}) copy-start(pred[4]{0:T(512)(128)(4,1)S(1)} %get-tuple-element.315) | copy-start | bytes 16
  24.7 17.2 %copy-start.257 = (pred[4]{0:T(512)(128)(4,1)}, pred[4]{0:T(512)(128)(4,1)S(1)}, u32[]{:S(2)}) copy-start(pred[4]{0:T(512)(128)(4,1)S(1)} %get-tuple-element.317) | copy-start | bytes 16
  25.3 22.7 %copy-start.161 = (pred[4]{0:T(512)(128)(4,1)}, pred[4]{0:T(512)(128)(4,1)S(1)}, u32[]{:S(2)}) copy-start(pred[4]{0:T(512)(128)(4,1)S(1)} %get-tuple-element.319) | copy-start | bytes 16
  26.1 16.6 %copy-start.177 = (pred[4]{0:T(512)(128)(4,1)}, pred[4]{0:T(512)(128)(4,1)S(1)}, u32[]{:S(2)}) copy-start(pred[4]{0:T(512)(128)(4,1)S(1)} %get-tuple-element.62) | copy-start | bytes 16
  26.1 21.9 %copy-start.121 = (pred[4]{0:T(512)(128)(4,1)}, pred[4]{0:T(512)(128)(4,1)S(1)}, u32[]{:S(2)}) copy-start(pred[4]{0:T(512)(128)(4,1)S(1)} %get-tuple-element.59) | copy-start | bytes 16
  26.1 30.1 %copy-start.173 = (pred[4]{0:T(512)(128)(4,1)}, pred[4]{0:T(512)(128)(4,1)S(1)}, u32[]{:S(2)}) copy-start(pred[4]{0:T(512)(128)(4,1)S(1)} %get-tuple-element.60) | copy-start | bytes 16
  27.1 14.8 %copy-start.209 = (pred[4]{0:T(512)(128)(4,1)}, pred[4]{0:T(512)(128)(4,1)S(1)}, u32[]{:S(2)}) copy-start(pred[4]{0:T(512)(128)(4,1)S(1)} %get-tuple-element.55) | copy-start | bytes 16
  27.1 14.9 %copy-start.205 = (pred[4]{0:T(512)(128)(4,1)}, pred[4]{0:T(512)(128)(4,1)S(1)}, u32[]{:S(2)}) copy-start(pred[4]{0:T(512)(128)(4,1)S(1)} %get-tuple-element.39) | copy-start | bytes 16
  27.1 16.3 %copy-start.141 = (pred[4]{0:T(512)(128)(4,1)}, pred[4]{0:T(512)(128)(4,1)S(1)}, u32[]{:S(2)}) copy-start(pred[4]{0:T(512)(128)(4,1)S(1)} %get-tuple-element.52) | copy-start | bytes 16
  27.1 16.4 %copy-start.137 = (pred[4]{0:T(512)(128)(4,1)}, pred[4]{0:T(512)(128)(4,1)S(1)}, u32[]{:S(2)}) copy-start(pred[4]{0:T(512)(128)(4,1)S(1)} %get-tuple-element.47) | copy-start | bytes 16
  27.1 16.5 %copy-start.133 = (pred[4]{0:T(512)(128)(4,1)}, pred[4]{0:T(512)(128)(4,1)S(1)}, u32[]{:S(2)}) copy-start(pred[4]{0:T(512)(128)(4,1)S(1)} %get-tuple-element.42) | copy-start | bytes 16
  27.1 28.3 %copy-start.201 = (pred[4]{0:T(512)(128)(4,1)}, pred[4]{0:T(512)(128)(4,1)S(1)}, u32[]{:S(2)}) copy-start(pred[4]{0:T(512)(128)(4,1)S(1)} %get-tuple-element.43) | copy-start | bytes 16
  27.1 30.0 %copy-start.197 = (pred[4]{0:T(512)(128)(4,1)}, pred[4]{0:T(512)(128)(4,1)S(1)}, u32[]{:S(2)}) copy-start(pred[4]{0:T(512)(128)(4,1)S(1)} %get-tuple-element.53) | copy-start | bytes 16
  28.4 19.0 %copy-start.321 = (s32[1024]{0:T(1024)}, s32[1024]{0:T(1024)S(1)}, u32[]{:S(2)}) copy-start(s32[1024]{0:T(1024)S(1)} %pad_clamp_fusion.21) | copy-start | bytes 12292
  43.5 28.0 %copy-start.33 = (bf16[1,4,64,8,1,8]{2,5,4,3,1,0:T(8,128)(2,1)}, bf16[1,4,64,8,1,8]{2,5,4,3,1,0:T(8,128)(2,1)S(1)}, u32[]{:S(2)}) copy-start(bf16[1,4,64,8,1,8]{2,5,4,3,1,0:T(8,128)(2,1)S(1)} %fusion.41) | copy-start | bytes 98308
  49.8 14.7 %copy-start.185 = (pred[4]{0:T(512)(128)(4,1)S(1)}, pred[4]{0:T(512)(128)(4,1)}, u32[]{:S(2)}) copy-start(pred[4]{0:T(512)(128)(4,1)} %get-tuple-element.51) | copy-start | bytes 16
  49.8 15.4 %copy-start.181 = (pred[4]{0:T(512)(128)(4,1)S(1)}, pred[4]{0:T(512)(128)(4,1)}, u32[]{:S(2)}) copy-start(pred[4]{0:T(512)(128)(4,1)} %get-tuple-element.46) | copy-start | bytes 16
  49.8 15.4 %copy-start.217 = (pred[4]{0:T(512)(128)(4,1)S(1)}, pred[4]{0:T(512)(128)(4,1)}, u32[]{:S(2)}) copy-start(pred[4]{0:T(512)(128)(4,1)} %get-tuple-element.311) | copy-start | bytes 16
  51.2 14.8 %copy-start.125 = (pred[4]{0:T(512)(128)(4,1)S(1)}, pred[4]{0:T(512)(128)(4,1)}, u32[]{:S(2)}) copy-start(pred[4]{0:T(512)(128)(4,1)} %get-tuple-element.49) | copy-start | bytes 16
  51.3 14.8 %copy-start.145 = (pred[4]{0:T(512)(128)(4,1)S(1)}, pred[4]{0:T(512)(128)(4,1)}, u32[]{:S(2)}) copy-start(pred[4]{0:T(512)(128)(4,1)} %get-tuple-element.313) | copy-start | bytes 16
  133.0 15.3 %collective-permute-start.3 = (bf16[1,4,64,512]{3,2,1,0:T(8,128)(2,1)}, bf16[1,4,64,512]{3,2,1,0:T(8,128)(2,1)S(1)}, u32[]{:S(2)}, u32[]{:S(2)}) collective-permute-start(bf16[1,4,64,512]{3,2,1,0:T(8,128)(2,1)} %get-tuple-element.285), channel_id=1, source_target_pairs={{8,0},{16,8},{24,16},{32,24},{40,32},{48,40},{56,48},{64,56},{72,6... | collective-permute-start | bytes 786440 | tf_op jit(solution)/shard_map/ppermute | solution.py:21
  134.3 13.1 %collective-permute-start.2 = (bf16[1,4,64,512]{3,2,1,0:T(8,128)(2,1)}, bf16[1,4,64,512]{3,2,1,0:T(8,128)(2,1)S(1)}, u32[]{:S(2)}, u32[]{:S(2)}) collective-permute-start(bf16[1,4,64,512]{3,2,1,0:T(8,128)(2,1)} %get-tuple-element.285), channel_id=1, source_target_pairs={{0,8},{8,16},{16,24},{24,32},{32,40},{40,48},{48,56},{56,64},{64,7... | collective-permute-start | bytes 786440 | tf_op jit(solution)/shard_map/ppermute | solution.py:20
  144.6 24.2 %copy-start.34 = (bf16[1,4,64,8,1,8]{2,5,4,3,1,0:T(8,128)(2,1)}, bf16[1,4,64,8,1,8]{2,5,4,3,1,0:T(8,128)(2,1)S(1)}, u32[]{:S(2)}) copy-start(bf16[1,4,64,8,1,8]{2,5,4,3,1,0:T(8,128)(2,1)S(1)} %fusion.35) | copy-start | bytes 98308
  148.7 14.8 %copy-start.182 = (pred[4]{0:T(512)(128)(4,1)S(1)}, pred[4]{0:T(512)(128)(4,1)}, u32[]{:S(2)}) copy-start(pred[4]{0:T(512)(128)(4,1)} %get-tuple-element.46) | copy-start | bytes 16
  148.7 14.8 %copy-start.218 = (pred[4]{0:T(512)(128)(4,1)S(1)}, pred[4]{0:T(512)(128)(4,1)}, u32[]{:S(2)}) copy-start(pred[4]{0:T(512)(128)(4,1)} %get-tuple-element.311) | copy-start | bytes 16
  233.1 15.2 %collective-permute-start.5 = (bf16[1,4,64,512]{3,2,1,0:T(8,128)(2,1)}, bf16[1,4,64,512]{3,2,1,0:T(8,128)(2,1)S(1)}, u32[]{:S(2)}, u32[]{:S(2)}) collective-permute-start(bf16[1,4,64,512]{3,2,1,0:T(8,128)(2,1)} %get-tuple-element.171), channel_id=1, source_target_pairs={{8,0},{16,8},{24,16},{32,24},{40,32},{48,40},{56,48},{64,56},{72,6... | collective-permute-start | bytes 786440 | tf_op jit(solution)/shard_map/ppermute | solution.py:21
  234.4 13.1 %collective-permute-start.4 = (bf16[1,4,64,512]{3,2,1,0:T(8,128)(2,1)}, bf16[1,4,64,512]{3,2,1,0:T(8,128)(2,1)S(1)}, u32[]{:S(2)}, u32[]{:S(2)}) collective-permute-start(bf16[1,4,64,512]{3,2,1,0:T(8,128)(2,1)} %get-tuple-element.171), channel_id=1, source_target_pairs={{0,8},{8,16},{16,24},{24,32},{32,40},{40,48},{48,56},{56,64},{64,7... | collective-permute-start | bytes 786440 | tf_op jit(solution)/shard_map/ppermute | solution.py:20
  244.7 24.1 %copy-start.35 = (bf16[1,4,64,8,1,8]{2,5,4,3,1,0:T(8,128)(2,1)}, bf16[1,4,64,8,1,8]{2,5,4,3,1,0:T(8,128)(2,1)S(1)}, u32[]{:S(2)}) copy-start(bf16[1,4,64,8,1,8]{2,5,4,3,1,0:T(8,128)(2,1)S(1)} %fusion.29) | copy-start | bytes 98308
  248.7 14.8 %copy-start.183 = (pred[4]{0:T(512)(128)(4,1)S(1)}, pred[4]{0:T(512)(128)(4,1)}, u32[]{:S(2)}) copy-start(pred[4]{0:T(512)(128)(4,1)} %get-tuple-element.46) | copy-start | bytes 16
  248.8 14.8 %copy-start.219 = (pred[4]{0:T(512)(128)(4,1)S(1)}, pred[4]{0:T(512)(128)(4,1)}, u32[]{:S(2)}) copy-start(pred[4]{0:T(512)(128)(4,1)} %get-tuple-element.311) | copy-start | bytes 16
  314.5 15.1 %copy-start.62 = (bf16[1,4,1,64,512]{4,3,1,2,0:T(8,128)(2,1)S(1)}, bf16[1,4,1,64,512]{4,3,1,2,0:T(8,128)(2,1)}, u32[]{:S(2)}) copy-start(bf16[1,4,1,64,512]{4,3,1,2,0:T(8,128)(2,1)} %copy.591) | copy-start | bytes 786436
  315.4 14.9 %copy-start.58 = (bf16[1,4,1,64,512]{4,3,1,2,0:T(8,128)(2,1)S(1)}, bf16[1,4,1,64,512]{4,3,1,2,0:T(8,128)(2,1)}, u32[]{:S(2)}) copy-start(bf16[1,4,1,64,512]{4,3,1,2,0:T(8,128)(2,1)} %copy.592) | copy-start | bytes 786436
  353.0 15.5 %collective-permute-start.7 = (bf16[1,4,64,512]{3,2,1,0:T(8,128)(2,1)S(1)}, bf16[1,4,64,512]{3,2,1,0:T(8,128)(2,1)S(1)}, u32[]{:S(2)}, u32[]{:S(2)}) collective-permute-start(bf16[1,4,64,512]{3,2,1,0:T(8,128)(2,1)S(1)} %get-tuple-element.287), channel_id=1, source_target_pairs={{8,0},{16,8},{24,16},{32,24},{40,32},{48,40},{56,48},{64,56},{72,6... | collective-permute-start | bytes 786440 | tf_op jit(solution)/shard_map/ppermute | solution.py:21
  354.3 13.3 %collective-permute-start.6 = (bf16[1,4,64,512]{3,2,1,0:T(8,128)(2,1)S(1)}, bf16[1,4,64,512]{3,2,1,0:T(8,128)(2,1)S(1)}, u32[]{:S(2)}, u32[]{:S(2)}) collective-permute-start(bf16[1,4,64,512]{3,2,1,0:T(8,128)(2,1)S(1)} %get-tuple-element.287), channel_id=1, source_target_pairs={{0,8},{8,16},{16,24},{24,32},{32,40},{40,48},{48,56},{56,64},{64,7... | collective-permute-start | bytes 786440 | tf_op jit(solution)/shard_map/ppermute | solution.py:20
  365.0 24.0 %copy-start.32 = (bf16[1,4,64,8,1,8]{2,5,4,3,1,0:T(8,128)(2,1)}, bf16[1,4,64,8,1,8]{2,5,4,3,1,0:T(8,128)(2,1)S(1)}, u32[]{:S(2)}) copy-start(bf16[1,4,64,8,1,8]{2,5,4,3,1,0:T(8,128)(2,1)S(1)} %fusion.23) | copy-start | bytes 98308
  368.9 14.8 %copy-start.184 = (pred[4]{0:T(512)(128)(4,1)S(1)}, pred[4]{0:T(512)(128)(4,1)}, u32[]{:S(2)}) copy-start(pred[4]{0:T(512)(128)(4,1)} %get-tuple-element.46) | copy-start | bytes 16
  368.9 14.8 %copy-start.220 = (pred[4]{0:T(512)(128)(4,1)S(1)}, pred[4]{0:T(512)(128)(4,1)}, u32[]{:S(2)}) copy-start(pred[4]{0:T(512)(128)(4,1)} %get-tuple-element.311) | copy-start | bytes 16
  (304 other events, 2572.2 us)
Sparse Core Ops, SparseCore 0:
  367.6 275.9 all-reduce.2
where the time goes:
time: 667 us; the launch traced here: 655 us
  local copies, waits for them, and re-layouts  330 us (49%)
  waiting for transfers between devices  195 us (29%)
  other arithmetic  63.3 us (9%)
  starting transfers between devices  23.7 us (4%)
  between operations  22.1 us (3%)
  matrix products  20.5 us (3%)
    psum x1, waiting for transfers between devices, body(): lax.psum((first_local, second_local), ('brick', 'scene'))  195 us
    another operation x112, local copies, waits for them, and re-layouts, columns_of(): joined = jnp.stack(stacked, axis=2)  148 us
    gather x104, local copies, waits for them, and re-layouts, assemble(): picked = jnp.take(slab_part, chosen_rows, axis=0)  70.4 us
    unnamed x805, local copies, waits for them, and re-layouts  57.1 us
    slice x16, local copies, waits for them, and re-layouts, columns_of(): part = padded[..., 1 + a:1 + a + E, 1 + b:1 + b + E, 1 + c:1 + c + E]  38.4 us
    ppermute x4, starting transfers between devices, with_halo(): before = lax.ppermute(last, axis, up)  18.5 us
    dot_general x4, matrix products, apply_flat(): jnp.einsum('ko,nskp->nsop', weight_flat, columns, preferred_element_type=...  13.8 us
  transfers between devices with their start and end apart: 9, of which 1 were waited for; matrix products, arithmetic and copies ran while one was open for 21% of the time, Pallas kernels for 0%

commit v1 on v0

v1 whole, which is shorter than its diff:
```python
import jax
import jax.numpy as jnp
from jax import lax
from jax.experimental import pallas as pl
from jax.experimental.pallas import tpu as pltpu
from jax.sharding import PartitionSpec as P

E = 8
C = 64
CAP = 4
f32 = jnp.float32
bf16 = jnp.bfloat16
offsets = [(a, b, c) for a in (-1, 0, 1) for b in (-1, 0, 1) for c in (-1, 0, 1)]
directions = [item for item in offsets if item != (0, 0, 0)]
number_of = {item: n for n, item in enumerate(directions)}

ROWS = CAP * 256
PLANE = CAP * 32
PACKED = 896


def row0(s, n, l):
    return s * 256 + (n // 2) * 128 + l * 16 + (n % 2) * 8


def flip(t):
    tt = t.T
    return jnp.concatenate([tt[:C], tt[C:]], axis=1)


def lane_low(shape):
    return lax.broadcasted_iota(jnp.int32, shape, 1) < C


def to_rows(x_ref, a_ref, tmp_ref, counts_ref):
    for s in range(CAP):
        occupied = jnp.where(s < counts_ref[0], 1.0, 0.0).astype(f32)
        for n in range(4):
            t = x_ref[0, s, :, n * 128 : (n + 1) * 128] * occupied
            tmp_ref[s * 4 + n] = flip(t)
            for l in range(E):
                a_ref[pl.ds(row0(s, n, l), 8), :] = tmp_ref[s * 4 + n, pl.ds(l, 8, stride=8), :]


def from_rows(a_ref, o_ref, tmp_ref):
    for s in range(CAP):
        for n in range(4):
            for l in range(E):
                tmp_ref[s * 4 + n, pl.ds(l, 8, stride=8), :] = a_ref[pl.ds(row0(s, n, l), 8), :]
            o_ref[0, s, :, n * 128 : (n + 1) * 128] = flip(tmp_ref[s * 4 + n])


def planes_out(a_ref, up_ref, down_ref):
    for s in range(CAP):
        for nh in range(2):
            base = s * 256 + nh * 128
            to = pl.ds(s * 32 + nh * 16, 16)
            up_ref[to, :] = a_ref[pl.ds(base + 7 * 16, 16), :].astype(bf16)
            down_ref[to, :] = a_ref[pl.ds(base, 16), :].astype(bf16)


def pre_kernel(counts_ref, x_ref, a_ref, up_ref, down_ref, tmp_ref):
    to_rows(x_ref, a_ref, tmp_ref, counts_ref)
    planes_out(a_ref, up_ref, down_ref)


def flat_weights(w_ref, o_ref, back):
    zero = jnp.zeros((C, C), f32)

    def block(a, b, c):
        k = 9 * (a + 1) + 3 * (b + 1) + (c + 1)
        return w_ref[26 - k].T if back else w_ref[k]

    for ci, c in enumerate((-1, 0, 1)):
        for bi, b in enumerate((-1, 0, 1)):
            low, mid, high = (block(a, b, c) for a in (-1, 0, 1))
            rows = ((mid, low), (high, mid), (zero, high), (low, zero))
            for r, (left, right) in enumerate(rows):
                joined = jnp.concatenate([left, right], axis=1).astype(bf16)
                o_ref[ci, pl.ds(bi * 256 + r * C, C), :] = joined


def prep_kernel(counts_ref, w1_ref, w2_ref, x_ref, f1_ref, f2_ref, b1_ref, b2_ref, u_ref, tmp_ref):
    flat_weights(w1_ref, f1_ref, False)
    flat_weights(w2_ref, f2_ref, False)
    flat_weights(w1_ref, b1_ref, True)
    flat_weights(w2_ref, b2_ref, True)
    to_rows(x_ref, u_ref, tmp_ref, counts_ref)


def build(a_ref, lo_ref, hi_ref, idx_ref, g_ref, pool_ref, x_ref):
    g_ref[pl.ds(0, ROWS), :] = a_ref[...]
    g_ref[pl.ds(ROWS, 256), :] = jnp.zeros((256, 128), f32)
    for side, (ref, layer) in enumerate(((lo_ref, 7), (hi_ref, 0))):
        for s in range(CAP):
            for nh in range(2):
                pool_ref[side, pl.ds(s * 32 + nh * 16, 16), :] = a_ref[
                    pl.ds(s * 256 + nh * 128 + layer * 16, 16), :
                ]
        pool_ref[side, pl.ds(PLANE, PLANE), :] = ref[...].astype(f32)
        pool_ref[side, pl.ds(2 * PLANE, 32), :] = jnp.zeros((32, 128), f32)
    row = lax.broadcasted_iota(jnp.int32, (8, 128), 0)
    low = lane_low((8, 128))

    def one_slot(s, carry):
        def tile(a, b, c, n, l):
            nh, nl = n // 2, n % 2
            if (a, b, c) == (0, 0, 0):
                base = s * 256
            else:
                base = idx_ref[s, number_of[a, b, c]]
            if c == 0:
                return g_ref[pl.ds(pl.multiple_of(base + (nh * 128 + l * 16 + nl * 8), 8), 8), :]
            side = 0 if c < 0 else 1
            return pool_ref[side, pl.ds(pl.multiple_of(base + (nh * 16 + nl * 8), 8), 8), :]

        def pair(b, c, n, l):
            full = tile(0, b, c, n, l)
            after = tile(0, b, c, n + 1, l) if n < 3 else tile(1, b, c, 0, l)
            before = tile(0, b, c, n - 1, l) if n > 0 else tile(-1, b, c, 3, l)
            return full, jnp.where(low, after, before)

        for nh in range(2):
            for ll in range(10):
                c = -1 if ll == 0 else (1 if ll == 9 else 0)
                parts = [[] for _ in range(6)]
                for nl in range(2):
                    n = 2 * nh + nl
                    own = pair(0, c, n, ll - 1)
                    left = pair(-1, c, n, ll - 1)
                    right = pair(1, c, n, ll - 1)
                    for h in range(2):
                        parts[h].append(pltpu.roll(jnp.where(row == 7, left[h], own[h]), 1, 0))
                        parts[2 + h].append(own[h])
                        parts[4 + h].append(pltpu.roll(jnp.where(row == 0, right[h], own[h]), 7, 0))
                for q in range(6):
                    x_ref[s, nh, ll, :, q * 128 : (q + 1) * 128] = jnp.concatenate(
                        parts[q], axis=0
                    ).astype(bf16)
        return carry

    lax.fori_loop(0, CAP, one_slot, 0)


def convolve(x_ref, w_ref, epilogue):
    def one_slot(s, carry):
        total = None
        for c in range(3):
            rows = x_ref[s, :, c : c + E].reshape(256, 768)
            term = jnp.dot(rows, w_ref[c], preferred_element_type=f32)
            total = term if total is None else total + term
        epilogue(pl.ds(pl.multiple_of(s * 256, 256), 256), total)
        return carry

    lax.fori_loop(0, CAP, one_slot, 0)


def logistic(v):
    return 1.0 / (1.0 + jnp.exp(-v))


def conv1_kernel(idx_ref, a_ref, lo_ref, hi_ref, w_ref, x_ref, h_ref, slope_ref, up_ref, down_ref, g_ref, pool_ref):
    build(a_ref, lo_ref, hi_ref, idx_ref, g_ref, pool_ref, x_ref)

    def epilogue(rows, v):
        q = logistic(v)
        h_ref[rows, :] = a_ref[rows, :] + v * q
        slope_ref[rows, :] = q * (1.0 + v * (1.0 - q))

    convolve(x_ref, w_ref, epilogue)
    planes_out(h_ref, up_ref, down_ref)


def conv2_kernel(
    idx_ref, a_ref, lo_ref, hi_ref, w_ref, u_ref, x_ref, o_ref, e_ref, up_ref, down_ref, g_ref, pool_ref
):
    build(a_ref, lo_ref, hi_ref, idx_ref, g_ref, pool_ref, x_ref)

    def epilogue(rows, v):
        q = logistic(v)
        o_ref[rows, :] = a_ref[rows, :] + v * q
        e_ref[rows, :] = u_ref[rows, :] * (q * (1.0 + v * (1.0 - q)))

    convolve(x_ref, w_ref, epilogue)
    planes_out(e_ref, up_ref, down_ref)


def conv3_kernel(
    idx_ref, a_ref, lo_ref, hi_ref, w_ref, u_ref, slope_ref, hg_ref, e_ref, up_ref, down_ref, g_ref, pool_ref, x_ref
):
    build(a_ref, lo_ref, hi_ref, idx_ref, g_ref, pool_ref, x_ref)

    def epilogue(rows, v):
        grad = u_ref[rows, :] + v
        hg_ref[rows, :] = grad
        e_ref[rows, :] = grad * slope_ref[rows, :]

    convolve(x_ref, w_ref, epilogue)
    planes_out(e_ref, up_ref, down_ref)


def conv4_kernel(idx_ref, a_ref, lo_ref, hi_ref, w_ref, hg_ref, o_ref, g_ref, pool_ref, x_ref, r_ref, tmp_ref):
    build(a_ref, lo_ref, hi_ref, idx_ref, g_ref, pool_ref, x_ref)

    def epilogue(rows, v):
        r_ref[rows, :] = hg_ref[rows, :] + v

    convolve(x_ref, w_ref, epilogue)
    from_rows(r_ref, o_ref, tmp_ref)


def weight_grad(x_ref, e_ref, p_ref):
    low = lane_low((C, 128))
    errors = e_ref[...].T.astype(bf16)
    held = None
    for c in range(3):
        rows = x_ref[:, :, c : c + E].reshape(ROWS, 768)
        m = jnp.dot(errors, rows, preferred_element_type=f32)
        for b in range(3):
            number = 3 * c + b
            z0, z1 = m[:C, b * 256 : b * 256 + 128], m[C:, b * 256 : b * 256 + 128]
            y0, y1 = m[:C, b * 256 + 128 : (b + 1) * 256], m[C:, b * 256 + 128 : (b + 1) * 256]
            p_ref[pl.ds(number * C, C), :] = (z0 + pltpu.roll(jnp.where(low, y1, z1), C, 1)).astype(p_ref.dtype)
            if number % 2 == 0:
                held = z1 + pltpu.roll(y0, C, 1)
                if number == 8:
                    p_ref[pl.ds((9 + number // 2) * C, C), :] = jnp.where(low, held, 0.0).astype(p_ref.dtype)
            else:
                odd = pltpu.roll(z1, C, 1) + y0
                p_ref[pl.ds((9 + number // 2) * C, C), :] = jnp.where(low, held, odd).astype(p_ref.dtype)


def w2_kernel(x_ref, e_ref, r_ref, o_ref, p_ref, tmp_ref):
    from_rows(r_ref, o_ref, tmp_ref)
    weight_grad(x_ref, e_ref, p_ref)


def w1_kernel(x_ref, e_ref, p_ref):
    weight_grad(x_ref, e_ref, p_ref)


def finish_kernel(scale, r_ref, first_ref, second_ref):
    for which, ref in enumerate((first_ref, second_ref)):
        for c in range(3):
            for b in range(3):
                number = 3 * c + b
                k = 3 * b + c
                t = (r_ref[pl.ds(which * PACKED + number * C, C), :].astype(f32) * scale).T
                ref[9 + k] = t[:C]
                ref[18 + k] = t[C:]
                if number % 2 == 0:
                    t = (r_ref[pl.ds(which * PACKED + (9 + number // 2) * C, C), :].astype(f32) * scale).T
                    held = t[C:]
                    ref[k] = t[:C]
                else:
                    ref[k] = held


VMEM = pl.BlockSpec(memory_space=pltpu.VMEM)
SMEM = pl.BlockSpec(memory_space=pltpu.SMEM)
FIELD = jax.ShapeDtypeStruct((ROWS, 128), f32)
PLANES = jax.ShapeDtypeStruct((PLANE, 128), bf16)
WINDOWS = (CAP, 2, 10, 16, 768)
WEIGHTS = jax.ShapeDtypeStruct((3, 768, 128), bf16)
CUBES = jax.ShapeDtypeStruct((1, CAP, C, E * E * E), f32)
POOLS = [pltpu.VMEM((ROWS + 256, 128), f32), pltpu.VMEM((2, 2 * PLANE + 32, 128), f32)]
TMP = pltpu.VMEM((16, C, 128), f32)


def call(kernel, name, scalars, arrays, outs, scratch=(), flops=0):
    moved = sum(x.size * x.dtype.itemsize for x in arrays) + sum(o.size * o.dtype.itemsize for o in outs)
    return pl.pallas_call(
        kernel,
        name=name,
        out_shape=outs,
        in_specs=[SMEM] * len(scalars) + [VMEM] * len(arrays),
        out_specs=[VMEM] * len(outs),
        scratch_shapes=list(scratch),
        cost_estimate=pl.CostEstimate(flops=flops, bytes_accessed=moved, transcendentals=0),
        compiler_params=pltpu.CompilerParams(vmem_limit_bytes=24 << 20),
    )(*scalars, *arrays)


def slot_table(neighbours):
    own = neighbours - lax.axis_index("brick") * CAP
    depth = jnp.array([item[2] for item in directions], jnp.int32)[None, :]
    inside = jnp.clip(own, 0, CAP - 1)
    below = jnp.where(own >= 0, inside, jnp.clip(own + 2 * CAP, CAP, 2 * CAP - 1))
    above = jnp.clip(own, 0, 2 * CAP - 1)
    present = neighbours >= 0
    middle = jnp.where(present, inside * 256, ROWS)
    outer = jnp.where(present, jnp.where(depth < 0, below, above) * 32, 2 * PLANE)
    return jnp.where(depth == 0, middle, outer).astype(jnp.int32)


def body(features, cotangent, first_kernel, second_kernel, counts, neighbours):
    bricks = lax.axis_size("brick")
    up_pairs = [(i, (i + 1) % bricks) for i in range(bricks)]
    down_pairs = [(j, i) for i, j in up_pairs]

    def exchange(up, down):
        return lax.ppermute(up, "brick", up_pairs), lax.ppermute(down, "brick", down_pairs)

    idx = slot_table(neighbours)
    windows = jax.ShapeDtypeStruct(WINDOWS, bf16)
    packed = jax.ShapeDtypeStruct((PACKED, 128), bf16)
    scratch_x = pltpu.VMEM(WINDOWS, bf16)
    work = 2 * ROWS * 2304 * 128

    inputs, up, down = call(pre_kernel, "pre", [counts], [features], [FIELD, PLANES, PLANES], [TMP])
    lo, hi = exchange(up, down)
    f1, f2, b1, b2, upstream = call(
        prep_kernel, "prep", [counts], [first_kernel, second_kernel, cotangent], [WEIGHTS] * 4 + [FIELD], [TMP]
    )
    x_in, hidden, slope1, up, down = call(
        conv1_kernel, "conv1", [idx], [inputs, lo, hi, f1], [windows, FIELD, FIELD, PLANES, PLANES], POOLS, work
    )
    lo, hi = exchange(up, down)
    x_hidden, out_rows, second_err, up, down = call(
        conv2_kernel,
        "conv2",
        [idx],
        [hidden, lo, hi, f2, upstream],
        [windows, FIELD, FIELD, PLANES, PLANES],
        POOLS,
        work,
    )
    lo, hi = exchange(up, down)
    outputs, second_local = call(w2_kernel, "w2", [], [x_hidden, second_err, out_rows], [CUBES, packed], [TMP], work)
    hidden_grad, first_err, up, down = call(
        conv3_kernel,
        "conv3",
        [idx],
        [second_err, lo, hi, b2, upstream, slope1],
        [FIELD, FIELD, PLANES, PLANES],
        POOLS + [scratch_x],
        work,
    )
    lo, hi = exchange(up, down)
    (first_local,) = call(w1_kernel, "w1", [], [x_in, first_err], [packed], (), work)
    (input_grad,) = call(
        conv4_kernel,
        "conv4",
        [idx],
        [first_err, lo, hi, b1, hidden_grad],
        [CUBES],
        POOLS + [scratch_x, pltpu.VMEM((ROWS, 128), f32), TMP],
        work,
    )
    axes = ("brick", "scene")
    devices = lax.axis_size("brick") * lax.axis_size("scene")
    share = 2 * PACKED // devices
    partial = jnp.concatenate([first_local, second_local]).reshape(devices, share, 128)
    partial = lax.all_to_all(partial, axes, 0, 0)
    mine = jnp.sum(partial.astype(f32), axis=0).astype(bf16)
    total = lax.all_to_all(jnp.broadcast_to(mine[None], (devices, share, 128)), axes, 0, 0)
    scale = float((devices * CAP * E * E * E) ** -0.5)
    grads = jax.ShapeDtypeStruct((27, C, C), f32)
    first_grad, second_grad = call(
        lambda *refs: finish_kernel(scale, *refs), "finish", [], [total.reshape(2 * PACKED, 128)], [grads, grads]
    )
    return (outputs, input_grad, first_grad, second_grad)


def solution(mesh):
    return jax.shard_map(
        body,
        mesh=mesh,
        in_specs=(
            P("scene", "brick", None, None),
            P("scene", "brick", None, None),
            P(),
            P(),
            P("brick"),
            P("brick", None),
        ),
        out_specs=(P("scene", "brick", None, None), P("scene", "brick", None, None), P(), P()),
        check_vma=False,
    )
```

time: 667 us -> 104 us (0.16); the launches traced: 655 us -> 104 us
  local copies, waits for them, and re-layouts: 330 us -> 5.58 us
  waiting for transfers between devices: 195 us -> 11.2 us
  other arithmetic: 63.3 us -> 1.01 us
  blocking collectives: 0 us -> 34.4 us
  between operations: 22.1 us -> 1.4 us
  matrix products: 20.5 us -> 0 us
  Pallas kernels: 0 us -> 18.6 us
  starting transfers between devices: 23.7 us -> 31.4 us
    psum x1 -> x0, waiting for transfers between devices: 195 us -> none  [body(): lax.psum((first_local, second_local), ('brick', 'scene'))]
    another operation x164 -> x0, local copies, waits for them, and re-layouts: 149 us -> none  [the longest x112 148 us: columns_of(): joined = jnp.stack(stacked, axis=2)]
    gather x104 -> x0, local copies, waits for them, and re-layouts: 70.4 us -> none  [assemble(): picked = jnp.take(slab_part, chosen_rows, axis=0)]
    unnamed x805 -> x8, local copies, waits for them, and re-layouts: 57.1 us -> 4.41 us
    slice x30 -> x0, local copies, waits for them, and re-layouts: 42.4 us -> none  [the longest x16 38.4 us: columns_of(): part = padded[..., 1 + a:1 + a + E, 1 + b:1 + b + E, 1 + c:1 + c + E]]
    all_to_all x0 -> x1, blocking collectives: none -> 34.4 us  [body(): partial = lax.all_to_all(partial, axes, 0, 0)]
    concatenate x24 -> x1, other arithmetic: 26.2 us -> 0.03 us  [body(): jnp.concatenate([first_local, second_local]).reshape(devices, share, 128)]
    dot_general x6 -> x0, matrix products: 20.5 us -> none  [the longest x4 13.8 us: apply_flat(): jnp.einsum('ko,nskp->nsop', weight_flat, columns, preferred_element_type=...]
  transfers between devices with their start and end apart: 9 -> 9, of which waited for: 1 -> 2; matrix products, arithmetic and copies ran while one was open for 21% -> 1% of each run, Pallas kernels for 0% -> 7%
where the time goes in v1:
time: 104 us
  blocking collectives  34.4 us (33%)
  starting transfers between devices  31.4 us (30%)
  Pallas kernels  18.6 us (18%)
  waiting for transfers between devices  11.2 us (11%)
  local copies, waits for them, and re-layouts  5.58 us (5%)
  between operations  1.4 us (1%)
    all_to_all x1, blocking collectives, body(): partial = lax.all_to_all(partial, axes, 0, 0)  34.4 us
    ppermute x4, starting transfers between devices, exchange(): lax.ppermute(down, 'brick', down_pairs)  21.6 us
    pallas_call x9, Pallas kernels, call(): pl.pallas_call(kernel, name=name, out_shape=outs, in_specs=[SMEM] * len(s...  18.6 us
    ppermute x4, waiting for transfers between devices, exchange(): lax.ppermute(up, 'brick', up_pairs)  11.2 us
    all_to_all x1, starting transfers between devices, body(): lax.all_to_all(jnp.broadcast_to(mine[None], (devices, share, 128)), axes,...  6.13 us
    unnamed x8, local copies, waits for them, and re-layouts  4.41 us
    ppermute x4, starting transfers between devices, exchange(): lax.ppermute(up, 'brick', up_pairs)  3.7 us
  transfers between devices with their start and end apart: 9, of which 2 were waited for; matrix products, arithmetic and copies ran while one was open for 1% of the time, Pallas kernels for 7%

profile of v1, /device:TPU:1, one launch (start us, length us, event | category | flops | bytes accessed | tf_op | source)
XLA Modules:
  0.0 103.6 jit_solution(10293377850918548326)
XLA Ops:
  1.3 0.0 copy-start.3
  1.3 1.0 copy-done.3
  2.3 0.5 pre.1
  2.9 2.1 %collective-permute-start = (bf16[128,128]{1,0:T(8,128)(2,1)S(1)}, bf16[128,128]{1,0:T(8,128)(2,1)S(1)}, u32[]{:S(2)}, u32[]{:S(2)}) collective-permute-start(bf16[128,128]{1,0:T(8,128)(2,1)S(1)} %get-tuple-element.31), channel_id=1, source_target_pairs={{0,8},{8,16},{16,24},{24,32},{32,40},{40,48},{48,56},{56,64},{64,7... | collective-permute-start | bytes 98312 | tf_op jit(solution)/shard_map/ppermute | solution.py:302
  5.0 6.6 %collective-permute-start.1 = (bf16[128,128]{1,0:T(8,128)(2,1)S(1)}, bf16[128,128]{1,0:T(8,128)(2,1)S(1)}, u32[]{:S(2)}, u32[]{:S(2)}) collective-permute-start(bf16[128,128]{1,0:T(8,128)(2,1)S(1)} %get-tuple-element.32), channel_id=1, source_target_pairs={{8,0},{16,8},{24,16},{32,24},{40,32},{48,40},{56,48},{64,56},{72,6... | collective-permute-start | bytes 98312 | tf_op jit(solution)/shard_map/ppermute | solution.py:302
  11.6 0.7 select_select_fusion.idx_ref
  12.3 0.0 copy-start
  12.3 1.2 %copy-done = f32[27,64,64]{2,1,0:T(8,128)S(1)} copy-done((f32[27,64,64]{2,1,0:T(8,128)S(1)}, f32[27,64,64]{2,1,0:T(8,128)}, u32[]{:S(2)}) %copy-start) | copy-done | bytes 442392
  13.5 0.0 copy-start.1
  13.5 1.2 %copy-done.1 = f32[27,64,64]{2,1,0:T(8,128)S(1)} copy-done((f32[27,64,64]{2,1,0:T(8,128)S(1)}, f32[27,64,64]{2,1,0:T(8,128)}, u32[]{:S(2)}) %copy-start.1) | copy-done | bytes 442392
  14.7 0.0 copy-start.2
  14.7 1.0 %copy-done.2 = f32[1,4,64,512]{3,2,1,0:T(8,128)S(1)} copy-done((f32[1,4,64,512]{3,2,1,0:T(8,128)S(1)}, f32[1,4,64,512]{3,2,1,0:T(8,128)}, u32[]{:S(2)}) %copy-start.2) | copy-done | bytes 524312
  15.7 1.2 %prep.1 = (bf16[3,768,128]{2,1,0:T(8,128)(2,1)S(1)}, bf16[3,768,128]{2,1,0:T(8,128)(2,1)S(1)}, bf16[3,768,128]{2,1,0:T(8,128)(2,1)S(1)}, bf16[3,768,128]{2,1,0:T(8,128)(2,1)S(1)}, f32[1024,128]{1,0:T(8,128)S(1)}) custom-call(s32[1]{0:T(128)S(6)} %copy.11.counts_ref, f32[27,64,64]{2,1,0:T(8,128)S(1)} %copy-done, f32[27,64,64]{2,1,0:T(8,128)S(1)} %copy-done.1, ...), custom_call_target="tpu_custom_call" | custom-call | bytes 4292608 | tf_op jit(solution)/shard_map/prep/pallas_call | solution.py:272
  17.0 0.0 collective-permute-done.lo_ref
  17.0 0.0 collective-permute-done.1.hi_ref
  17.0 2.9 %conv1.1 = (bf16[4,2,10,16,768]{4,3,2,1,0:T(8,128)(2,1)S(1)}, f32[1024,128]{1,0:T(8,128)S(1)}, f32[1024,128]{1,0:T(8,128)S(1)}, bf16[128,128]{1,0:T(8,128)(2,1)S(1)}, bf16[128,128]{1,0:T(8,128)(2,1)S(1)}) custom-call(s32[4,26]{1,0:T(4,128)S(1)} %select_select_fusion.idx_ref, f32[1024,128]{1,0:T(8,128)S(1)} %get-tuple-element.30.a_ref, ...), custom_call_target="tpu_custom_call" | custom-call | flops 603979776 | bytes 4259840 | tf_op jit(solution)/shard_map/conv1/pallas_call | solution.py:272
  19.9 0.1 collective-permute-start.2
  20.0 4.8 %collective-permute-start.3 = (bf16[128,128]{1,0:T(8,128)(2,1)S(1)}, bf16[128,128]{1,0:T(8,128)(2,1)S(1)}, u32[]{:S(2)}, u32[]{:S(2)}) collective-permute-start(bf16[128,128]{1,0:T(8,128)(2,1)S(1)} %get-tuple-element.36), channel_id=1, source_target_pairs={{8,0},{16,8},{24,16},{32,24},{40,32},{48,40},{56,48},{64,56},{72,6... | collective-permute-start | bytes 98312 | tf_op jit(solution)/shard_map/ppermute | solution.py:302
  24.8 1.3 %collective-permute-done.2.lo_ref = bf16[128,128]{1,0:T(8,128)(2,1)S(1)} collective-permute-done((bf16[128,128]{1,0:T(8,128)(2,1)S(1)}, bf16[128,128]{1,0:T(8,128)(2,1)S(1)}, u32[]{:S(2)}, u32[]{:S(2)}) %collective-permute-start.2) | collective-permute-done | bytes 32800 | tf_op jit(solution)/shard_map/ppermute | solution.py:302
  26.1 0.0 collective-permute-done.3.hi_ref
  26.1 2.9 %conv2.1 = (bf16[4,2,10,16,768]{4,3,2,1,0:T(8,128)(2,1)S(1)}, f32[1024,128]{1,0:T(8,128)S(1)}, f32[1024,128]{1,0:T(8,128)S(1)}, bf16[128,128]{1,0:T(8,128)(2,1)S(1)}, bf16[128,128]{1,0:T(8,128)(2,1)S(1)}) custom-call(s32[4,26]{1,0:T(4,128)S(1)} %select_select_fusion.idx_ref, f32[1024,128]{1,0:T(8,128)S(1)} %get-tuple-element.34.a_ref, ...), custom_call_target="tpu_custom_call" | custom-call | flops 603979776 | bytes 4784128 | tf_op jit(solution)/shard_map/conv2/pallas_call | solution.py:272
  29.0 0.1 collective-permute-start.4
  29.1 4.9 %collective-permute-start.5 = (bf16[128,128]{1,0:T(8,128)(2,1)S(1)}, bf16[128,128]{1,0:T(8,128)(2,1)S(1)}, u32[]{:S(2)}, u32[]{:S(2)}) collective-permute-start(bf16[128,128]{1,0:T(8,128)(2,1)S(1)} %get-tuple-element.44), channel_id=1, source_target_pairs={{8,0},{16,8},{24,16},{32,24},{40,32},{48,40},{56,48},{64,56},{72,6... | collective-permute-start | bytes 98312 | tf_op jit(solution)/shard_map/ppermute | solution.py:302
  33.9 1.5 %w2.1 = (f32[1,4,64,512]{3,2,1,0:T(8,128)}, bf16[896,128]{1,0:T(8,128)(2,1)S(1)}) custom-call(bf16[4,2,10,16,768]{4,3,2,1,0:T(8,128)(2,1)S(1)} %get-tuple-element.39.x_ref, f32[1024,128]{1,0:T(8,128)S(1)} %get-tuple-element.40.e_ref.a_ref, f32[1024,128]{1,0:T(8,128)S(1)} %get-tuple-element.41.r_ref), custom_call_target="tpu_custom_call" | custom-call | flops 603979776 | bytes 3768320 | tf_op jit(solution)/shard_map/w2/pallas_call | solution.py:272
  35.4 0.0 collective-permute-done.4.lo_ref
  35.4 0.0 collective-permute-done.5.hi_ref
  35.4 2.8 %conv3.1 = (f32[1024,128]{1,0:T(8,128)S(1)}, f32[1024,128]{1,0:T(8,128)S(1)}, bf16[128,128]{1,0:T(8,128)(2,1)S(1)}, bf16[128,128]{1,0:T(8,128)(2,1)S(1)}) custom-call(s32[4,26]{1,0:T(4,128)S(1)} %select_select_fusion.idx_ref, f32[1024,128]{1,0:T(8,128)S(1)} %get-tuple-element.40.e_ref.a_ref, bf16[128,128]{1,0:T(8,128)(2,1)S(1)} %collective-permute-done.4.lo_ref, ...), custom_call_target="tpu_custom_call" | custom-call | flops 603979776 | bytes 3342336 | tf_op jit(solution)/shard_map/conv3/pallas_call | solution.py:272
  38.3 0.9 w1.1
  39.2 0.1 reshape.19
  39.4 34.4 %all_to_all.10 = bf16[256,7,128]{2,1,0:T(8,128)(2,1)S(1)} all-to-all(bf16[256,7,128]{2,1,0:T(8,128)(2,1)S(1)} %reshape.19), channel_id=1, replica_groups=mesh['brick'=32,'scene'=8] {'brick','scene'}, dimensions={0} | all-to-all | bytes 917504 | tf_op jit(solution)/shard_map/all_to_all | solution.py:354
  73.8 0.3 reduce_sum.12
  74.1 0.9 broadcast_in_dim.28
  74.9 6.1 %all-to-all-start.1 = ((bf16[256,7,128]{2,1,0:T(8,128)(2,1)}), bf16[256,7,128]{2,1,0:T(8,128)(2,1)S(1)}, u32[]{:S(2)}, u32[]{:S(2)}) async-start(bf16[256,7,128]{2,1,0:T(8,128)(2,1)} %broadcast_in_dim.28), calls=%async_computation.1 | async-start | bytes 1048576 | tf_op jit(solution)/shard_map/all_to_all | solution.py:356
  81.1 1.4 %collective-permute-start.6 = (bf16[128,128]{1,0:T(8,128)(2,1)S(1)}, bf16[128,128]{1,0:T(8,128)(2,1)S(1)}, u32[]{:S(2)}, u32[]{:S(2)}) collective-permute-start(bf16[128,128]{1,0:T(8,128)(2,1)S(1)} %get-tuple-element.48), channel_id=1, source_target_pairs={{0,8},{8,16},{16,24},{24,32},{32,40},{40,48},{48,56},{56,64},{64,7... | collective-permute-start | bytes 98312 | tf_op jit(solution)/shard_map/ppermute | solution.py:302
  82.5 5.3 %collective-permute-start.7 = (bf16[128,128]{1,0:T(8,128)(2,1)S(1)}, bf16[128,128]{1,0:T(8,128)(2,1)S(1)}, u32[]{:S(2)}, u32[]{:S(2)}) collective-permute-start(bf16[128,128]{1,0:T(8,128)(2,1)S(1)} %get-tuple-element.49), channel_id=1, source_target_pairs={{8,0},{16,8},{24,16},{32,24},{40,32},{48,40},{56,48},{64,56},{72,6... | collective-permute-start | bytes 98312 | tf_op jit(solution)/shard_map/ppermute | solution.py:302
  87.8 9.9 %collective-permute-done.6.lo_ref = bf16[128,128]{1,0:T(8,128)(2,1)S(1)} collective-permute-done((bf16[128,128]{1,0:T(8,128)(2,1)S(1)}, bf16[128,128]{1,0:T(8,128)(2,1)S(1)}, u32[]{:S(2)}, u32[]{:S(2)}) %collective-permute-start.6) | collective-permute-done | bytes 32800 | tf_op jit(solution)/shard_map/ppermute | solution.py:302
  97.7 0.0 collective-permute-done.7.hi_ref
  97.7 4.1 %conv4.1 = f32[1,4,64,512]{3,2,1,0:T(8,128)} custom-call(s32[4,26]{1,0:T(4,128)S(1)} %select_select_fusion.idx_ref, f32[1024,128]{1,0:T(8,128)S(1)} %get-tuple-element.47.a_ref.e_ref, bf16[128,128]{1,0:T(8,128)(2,1)S(1)} %collective-permute-done.6.lo_ref, bf16[128,128]{1,0:T(8,128)(2,1)S(1)} %collective-permute-done.7.hi_ref, ...), custom_call_target="tpu_custom_call" | custom-call | flops 603979776 | bytes 2228224 | tf_op jit(solution)/shard_map/conv4/pallas_call | solution.py:272
  101.8 0.0 all-to-all-done.1
  101.8 0.2 reshape.20.refs_0_
  102.0 1.6 %finish.1 = (f32[27,64,64]{2,1,0:T(8,128)}, f32[27,64,64]{2,1,0:T(8,128)}) custom-call(bf16[1792,128]{1,0:T(8,128)(2,1)S(1)} %reshape.20.refs_0_), custom_call_target="tpu_custom_call" | custom-call | bytes 1343488 | tf_op jit(solution)/shard_map/finish/pallas_call | solution.py:272
  (1 shorter events, 0.0 us)
Async XLA Ops:
  1.3 1.0 %copy-start.3 = (f32[1,4,64,512]{3,2,1,0:T(8,128)S(1)}, f32[1,4,64,512]{3,2,1,0:T(8,128)}, u32[]{:S(2)}) copy-start(f32[1,4,64,512]{3,2,1,0:T(8,128)} %x_ref.2) | copy-start | bytes 1572868
  2.9 14.1 %collective-permute-start = (bf16[128,128]{1,0:T(8,128)(2,1)S(1)}, bf16[128,128]{1,0:T(8,128)(2,1)S(1)}, u32[]{:S(2)}, u32[]{:S(2)}) collective-permute-start(bf16[128,128]{1,0:T(8,128)(2,1)S(1)} %get-tuple-element.31), channel_id=1, source_target_pairs={{0,8},{8,16},{16,24},{24,32},{32,40},{40,48},{48,56},{56,64},{64,7... | collective-permute-start | bytes 98312 | tf_op jit(solution)/shard_map/ppermute | solution.py:302
  5.0 12.0 %collective-permute-start.1 = (bf16[128,128]{1,0:T(8,128)(2,1)S(1)}, bf16[128,128]{1,0:T(8,128)(2,1)S(1)}, u32[]{:S(2)}, u32[]{:S(2)}) collective-permute-start(bf16[128,128]{1,0:T(8,128)(2,1)S(1)} %get-tuple-element.32), channel_id=1, source_target_pairs={{8,0},{16,8},{24,16},{32,24},{40,32},{48,40},{56,48},{64,56},{72,6... | collective-permute-start | bytes 98312 | tf_op jit(solution)/shard_map/ppermute | solution.py:302
  12.3 1.2 %copy-start = (f32[27,64,64]{2,1,0:T(8,128)S(1)}, f32[27,64,64]{2,1,0:T(8,128)}, u32[]{:S(2)}) copy-start(f32[27,64,64]{2,1,0:T(8,128)} %w1_ref.1) | copy-start | bytes 1327108
  13.5 1.2 %copy-start.1 = (f32[27,64,64]{2,1,0:T(8,128)S(1)}, f32[27,64,64]{2,1,0:T(8,128)}, u32[]{:S(2)}) copy-start(f32[27,64,64]{2,1,0:T(8,128)} %w2_ref.1) | copy-start | bytes 1327108
  14.7 1.0 %copy-start.2 = (f32[1,4,64,512]{3,2,1,0:T(8,128)S(1)}, f32[1,4,64,512]{3,2,1,0:T(8,128)}, u32[]{:S(2)}) copy-start(f32[1,4,64,512]{3,2,1,0:T(8,128)} %x_ref.3) | copy-start | bytes 1572868
  19.9 6.2 %collective-permute-start.2 = (bf16[128,128]{1,0:T(8,128)(2,1)S(1)}, bf16[128,128]{1,0:T(8,128)(2,1)S(1)}, u32[]{:S(2)}, u32[]{:S(2)}) collective-permute-start(bf16[128,128]{1,0:T(8,128)(2,1)S(1)} %get-tuple-element.35), channel_id=1, source_target_pairs={{0,8},{8,16},{16,24},{24,32},{32,40},{40,48},{48,56},{56,64},{64,7... | collective-permute-start | bytes 98312 | tf_op jit(solution)/shard_map/ppermute | solution.py:302
  20.0 6.1 %collective-permute-start.3 = (bf16[128,128]{1,0:T(8,128)(2,1)S(1)}, bf16[128,128]{1,0:T(8,128)(2,1)S(1)}, u32[]{:S(2)}, u32[]{:S(2)}) collective-permute-start(bf16[128,128]{1,0:T(8,128)(2,1)S(1)} %get-tuple-element.36), channel_id=1, source_target_pairs={{8,0},{16,8},{24,16},{32,24},{40,32},{48,40},{56,48},{64,56},{72,6... | collective-permute-start | bytes 98312 | tf_op jit(solution)/shard_map/ppermute | solution.py:302
  29.0 6.4 %collective-permute-start.4 = (bf16[128,128]{1,0:T(8,128)(2,1)S(1)}, bf16[128,128]{1,0:T(8,128)(2,1)S(1)}, u32[]{:S(2)}, u32[]{:S(2)}) collective-permute-start(bf16[128,128]{1,0:T(8,128)(2,1)S(1)} %get-tuple-element.43), channel_id=1, source_target_pairs={{0,8},{8,16},{16,24},{24,32},{32,40},{40,48},{48,56},{56,64},{64,7... | collective-permute-start | bytes 98312 | tf_op jit(solution)/shard_map/ppermute | solution.py:302
  29.1 6.3 %collective-permute-start.5 = (bf16[128,128]{1,0:T(8,128)(2,1)S(1)}, bf16[128,128]{1,0:T(8,128)(2,1)S(1)}, u32[]{:S(2)}, u32[]{:S(2)}) collective-permute-start(bf16[128,128]{1,0:T(8,128)(2,1)S(1)} %get-tuple-element.44), channel_id=1, source_target_pairs={{8,0},{16,8},{24,16},{32,24},{40,32},{48,40},{56,48},{64,56},{72,6... | collective-permute-start | bytes 98312 | tf_op jit(solution)/shard_map/ppermute | solution.py:302
  74.9 26.9 %all-to-all-start.1 = ((bf16[256,7,128]{2,1,0:T(8,128)(2,1)}), bf16[256,7,128]{2,1,0:T(8,128)(2,1)S(1)}, u32[]{:S(2)}, u32[]{:S(2)}) async-start(bf16[256,7,128]{2,1,0:T(8,128)(2,1)} %broadcast_in_dim.28), calls=%async_computation.1 | async-start | bytes 1048576 | tf_op jit(solution)/shard_map/all_to_all | solution.py:356
  81.1 16.6 %collective-permute-start.6 = (bf16[128,128]{1,0:T(8,128)(2,1)S(1)}, bf16[128,128]{1,0:T(8,128)(2,1)S(1)}, u32[]{:S(2)}, u32[]{:S(2)}) collective-permute-start(bf16[128,128]{1,0:T(8,128)(2,1)S(1)} %get-tuple-element.48), channel_id=1, source_target_pairs={{0,8},{8,16},{16,24},{24,32},{32,40},{40,48},{48,56},{56,64},{64,7... | collective-permute-start | bytes 98312 | tf_op jit(solution)/shard_map/ppermute | solution.py:302
  82.5 15.2 %collective-permute-start.7 = (bf16[128,128]{1,0:T(8,128)(2,1)S(1)}, bf16[128,128]{1,0:T(8,128)(2,1)S(1)}, u32[]{:S(2)}, u32[]{:S(2)}) collective-permute-start(bf16[128,128]{1,0:T(8,128)(2,1)S(1)} %get-tuple-element.49), channel_id=1, source_target_pairs={{8,0},{16,8},{24,16},{32,24},{40,32},{48,40},{56,48},{64,56},{72,6... | collective-permute-start | bytes 98312 | tf_op jit(solution)/shard_map/ppermute | solution.py:302

commit v2 on v1

--- a/solution.py
+++ b/solution.py
@@ -80,11 +80,20 @@
                 o_ref[ci, pl.ds(bi * 256 + r * C, C), :] = joined
 
 
-def prep_kernel(counts_ref, w1_ref, w2_ref, x_ref, f1_ref, f2_ref, b1_ref, b2_ref, u_ref, tmp_ref):
+def prep_kernel(
+    counts_ref, w1_hbm, w2_hbm, x_hbm, f1_ref, f2_ref, b1_ref, b2_ref, u_ref, tmp_ref, w1_ref, w2_ref, x_ref, sems
+):
+    pairs = ((w1_hbm, w1_ref), (w2_hbm, w2_ref), (x_hbm, x_ref))
+    copies = [pltpu.make_async_copy(src, dst, sems.at[n]) for n, (src, dst) in enumerate(pairs)]
+    for copy in copies:
+        copy.start()
+    copies[0].wait()
     flat_weights(w1_ref, f1_ref, False)
+    flat_weights(w1_ref, b1_ref, True)
+    copies[1].wait()
     flat_weights(w2_ref, f2_ref, False)
-    flat_weights(w1_ref, b1_ref, True)
     flat_weights(w2_ref, b2_ref, True)
+    copies[2].wait()
     to_rows(x_ref, u_ref, tmp_ref, counts_ref)
 
 
@@ -258,6 +267,7 @@
 
 VMEM = pl.BlockSpec(memory_space=pltpu.VMEM)
 SMEM = pl.BlockSpec(memory_space=pltpu.SMEM)
+HBM = pl.BlockSpec(memory_space=pltpu.HBM)
 FIELD = jax.ShapeDtypeStruct((ROWS, 128), f32)
 PLANES = jax.ShapeDtypeStruct((PLANE, 128), bf16)
 WINDOWS = (CAP, 2, 10, 16, 768)
@@ -267,13 +277,13 @@
 TMP = pltpu.VMEM((16, C, 128), f32)
 
 
-def call(kernel, name, scalars, arrays, outs, scratch=(), flops=0):
+def call(kernel, name, scalars, arrays, outs, scratch=(), flops=0, place=VMEM):
     moved = sum(x.size * x.dtype.itemsize for x in arrays) + sum(o.size * o.dtype.itemsize for o in outs)
     return pl.pallas_call(
         kernel,
         name=name,
         out_shape=outs,
-        in_specs=[SMEM] * len(scalars) + [VMEM] * len(arrays),
+        in_specs=[SMEM] * len(scalars) + [place] * len(arrays),
         out_specs=[VMEM] * len(outs),
         scratch_shapes=list(scratch),
         cost_estimate=pl.CostEstimate(flops=flops, bytes_accessed=moved, transcendentals=0),
@@ -310,7 +320,19 @@
     inputs, up, down = call(pre_kernel, "pre", [counts], [features], [FIELD, PLANES, PLANES], [TMP])
     lo, hi = exchange(up, down)
     f1, f2, b1, b2, upstream = call(
-        prep_kernel, "prep", [counts], [first_kernel, second_kernel, cotangent], [WEIGHTS] * 4 + [FIELD], [TMP]
+        prep_kernel,
+        "prep",
+        [counts],
+        [pltpu.with_memory_space_constraint(v, pltpu.HBM) for v in (first_kernel, second_kernel, cotangent)],
+        [WEIGHTS] * 4 + [FIELD],
+        [
+            TMP,
+            pltpu.VMEM((27, C, C), f32),
+            pltpu.VMEM((27, C, C), f32),
+            pltpu.VMEM((1, CAP, C, E * E * E), f32),
+            pltpu.SemaphoreType.DMA((3,)),
+        ],
+        place=HBM,
     )
     x_in, hidden, slope1, up, down = call(
         conv1_kernel, "conv1", [idx], [inputs, lo, hi, f1], [windows, FIELD, FIELD, PLANES, PLANES], POOLS, work
@@ -348,12 +370,30 @@
         work,
     )
     axes = ("brick", "scene")
-    devices = lax.axis_size("brick") * lax.axis_size("scene")
-    share = 2 * PACKED // devices
-    partial = jnp.concatenate([first_local, second_local]).reshape(devices, share, 128)
-    partial = lax.all_to_all(partial, axes, 0, 0)
-    mine = jnp.sum(partial.astype(f32), axis=0).astype(bf16)
-    total = lax.all_to_all(jnp.broadcast_to(mine[None], (devices, share, 128)), axes, 0, 0)
+    scenes = lax.axis_size("scene")
+    devices = bricks * scenes
+    row = 4 if bricks % 4 == 0 else 1
+    near, far = row * scenes, bricks // row
+    near_groups = [list(range(z * near, (z + 1) * near)) for z in range(far)]
+    far_groups = [[x + row * z for z in range(far)] for x in range(row)]
+    share = 2 * PACKED // near
+
+    def near_exchange(blocks):
+        return lax.all_to_all(blocks, axes, 0, 0, axis_index_groups=near_groups, tiled=True)
+
+    def far_exchange(blocks):
+        return lax.all_to_all(blocks, "brick", 0, 0, axis_index_groups=far_groups, tiled=True)
+
+    def total_of(blocks):
+        return jnp.sum(blocks.astype(f32), axis=0).astype(bf16)
+
+    def spread(block, count):
+        return jnp.broadcast_to(block[None], (count,) + block.shape)
+
+    partial = jnp.concatenate([first_local, second_local]).reshape(near, share, 128)
+    mine = total_of(near_exchange(partial))
+    mine = total_of(far_exchange(spread(mine, far)))
+    total = near_exchange(spread(mine, near))
     scale = float((devices * CAP * E * E * E) ** -0.5)
     grads = jax.ShapeDtypeStruct((27, C, C), f32)
     first_grad, second_grad = call(

time: 104 us -> 91.6 us (0.88)
  waiting for transfers between devices: 11.2 us -> 4.24 us
  local copies, waits for them, and re-layouts: 5.58 us -> 1.88 us
  starting transfers between devices: 31.4 us -> 28.1 us
  Pallas kernels: 18.6 us -> 20 us
    ppermute x4, waiting for transfers between devices: 11.2 us -> 2.91 us  [exchange(): lax.ppermute(up, 'brick', up_pairs)]
    unnamed x8 -> x2, local copies, waits for them, and re-layouts: 4.41 us -> 1.03 us
    ppermute x4, starting transfers between devices: 21.6 us -> 19.7 us  [exchange(): lax.ppermute(down, 'brick', down_pairs)]
    all_to_all x1, starting transfers between devices: 6.13 us -> 4.71 us  [near_exchange(): lax.all_to_all(blocks, axes, 0, 0, axis_index_groups=near_groups, tiled=T...]
    pallas_call x9, Pallas kernels: 18.6 us -> 20 us  [call(): pl.pallas_call(kernel, name=name, out_shape=outs, in_specs=[SMEM] * len(s...]
    ppermute x4, waiting for transfers between devices: 0.01 us -> 1.33 us  [exchange(): lax.ppermute(down, 'brick', down_pairs)]
    all_to_all x1 -> x2, blocking collectives: 34.4 us -> 34.8 us  [the longest x1 18.4 us: near_exchange(): lax.all_to_all(blocks, axes, 0, 0, axis_index_groups=near_groups, tiled=T...]
  transfers between devices with their start and end apart: 9 -> 9, of which waited for: 2 -> 3; matrix products, arithmetic and copies ran while one was open for 1% -> 1% of each run, Pallas kernels for 7% -> 9%
where the time goes in v2:
time: 91.6 us; the launch traced here: 91.3 us
  blocking collectives  34.8 us (38%)
  starting transfers between devices  28.1 us (31%)
  Pallas kernels  20 us (22%)
  waiting for transfers between devices  4.24 us (5%)
  local copies, waits for them, and re-layouts  1.88 us (2%)
  between operations  1.4 us (2%)
    pallas_call x9, Pallas kernels, call(): pl.pallas_call(kernel, name=name, out_shape=outs, in_specs=[SMEM] * len(s...  20 us
    ppermute x4, starting transfers between devices, exchange(): lax.ppermute(down, 'brick', down_pairs)  19.7 us
    all_to_all x1, blocking collectives, near_exchange(): lax.all_to_all(blocks, axes, 0, 0, axis_index_groups=near_groups, tiled=T...  18.4 us
    all_to_all x1, blocking collectives, far_exchange(): lax.all_to_all(blocks, 'brick', 0, 0, axis_index_groups=far_groups, tiled...  16.4 us
    all_to_all x1, starting transfers between devices, near_exchange(): lax.all_to_all(blocks, axes, 0, 0, axis_index_groups=near_groups, tiled=T...  4.71 us
    ppermute x4, starting transfers between devices, exchange(): lax.ppermute(up, 'brick', up_pairs)  3.76 us
    ppermute x4, waiting for transfers between devices, exchange(): lax.ppermute(up, 'brick', up_pairs)  2.91 us
  transfers between devices with their start and end apart: 9, of which 3 were waited for; matrix products, arithmetic and copies ran while one was open for 1% of the time, Pallas kernels for 9%

profile of v2, /device:TPU:1, one launch (start us, length us, event | category | flops | bytes accessed | tf_op | source)
XLA Modules:
  0.0 91.3 jit_solution(15709299655701619303)
XLA Ops:
  1.3 0.0 copy-start
  1.3 1.0 %copy-done = f32[1,4,64,512]{3,2,1,0:T(8,128)S(1)} copy-done((f32[1,4,64,512]{3,2,1,0:T(8,128)S(1)}, f32[1,4,64,512]{3,2,1,0:T(8,128)}, u32[]{:S(2)}) %copy-start) | copy-done | bytes 524312
  2.3 0.5 pre.1
  2.9 2.1 %collective-permute-start = (bf16[128,128]{1,0:T(8,128)(2,1)S(1)}, bf16[128,128]{1,0:T(8,128)(2,1)S(1)}, u32[]{:S(2)}, u32[]{:S(2)}) collective-permute-start(bf16[128,128]{1,0:T(8,128)(2,1)S(1)} %get-tuple-element.31), channel_id=1, source_target_pairs={{0,8},{8,16},{16,24},{24,32},{32,40},{40,48},{48,56},{56,64},{64,7... | collective-permute-start | bytes 98312 | tf_op jit(solution)/shard_map/ppermute | solution.py:312
  5.0 6.6 %collective-permute-start.1 = (bf16[128,128]{1,0:T(8,128)(2,1)S(1)}, bf16[128,128]{1,0:T(8,128)(2,1)S(1)}, u32[]{:S(2)}, u32[]{:S(2)}) collective-permute-start(bf16[128,128]{1,0:T(8,128)(2,1)S(1)} %get-tuple-element.32), channel_id=1, source_target_pairs={{8,0},{16,8},{24,16},{32,24},{40,32},{48,40},{56,48},{64,56},{72,6... | collective-permute-start | bytes 98312 | tf_op jit(solution)/shard_map/ppermute | solution.py:312
  11.6 0.7 select_select_fusion.idx_ref
  12.3 2.6 %prep.1 = (bf16[3,768,128]{2,1,0:T(8,128)(2,1)S(1)}, bf16[3,768,128]{2,1,0:T(8,128)(2,1)S(1)}, bf16[3,768,128]{2,1,0:T(8,128)(2,1)S(1)}, bf16[3,768,128]{2,1,0:T(8,128)(2,1)S(1)}, f32[1024,128]{1,0:T(8,128)S(1)}) custom-call(s32[1]{0:T(128)S(6)} %copy.11.counts_ref, f32[27,64,64]{2,1,0:T(8,128)} %w1_hbm.1, f32[27,64,64]{2,1,0:T(8,128)} %w2_hbm.1, ...), custom_call_target="tpu_custom_call" | custom-call | bytes 4292608 | tf_op jit(solution)/shard_map/prep/pallas_call | solution.py:282
  15.0 0.0 collective-permute-done.lo_ref
  15.0 0.0 collective-permute-done.1.hi_ref
  15.0 2.9 %conv1.1 = (bf16[4,2,10,16,768]{4,3,2,1,0:T(8,128)(2,1)S(1)}, f32[1024,128]{1,0:T(8,128)S(1)}, f32[1024,128]{1,0:T(8,128)S(1)}, bf16[128,128]{1,0:T(8,128)(2,1)S(1)}, bf16[128,128]{1,0:T(8,128)(2,1)S(1)}) custom-call(s32[4,26]{1,0:T(4,128)S(1)} %select_select_fusion.idx_ref, f32[1024,128]{1,0:T(8,128)S(1)} %get-tuple-element.30.a_ref, ...), custom_call_target="tpu_custom_call" | custom-call | flops 603979776 | bytes 4259840 | tf_op jit(solution)/shard_map/conv1/pallas_call | solution.py:282
  17.9 0.1 collective-permute-start.2
  18.0 4.8 %collective-permute-start.3 = (bf16[128,128]{1,0:T(8,128)(2,1)S(1)}, bf16[128,128]{1,0:T(8,128)(2,1)S(1)}, u32[]{:S(2)}, u32[]{:S(2)}) collective-permute-start(bf16[128,128]{1,0:T(8,128)(2,1)S(1)} %get-tuple-element.36), channel_id=1, source_target_pairs={{8,0},{16,8},{24,16},{32,24},{40,32},{48,40},{56,48},{64,56},{72,6... | collective-permute-start | bytes 98312 | tf_op jit(solution)/shard_map/ppermute | solution.py:312
  22.8 1.3 %collective-permute-done.2.lo_ref = bf16[128,128]{1,0:T(8,128)(2,1)S(1)} collective-permute-done((bf16[128,128]{1,0:T(8,128)(2,1)S(1)}, bf16[128,128]{1,0:T(8,128)(2,1)S(1)}, u32[]{:S(2)}, u32[]{:S(2)}) %collective-permute-start.2) | collective-permute-done | bytes 32800 | tf_op jit(solution)/shard_map/ppermute | solution.py:312
  24.1 0.0 collective-permute-done.3.hi_ref
  24.1 2.9 %conv2.1 = (bf16[4,2,10,16,768]{4,3,2,1,0:T(8,128)(2,1)S(1)}, f32[1024,128]{1,0:T(8,128)S(1)}, f32[1024,128]{1,0:T(8,128)S(1)}, bf16[128,128]{1,0:T(8,128)(2,1)S(1)}, bf16[128,128]{1,0:T(8,128)(2,1)S(1)}) custom-call(s32[4,26]{1,0:T(4,128)S(1)} %select_select_fusion.idx_ref, f32[1024,128]{1,0:T(8,128)S(1)} %get-tuple-element.34.a_ref, ...), custom_call_target="tpu_custom_call" | custom-call | flops 603979776 | bytes 4784128 | tf_op jit(solution)/shard_map/conv2/pallas_call | solution.py:282
  27.0 0.1 collective-permute-start.4
  27.1 4.9 %collective-permute-start.5 = (bf16[128,128]{1,0:T(8,128)(2,1)S(1)}, bf16[128,128]{1,0:T(8,128)(2,1)S(1)}, u32[]{:S(2)}, u32[]{:S(2)}) collective-permute-start(bf16[128,128]{1,0:T(8,128)(2,1)S(1)} %get-tuple-element.44), channel_id=1, source_target_pairs={{8,0},{16,8},{24,16},{32,24},{40,32},{48,40},{56,48},{64,56},{72,6... | collective-permute-start | bytes 98312 | tf_op jit(solution)/shard_map/ppermute | solution.py:312
  32.0 1.5 %w2.1 = (f32[1,4,64,512]{3,2,1,0:T(8,128)}, bf16[896,128]{1,0:T(8,128)(2,1)S(1)}) custom-call(bf16[4,2,10,16,768]{4,3,2,1,0:T(8,128)(2,1)S(1)} %get-tuple-element.39.x_ref, f32[1024,128]{1,0:T(8,128)S(1)} %get-tuple-element.40.e_ref.a_ref, f32[1024,128]{1,0:T(8,128)S(1)} %get-tuple-element.41.r_ref), custom_call_target="tpu_custom_call" | custom-call | flops 603979776 | bytes 3768320 | tf_op jit(solution)/shard_map/w2/pallas_call | solution.py:282
  33.4 0.0 collective-permute-done.4.lo_ref
  33.4 0.0 collective-permute-done.5.hi_ref
  33.4 2.8 %conv3.1 = (f32[1024,128]{1,0:T(8,128)S(1)}, f32[1024,128]{1,0:T(8,128)S(1)}, bf16[128,128]{1,0:T(8,128)(2,1)S(1)}, bf16[128,128]{1,0:T(8,128)(2,1)S(1)}) custom-call(s32[4,26]{1,0:T(4,128)S(1)} %select_select_fusion.idx_ref, f32[1024,128]{1,0:T(8,128)S(1)} %get-tuple-element.40.e_ref.a_ref, bf16[128,128]{1,0:T(8,128)(2,1)S(1)} %collective-permute-done.4.lo_ref, ...), custom_call_target="tpu_custom_call" | custom-call | flops 603979776 | bytes 3342336 | tf_op jit(solution)/shard_map/conv3/pallas_call | solution.py:282
  36.3 0.9 %w1.1 = bf16[896,128]{1,0:T(8,128)(2,1)S(1)} custom-call(bf16[4,2,10,16,768]{4,3,2,1,0:T(8,128)(2,1)S(1)} %get-tuple-element.52.x_ref, f32[1024,128]{1,0:T(8,128)S(1)} %get-tuple-element.47.a_ref.e_ref), custom_call_target="tpu_custom_call" | custom-call | flops 603979776 | bytes 2719744 | tf_op jit(solution)/shard_map/w1/pallas_call | solution.py:282
  37.2 18.4 %all_to_all.15 = bf16[32,56,128]{2,1,0:T(8,128)(2,1)S(1)} all-to-all(bf16[32,56,128]{2,1,0:T(8,128)(2,1)S(1)} %bitcast.3), channel_id=1, replica_groups={{0,1,2,3,4,5,6,7,8,9,10,11,12,13,14,15,16,17,18,19,20,21,22,23,24,25,26..., dimensions={0} | all-to-all | bytes 917504 | tf_op jit(solution)/shard_map/all_to_all | solution.py:382
  55.6 0.1 reduce_sum.24
  55.7 16.4 %all_to_all.16 = bf16[8,56,128]{2,1,0:T(8,128)(2,1)S(1)} all-to-all(bf16[8,56,128]{2,1,0:T(8,128)(2,1)S(1)} %broadcast_in_dim.34), channel_id=1, replica_groups={{0,32,64,96,128,160,192,224},{8,40,72,104,136,168,200,232},{16,48,80,11..., dimensions={0} | all-to-all | bytes 229376 | tf_op jit(solution)/shard_map/all_to_all | solution.py:385
  72.2 0.8 broadcast_in_dim.35
  73.0 4.7 %all-to-all-start.2 = ((bf16[32,56,128]{2,1,0:T(8,128)(2,1)}), bf16[32,56,128]{2,1,0:T(8,128)(2,1)S(1)}, u32[]{:S(2)}, u32[]{:S(2)}) async-start(bf16[32,56,128]{2,1,0:T(8,128)(2,1)} %broadcast_in_dim.35), calls=%async_computation.2 | async-start | bytes 917504 | tf_op jit(solution)/shard_map/all_to_all | solution.py:382
  77.7 1.5 %collective-permute-start.6 = (bf16[128,128]{1,0:T(8,128)(2,1)S(1)}, bf16[128,128]{1,0:T(8,128)(2,1)S(1)}, u32[]{:S(2)}, u32[]{:S(2)}) collective-permute-start(bf16[128,128]{1,0:T(8,128)(2,1)S(1)} %get-tuple-element.48), channel_id=1, source_target_pairs={{0,8},{8,16},{16,24},{24,32},{32,40},{40,48},{48,56},{56,64},{64,7... | collective-permute-start | bytes 98312 | tf_op jit(solution)/shard_map/ppermute | solution.py:312
  79.2 3.4 %collective-permute-start.7 = (bf16[128,128]{1,0:T(8,128)(2,1)S(1)}, bf16[128,128]{1,0:T(8,128)(2,1)S(1)}, u32[]{:S(2)}, u32[]{:S(2)}) collective-permute-start(bf16[128,128]{1,0:T(8,128)(2,1)S(1)} %get-tuple-element.49), channel_id=1, source_target_pairs={{8,0},{16,8},{24,16},{32,24},{40,32},{48,40},{56,48},{64,56},{72,6... | collective-permute-start | bytes 98312 | tf_op jit(solution)/shard_map/ppermute | solution.py:312
  82.6 1.6 %collective-permute-done.6.lo_ref = bf16[128,128]{1,0:T(8,128)(2,1)S(1)} collective-permute-done((bf16[128,128]{1,0:T(8,128)(2,1)S(1)}, bf16[128,128]{1,0:T(8,128)(2,1)S(1)}, u32[]{:S(2)}, u32[]{:S(2)}) %collective-permute-start.6) | collective-permute-done | bytes 32800 | tf_op jit(solution)/shard_map/ppermute | solution.py:312
  84.2 1.3 %collective-permute-done.7.hi_ref = bf16[128,128]{1,0:T(8,128)(2,1)S(1)} collective-permute-done((bf16[128,128]{1,0:T(8,128)(2,1)S(1)}, bf16[128,128]{1,0:T(8,128)(2,1)S(1)}, u32[]{:S(2)}, u32[]{:S(2)}) %collective-permute-start.7) | collective-permute-done | bytes 32800 | tf_op jit(solution)/shard_map/ppermute | solution.py:312
  85.5 4.1 %conv4.1 = f32[1,4,64,512]{3,2,1,0:T(8,128)} custom-call(s32[4,26]{1,0:T(4,128)S(1)} %select_select_fusion.idx_ref, f32[1024,128]{1,0:T(8,128)S(1)} %get-tuple-element.47.a_ref.e_ref, bf16[128,128]{1,0:T(8,128)(2,1)S(1)} %collective-permute-done.6.lo_ref, bf16[128,128]{1,0:T(8,128)(2,1)S(1)} %collective-permute-done.7.hi_ref, ...), custom_call_target="tpu_custom_call" | custom-call | flops 603979776 | bytes 2228224 | tf_op jit(solution)/shard_map/conv4/pallas_call | solution.py:282
  89.7 0.0 all-to-all-done.2
  89.7 1.6 %finish.1 = (f32[27,64,64]{2,1,0:T(8,128)}, f32[27,64,64]{2,1,0:T(8,128)}) custom-call(bf16[1792,128]{1,0:T(8,128)(2,1)S(1)} %bitcast.2), custom_call_target="tpu_custom_call" | custom-call | bytes 1343488 | tf_op jit(solution)/shard_map/finish/pallas_call | solution.py:282
  (3 shorter events, 0.1 us)
Async XLA Ops:
  1.3 1.0 %copy-start = (f32[1,4,64,512]{3,2,1,0:T(8,128)S(1)}, f32[1,4,64,512]{3,2,1,0:T(8,128)}, u32[]{:S(2)}) copy-start(f32[1,4,64,512]{3,2,1,0:T(8,128)} %x_ref.1) | copy-start | bytes 1572868
  2.9 12.1 %collective-permute-start = (bf16[128,128]{1,0:T(8,128)(2,1)S(1)}, bf16[128,128]{1,0:T(8,128)(2,1)S(1)}, u32[]{:S(2)}, u32[]{:S(2)}) collective-permute-start(bf16[128,128]{1,0:T(8,128)(2,1)S(1)} %get-tuple-element.31), channel_id=1, source_target_pairs={{0,8},{8,16},{16,24},{24,32},{32,40},{40,48},{48,56},{56,64},{64,7... | collective-permute-start | bytes 98312 | tf_op jit(solution)/shard_map/ppermute | solution.py:312
  5.0 10.0 %collective-permute-start.1 = (bf16[128,128]{1,0:T(8,128)(2,1)S(1)}, bf16[128,128]{1,0:T(8,128)(2,1)S(1)}, u32[]{:S(2)}, u32[]{:S(2)}) collective-permute-start(bf16[128,128]{1,0:T(8,128)(2,1)S(1)} %get-tuple-element.32), channel_id=1, source_target_pairs={{8,0},{16,8},{24,16},{32,24},{40,32},{48,40},{56,48},{64,56},{72,6... | collective-permute-start | bytes 98312 | tf_op jit(solution)/shard_map/ppermute | solution.py:312
  17.9 6.2 %collective-permute-start.2 = (bf16[128,128]{1,0:T(8,128)(2,1)S(1)}, bf16[128,128]{1,0:T(8,128)(2,1)S(1)}, u32[]{:S(2)}, u32[]{:S(2)}) collective-permute-start(bf16[128,128]{1,0:T(8,128)(2,1)S(1)} %get-tuple-element.35), channel_id=1, source_target_pairs={{0,8},{8,16},{16,24},{24,32},{32,40},{40,48},{48,56},{56,64},{64,7... | collective-permute-start | bytes 98312 | tf_op jit(solution)/shard_map/ppermute | solution.py:312
  18.0 6.1 %collective-permute-start.3 = (bf16[128,128]{1,0:T(8,128)(2,1)S(1)}, bf16[128,128]{1,0:T(8,128)(2,1)S(1)}, u32[]{:S(2)}, u32[]{:S(2)}) collective-permute-start(bf16[128,128]{1,0:T(8,128)(2,1)S(1)} %get-tuple-element.36), channel_id=1, source_target_pairs={{8,0},{16,8},{24,16},{32,24},{40,32},{48,40},{56,48},{64,56},{72,6... | collective-permute-start | bytes 98312 | tf_op jit(solution)/shard_map/ppermute | solution.py:312
  27.0 6.4 %collective-permute-start.4 = (bf16[128,128]{1,0:T(8,128)(2,1)S(1)}, bf16[128,128]{1,0:T(8,128)(2,1)S(1)}, u32[]{:S(2)}, u32[]{:S(2)}) collective-permute-start(bf16[128,128]{1,0:T(8,128)(2,1)S(1)} %get-tuple-element.43), channel_id=1, source_target_pairs={{0,8},{8,16},{16,24},{24,32},{32,40},{40,48},{48,56},{56,64},{64,7... | collective-permute-start | bytes 98312 | tf_op jit(solution)/shard_map/ppermute | solution.py:312
  27.1 6.3 %collective-permute-start.5 = (bf16[128,128]{1,0:T(8,128)(2,1)S(1)}, bf16[128,128]{1,0:T(8,128)(2,1)S(1)}, u32[]{:S(2)}, u32[]{:S(2)}) collective-permute-start(bf16[128,128]{1,0:T(8,128)(2,1)S(1)} %get-tuple-element.44), channel_id=1, source_target_pairs={{8,0},{16,8},{24,16},{32,24},{40,32},{48,40},{56,48},{64,56},{72,6... | collective-permute-start | bytes 98312 | tf_op jit(solution)/shard_map/ppermute | solution.py:312
  73.0 16.6 %all-to-all-start.2 = ((bf16[32,56,128]{2,1,0:T(8,128)(2,1)}), bf16[32,56,128]{2,1,0:T(8,128)(2,1)S(1)}, u32[]{:S(2)}, u32[]{:S(2)}) async-start(bf16[32,56,128]{2,1,0:T(8,128)(2,1)} %broadcast_in_dim.35), calls=%async_computation.2 | async-start | bytes 917504 | tf_op jit(solution)/shard_map/all_to_all | solution.py:382
  77.7 6.5 %collective-permute-start.6 = (bf16[128,128]{1,0:T(8,128)(2,1)S(1)}, bf16[128,128]{1,0:T(8,128)(2,1)S(1)}, u32[]{:S(2)}, u32[]{:S(2)}) collective-permute-start(bf16[128,128]{1,0:T(8,128)(2,1)S(1)} %get-tuple-element.48), channel_id=1, source_target_pairs={{0,8},{8,16},{16,24},{24,32},{32,40},{40,48},{48,56},{56,64},{64,7... | collective-permute-start | bytes 98312 | tf_op jit(solution)/shard_map/ppermute | solution.py:312
  79.2 6.3 %collective-permute-start.7 = (bf16[128,128]{1,0:T(8,128)(2,1)S(1)}, bf16[128,128]{1,0:T(8,128)(2,1)S(1)}, u32[]{:S(2)}, u32[]{:S(2)}) collective-permute-start(bf16[128,128]{1,0:T(8,128)(2,1)S(1)} %get-tuple-element.49), channel_id=1, source_target_pairs={{8,0},{16,8},{24,16},{32,24},{40,32},{48,40},{56,48},{64,56},{72,6... | collective-permute-start | bytes 98312 | tf_op jit(solution)/shard_map/ppermute | solution.py:312

commit v3 on v2

--- a/solution.py
+++ b/solution.py
@@ -391,7 +391,7 @@
         return jnp.broadcast_to(block[None], (count,) + block.shape)
 
     partial = jnp.concatenate([first_local, second_local]).reshape(near, share, 128)
-    mine = total_of(near_exchange(partial))
+    mine, input_grad = lax.optimization_barrier((total_of(near_exchange(partial)), input_grad))
     mine = total_of(far_exchange(spread(mine, far)))
     total = near_exchange(spread(mine, near))
     scale = float((devices * CAP * E * E * E) ** -0.5)

time: 91.6 us -> 95.1 us (1.038)
  starting transfers between devices: 28.1 us -> 33.8 us
  waiting for transfers between devices: 4.24 us -> 2.83 us
    all_to_all x1, starting transfers between devices: 4.71 us -> 7.63 us  [near_exchange(): lax.all_to_all(blocks, axes, 0, 0, axis_index_groups=near_groups, tiled=T...]
    ppermute x4, starting transfers between devices: 19.7 us -> 22.5 us  [exchange(): lax.ppermute(down, 'brick', down_pairs)]
    all_to_all x1, blocking collectives: 16.4 us -> 14.4 us  [far_exchange(): lax.all_to_all(blocks, 'brick', 0, 0, axis_index_groups=far_groups, tiled...]
    ppermute x4, waiting for transfers between devices: 1.33 us -> 0.01 us  [exchange(): lax.ppermute(down, 'brick', down_pairs)]
    all_to_all x1, blocking collectives: 18.4 us -> 19.6 us  [near_exchange(): lax.all_to_all(blocks, axes, 0, 0, axis_index_groups=near_groups, tiled=T...]
  transfers between devices with their start and end apart: 9 -> 9, of which waited for: 3 -> 2; matrix products, arithmetic and copies ran while one was open for 1% -> 1% of each run, Pallas kernels for 9% -> 9%
where the time goes in v3:
time: 95.1 us; the launch traced here: 94.8 us
  blocking collectives  34 us (36%)
  starting transfers between devices  33.8 us (36%)
  Pallas kernels  20 us (21%)
  waiting for transfers between devices  2.83 us (3%)
  other arithmetic  1.61 us (2%)
  between operations  1.4 us (1%)
  local copies, waits for them, and re-layouts  1.11 us (1%)
    ppermute x4, starting transfers between devices, exchange(): lax.ppermute(down, 'brick', down_pairs)  22.5 us
    pallas_call x9, Pallas kernels, call(): pl.pallas_call(kernel, name=name, out_shape=outs, in_specs=[SMEM] * len(s...  20 us
    all_to_all x1, blocking collectives, near_exchange(): lax.all_to_all(blocks, axes, 0, 0, axis_index_groups=near_groups, tiled=T...  19.6 us
    all_to_all x1, blocking collectives, far_exchange(): lax.all_to_all(blocks, 'brick', 0, 0, axis_index_groups=far_groups, tiled...  14.4 us
    all_to_all x1, starting transfers between devices, near_exchange(): lax.all_to_all(blocks, axes, 0, 0, axis_index_groups=near_groups, tiled=T...  7.63 us
    ppermute x4, starting transfers between devices, exchange(): lax.ppermute(up, 'brick', up_pairs)  3.71 us
    ppermute x4, waiting for transfers between devices, exchange(): lax.ppermute(up, 'brick', up_pairs)  2.81 us
  transfers between devices with their start and end apart: 9, of which 2 were waited for; matrix products, arithmetic and copies ran while one was open for 1% of the time, Pallas kernels for 9%

profile of v3, /device:TPU:1, one launch (start us, length us, event | category | flops | bytes accessed | tf_op | source)
XLA Modules:
  0.0 94.8 jit_solution(15650017865516890527)
XLA Ops:
  1.3 0.0 copy-start
  1.3 1.0 %copy-done = f32[1,4,64,512]{3,2,1,0:T(8,128)S(1)} copy-done((f32[1,4,64,512]{3,2,1,0:T(8,128)S(1)}, f32[1,4,64,512]{3,2,1,0:T(8,128)}, u32[]{:S(2)}) %copy-start) | copy-done | bytes 524312
  2.3 0.5 pre.1
  2.9 2.1 %collective-permute-start = (bf16[128,128]{1,0:T(8,128)(2,1)S(1)}, bf16[128,128]{1,0:T(8,128)(2,1)S(1)}, u32[]{:S(2)}, u32[]{:S(2)}) collective-permute-start(bf16[128,128]{1,0:T(8,128)(2,1)S(1)} %get-tuple-element.33), channel_id=1, source_target_pairs={{0,8},{8,16},{16,24},{24,32},{32,40},{40,48},{48,56},{56,64},{64,7... | collective-permute-start | bytes 98312 | tf_op jit(solution)/shard_map/ppermute | solution.py:312
  5.0 6.6 %collective-permute-start.1 = (bf16[128,128]{1,0:T(8,128)(2,1)S(1)}, bf16[128,128]{1,0:T(8,128)(2,1)S(1)}, u32[]{:S(2)}, u32[]{:S(2)}) collective-permute-start(bf16[128,128]{1,0:T(8,128)(2,1)S(1)} %get-tuple-element.34), channel_id=1, source_target_pairs={{8,0},{16,8},{24,16},{32,24},{40,32},{48,40},{56,48},{64,56},{72,6... | collective-permute-start | bytes 98312 | tf_op jit(solution)/shard_map/ppermute | solution.py:312
  11.6 0.7 select_select_fusion.idx_ref
  12.3 2.6 %prep.1 = (bf16[3,768,128]{2,1,0:T(8,128)(2,1)S(1)}, bf16[3,768,128]{2,1,0:T(8,128)(2,1)S(1)}, bf16[3,768,128]{2,1,0:T(8,128)(2,1)S(1)}, bf16[3,768,128]{2,1,0:T(8,128)(2,1)S(1)}, f32[1024,128]{1,0:T(8,128)S(1)}) custom-call(s32[1]{0:T(128)S(6)} %copy.11.counts_ref, f32[27,64,64]{2,1,0:T(8,128)} %w1_hbm.1, f32[27,64,64]{2,1,0:T(8,128)} %w2_hbm.1, ...), custom_call_target="tpu_custom_call" | custom-call | bytes 4292608 | tf_op jit(solution)/shard_map/prep/pallas_call | solution.py:282
  15.0 0.0 collective-permute-done.lo_ref
  15.0 0.0 collective-permute-done.1.hi_ref
  15.0 2.9 %conv1.1 = (bf16[4,2,10,16,768]{4,3,2,1,0:T(8,128)(2,1)S(1)}, f32[1024,128]{1,0:T(8,128)S(1)}, f32[1024,128]{1,0:T(8,128)S(1)}, bf16[128,128]{1,0:T(8,128)(2,1)S(1)}, bf16[128,128]{1,0:T(8,128)(2,1)S(1)}) custom-call(s32[4,26]{1,0:T(4,128)S(1)} %select_select_fusion.idx_ref, f32[1024,128]{1,0:T(8,128)S(1)} %get-tuple-element.32.a_ref, ...), custom_call_target="tpu_custom_call" | custom-call | flops 603979776 | bytes 4259840 | tf_op jit(solution)/shard_map/conv1/pallas_call | solution.py:282
  17.9 0.1 collective-permute-start.2
  18.0 4.8 %collective-permute-start.3 = (bf16[128,128]{1,0:T(8,128)(2,1)S(1)}, bf16[128,128]{1,0:T(8,128)(2,1)S(1)}, u32[]{:S(2)}, u32[]{:S(2)}) collective-permute-start(bf16[128,128]{1,0:T(8,128)(2,1)S(1)} %get-tuple-element.38), channel_id=1, source_target_pairs={{8,0},{16,8},{24,16},{32,24},{40,32},{48,40},{56,48},{64,56},{72,6... | collective-permute-start | bytes 98312 | tf_op jit(solution)/shard_map/ppermute | solution.py:312
  22.8 1.3 %collective-permute-done.2.lo_ref = bf16[128,128]{1,0:T(8,128)(2,1)S(1)} collective-permute-done((bf16[128,128]{1,0:T(8,128)(2,1)S(1)}, bf16[128,128]{1,0:T(8,128)(2,1)S(1)}, u32[]{:S(2)}, u32[]{:S(2)}) %collective-permute-start.2) | collective-permute-done | bytes 32800 | tf_op jit(solution)/shard_map/ppermute | solution.py:312
  24.1 0.0 collective-permute-done.3.hi_ref
  24.1 2.9 %conv2.1 = (bf16[4,2,10,16,768]{4,3,2,1,0:T(8,128)(2,1)S(1)}, f32[1024,128]{1,0:T(8,128)S(1)}, f32[1024,128]{1,0:T(8,128)S(1)}, bf16[128,128]{1,0:T(8,128)(2,1)S(1)}, bf16[128,128]{1,0:T(8,128)(2,1)S(1)}) custom-call(s32[4,26]{1,0:T(4,128)S(1)} %select_select_fusion.idx_ref, f32[1024,128]{1,0:T(8,128)S(1)} %get-tuple-element.36.a_ref, ...), custom_call_target="tpu_custom_call" | custom-call | flops 603979776 | bytes 4784128 | tf_op jit(solution)/shard_map/conv2/pallas_call | solution.py:282
  27.0 0.1 collective-permute-start.4
  27.1 4.9 %collective-permute-start.5 = (bf16[128,128]{1,0:T(8,128)(2,1)S(1)}, bf16[128,128]{1,0:T(8,128)(2,1)S(1)}, u32[]{:S(2)}, u32[]{:S(2)}) collective-permute-start(bf16[128,128]{1,0:T(8,128)(2,1)S(1)} %get-tuple-element.47), channel_id=1, source_target_pairs={{8,0},{16,8},{24,16},{32,24},{40,32},{48,40},{56,48},{64,56},{72,6... | collective-permute-start | bytes 98312 | tf_op jit(solution)/shard_map/ppermute | solution.py:312
  32.0 1.5 %w2.1 = (f32[1,4,64,512]{3,2,1,0:T(8,128)}, bf16[896,128]{1,0:T(8,128)(2,1)S(1)}) custom-call(bf16[4,2,10,16,768]{4,3,2,1,0:T(8,128)(2,1)S(1)} %get-tuple-element.41.x_ref, f32[1024,128]{1,0:T(8,128)S(1)} %get-tuple-element.42.e_ref.a_ref, f32[1024,128]{1,0:T(8,128)S(1)} %get-tuple-element.43.r_ref), custom_call_target="tpu_custom_call" | custom-call | flops 603979776 | bytes 3768320 | tf_op jit(solution)/shard_map/w2/pallas_call | solution.py:282
  33.4 0.0 collective-permute-done.4.lo_ref
  33.4 0.0 collective-permute-done.5.hi_ref
  33.4 2.8 %conv3.1 = (f32[1024,128]{1,0:T(8,128)S(1)}, f32[1024,128]{1,0:T(8,128)S(1)}, bf16[128,128]{1,0:T(8,128)(2,1)S(1)}, bf16[128,128]{1,0:T(8,128)(2,1)S(1)}) custom-call(s32[4,26]{1,0:T(4,128)S(1)} %select_select_fusion.idx_ref, f32[1024,128]{1,0:T(8,128)S(1)} %get-tuple-element.42.e_ref.a_ref, bf16[128,128]{1,0:T(8,128)(2,1)S(1)} %collective-permute-done.4.lo_ref, ...), custom_call_target="tpu_custom_call" | custom-call | flops 603979776 | bytes 3342336 | tf_op jit(solution)/shard_map/conv3/pallas_call | solution.py:282
  36.3 0.9 w1.1
  37.2 0.8 pad_maximum_fusion
  38.0 7.6 %all-to-all-start = ((bf16[32,56,128]{2,1,0:T(8,128)(2,1)}), bf16[32,56,128]{2,1,0:T(8,128)(2,1)S(1)}, u32[]{:S(2)}, u32[]{:S(2)}) async-start(bf16[32,56,128]{2,1,0:T(8,128)(2,1)} %bitcast), calls=%async_computation | async-start | bytes 917504 | tf_op jit(solution)/shard_map/all_to_all | solution.py:382
  45.6 1.4 %collective-permute-start.6 = (bf16[128,128]{1,0:T(8,128)(2,1)S(1)}, bf16[128,128]{1,0:T(8,128)(2,1)S(1)}, u32[]{:S(2)}, u32[]{:S(2)}) collective-permute-start(bf16[128,128]{1,0:T(8,128)(2,1)S(1)} %get-tuple-element.52), channel_id=1, source_target_pairs={{0,8},{8,16},{16,24},{24,32},{32,40},{40,48},{48,56},{56,64},{64,7... | collective-permute-start | bytes 98312 | tf_op jit(solution)/shard_map/ppermute | solution.py:312
  47.1 6.2 %collective-permute-start.7 = (bf16[128,128]{1,0:T(8,128)(2,1)S(1)}, bf16[128,128]{1,0:T(8,128)(2,1)S(1)}, u32[]{:S(2)}, u32[]{:S(2)}) collective-permute-start(bf16[128,128]{1,0:T(8,128)(2,1)S(1)} %get-tuple-element.53), channel_id=1, source_target_pairs={{8,0},{16,8},{24,16},{32,24},{40,32},{48,40},{56,48},{64,56},{72,6... | collective-permute-start | bytes 98312 | tf_op jit(solution)/shard_map/ppermute | solution.py:312
  53.3 1.5 %collective-permute-done.6.lo_ref = bf16[128,128]{1,0:T(8,128)(2,1)S(1)} collective-permute-done((bf16[128,128]{1,0:T(8,128)(2,1)S(1)}, bf16[128,128]{1,0:T(8,128)(2,1)S(1)}, u32[]{:S(2)}, u32[]{:S(2)}) %collective-permute-start.6) | collective-permute-done | bytes 32800 | tf_op jit(solution)/shard_map/ppermute | solution.py:312
  54.8 0.0 collective-permute-done.7.hi_ref
  54.8 4.1 %conv4.1 = f32[1,4,64,512]{3,2,1,0:T(8,128)} custom-call(s32[4,26]{1,0:T(4,128)S(1)} %select_select_fusion.idx_ref, f32[1024,128]{1,0:T(8,128)S(1)} %get-tuple-element.50.e_ref.a_ref, bf16[128,128]{1,0:T(8,128)(2,1)S(1)} %collective-permute-done.6.lo_ref, bf16[128,128]{1,0:T(8,128)(2,1)S(1)} %collective-permute-done.7.hi_ref, ...), custom_call_target="tpu_custom_call" | custom-call | flops 603979776 | bytes 2228224 | tf_op jit(solution)/shard_map/conv4/pallas_call | solution.py:282
  58.9 0.0 all-to-all-done
  58.9 0.1 reduce_sum.24
  59.0 14.4 %all_to_all.15 = bf16[8,56,128]{2,1,0:T(8,128)(2,1)S(1)} all-to-all(bf16[8,56,128]{2,1,0:T(8,128)(2,1)S(1)} %broadcast_in_dim.34), channel_id=1, replica_groups={{0,32,64,96,128,160,192,224},{8,40,72,104,136,168,200,232},{16,48,80,11..., dimensions={0} | all-to-all | bytes 229376 | tf_op jit(solution)/shard_map/all_to_all | solution.py:385
  73.4 0.1 broadcast_in_dim.35
  73.5 19.6 %all_to_all.16 = bf16[32,56,128]{2,1,0:T(8,128)(2,1)S(1)} all-to-all(bf16[32,56,128]{2,1,0:T(8,128)(2,1)S(1)} %broadcast_in_dim.35), channel_id=1, replica_groups={{0,1,2,3,4,5,6,7,8,9,10,11,12,13,14,15,16,17,18,19,20,21,22,23,24,25,26..., dimensions={0} | all-to-all | bytes 917504 | tf_op jit(solution)/shard_map/all_to_all | solution.py:382
  93.1 1.6 %finish.1 = (f32[27,64,64]{2,1,0:T(8,128)}, f32[27,64,64]{2,1,0:T(8,128)}) custom-call(bf16[1792,128]{1,0:T(8,128)(2,1)S(1)} %bitcast.2), custom_call_target="tpu_custom_call" | custom-call | bytes 1343488 | tf_op jit(solution)/shard_map/finish/pallas_call | solution.py:282
  (2 shorter events, 0.0 us)
Async XLA Ops:
  1.3 1.0 %copy-start = (f32[1,4,64,512]{3,2,1,0:T(8,128)S(1)}, f32[1,4,64,512]{3,2,1,0:T(8,128)}, u32[]{:S(2)}) copy-start(f32[1,4,64,512]{3,2,1,0:T(8,128)} %x_ref.1) | copy-start | bytes 1572868
  2.9 12.1 %collective-permute-start = (bf16[128,128]{1,0:T(8,128)(2,1)S(1)}, bf16[128,128]{1,0:T(8,128)(2,1)S(1)}, u32[]{:S(2)}, u32[]{:S(2)}) collective-permute-start(bf16[128,128]{1,0:T(8,128)(2,1)S(1)} %get-tuple-element.33), channel_id=1, source_target_pairs={{0,8},{8,16},{16,24},{24,32},{32,40},{40,48},{48,56},{56,64},{64,7... | collective-permute-start | bytes 98312 | tf_op jit(solution)/shard_map/ppermute | solution.py:312
  5.0 10.0 %collective-permute-start.1 = (bf16[128,128]{1,0:T(8,128)(2,1)S(1)}, bf16[128,128]{1,0:T(8,128)(2,1)S(1)}, u32[]{:S(2)}, u32[]{:S(2)}) collective-permute-start(bf16[128,128]{1,0:T(8,128)(2,1)S(1)} %get-tuple-element.34), channel_id=1, source_target_pairs={{8,0},{16,8},{24,16},{32,24},{40,32},{48,40},{56,48},{64,56},{72,6... | collective-permute-start | bytes 98312 | tf_op jit(solution)/shard_map/ppermute | solution.py:312
  17.9 6.2 %collective-permute-start.2 = (bf16[128,128]{1,0:T(8,128)(2,1)S(1)}, bf16[128,128]{1,0:T(8,128)(2,1)S(1)}, u32[]{:S(2)}, u32[]{:S(2)}) collective-permute-start(bf16[128,128]{1,0:T(8,128)(2,1)S(1)} %get-tuple-element.37), channel_id=1, source_target_pairs={{0,8},{8,16},{16,24},{24,32},{32,40},{40,48},{48,56},{56,64},{64,7... | collective-permute-start | bytes 98312 | tf_op jit(solution)/shard_map/ppermute | solution.py:312
  18.0 6.1 %collective-permute-start.3 = (bf16[128,128]{1,0:T(8,128)(2,1)S(1)}, bf16[128,128]{1,0:T(8,128)(2,1)S(1)}, u32[]{:S(2)}, u32[]{:S(2)}) collective-permute-start(bf16[128,128]{1,0:T(8,128)(2,1)S(1)} %get-tuple-element.38), channel_id=1, source_target_pairs={{8,0},{16,8},{24,16},{32,24},{40,32},{48,40},{56,48},{64,56},{72,6... | collective-permute-start | bytes 98312 | tf_op jit(solution)/shard_map/ppermute | solution.py:312
  27.0 6.4 %collective-permute-start.4 = (bf16[128,128]{1,0:T(8,128)(2,1)S(1)}, bf16[128,128]{1,0:T(8,128)(2,1)S(1)}, u32[]{:S(2)}, u32[]{:S(2)}) collective-permute-start(bf16[128,128]{1,0:T(8,128)(2,1)S(1)} %get-tuple-element.46), channel_id=1, source_target_pairs={{0,8},{8,16},{16,24},{24,32},{32,40},{40,48},{48,56},{56,64},{64,7... | collective-permute-start | bytes 98312 | tf_op jit(solution)/shard_map/ppermute | solution.py:312
  27.1 6.3 %collective-permute-start.5 = (bf16[128,128]{1,0:T(8,128)(2,1)S(1)}, bf16[128,128]{1,0:T(8,128)(2,1)S(1)}, u32[]{:S(2)}, u32[]{:S(2)}) collective-permute-start(bf16[128,128]{1,0:T(8,128)(2,1)S(1)} %get-tuple-element.47), channel_id=1, source_target_pairs={{8,0},{16,8},{24,16},{32,24},{40,32},{48,40},{56,48},{64,56},{72,6... | collective-permute-start | bytes 98312 | tf_op jit(solution)/shard_map/ppermute | solution.py:312
  38.0 20.9 %all-to-all-start = ((bf16[32,56,128]{2,1,0:T(8,128)(2,1)}), bf16[32,56,128]{2,1,0:T(8,128)(2,1)S(1)}, u32[]{:S(2)}, u32[]{:S(2)}) async-start(bf16[32,56,128]{2,1,0:T(8,128)(2,1)} %bitcast), calls=%async_computation | async-start | bytes 917504 | tf_op jit(solution)/shard_map/all_to_all | solution.py:382
  45.6 9.1 %collective-permute-start.6 = (bf16[128,128]{1,0:T(8,128)(2,1)S(1)}, bf16[128,128]{1,0:T(8,128)(2,1)S(1)}, u32[]{:S(2)}, u32[]{:S(2)}) collective-permute-start(bf16[128,128]{1,0:T(8,128)(2,1)S(1)} %get-tuple-element.52), channel_id=1, source_target_pairs={{0,8},{8,16},{16,24},{24,32},{32,40},{40,48},{48,56},{56,64},{64,7... | collective-permute-start | bytes 98312 | tf_op jit(solution)/shard_map/ppermute | solution.py:312
  47.1 7.7 %collective-permute-start.7 = (bf16[128,128]{1,0:T(8,128)(2,1)S(1)}, bf16[128,128]{1,0:T(8,128)(2,1)S(1)}, u32[]{:S(2)}, u32[]{:S(2)}) collective-permute-start(bf16[128,128]{1,0:T(8,128)(2,1)S(1)} %get-tuple-element.53), channel_id=1, source_target_pairs={{8,0},{16,8},{24,16},{32,24},{40,32},{48,40},{56,48},{64,56},{72,6... | collective-permute-start | bytes 98312 | tf_op jit(solution)/shard_map/ppermute | solution.py:312

commit v4 on v3

--- a/solution.py
+++ b/solution.py
@@ -4,6 +4,7 @@
 from jax.experimental import pallas as pl
 from jax.experimental.pallas import tpu as pltpu
 from jax.sharding import PartitionSpec as P
+
 
 E = 8
 C = 64
@@ -71,13 +72,18 @@
         k = 9 * (a + 1) + 3 * (b + 1) + (c + 1)
         return w_ref[26 - k].T if back else w_ref[k]
 
-    for ci, c in enumerate((-1, 0, 1)):
-        for bi, b in enumerate((-1, 0, 1)):
+    blank = jnp.zeros((256, 128), bf16)
+    for bi, b in enumerate((-1, 0, 1)):
+        rows = pl.ds(bi * 256, 256)
+        o_ref[0, rows, 128:] = blank
+        o_ref[3, rows, :128] = blank
+        for ci, c in enumerate((-1, 0, 1)):
             low, mid, high = (block(a, b, c) for a in (-1, 0, 1))
-            rows = ((mid, low), (high, mid), (zero, high), (low, zero))
-            for r, (left, right) in enumerate(rows):
-                joined = jnp.concatenate([left, right], axis=1).astype(bf16)
-                o_ref[ci, pl.ds(bi * 256 + r * C, C), :] = joined
+            left = jnp.concatenate([mid, high, zero, low], axis=0)
+            right = jnp.concatenate([low, mid, high, zero], axis=0)
+            joined = jnp.concatenate([left, right], axis=1).astype(bf16)
+            o_ref[ci, rows, :128] = joined
+            o_ref[ci + 1, rows, 128:] = joined
 
 
 def prep_kernel(
@@ -152,16 +158,17 @@
 
 
 def convolve(x_ref, w_ref, epilogue):
-    def one_slot(s, carry):
-        total = None
-        for c in range(3):
-            rows = x_ref[s, :, c : c + E].reshape(256, 768)
-            term = jnp.dot(rows, w_ref[c], preferred_element_type=f32)
-            total = term if total is None else total + term
-        epilogue(pl.ds(pl.multiple_of(s * 256, 256), 256), total)
-        return carry
-
-    lax.fori_loop(0, CAP, one_slot, 0)
+    total = None
+    for d in range(4):
+        rows = jnp.concatenate([x_ref[:, :, d + 2 * m : d + 2 * m + 1] for m in range(4)], axis=2)
+        term = jnp.dot(rows.reshape(512, 768), w_ref[d], preferred_element_type=f32)
+        total = term if total is None else total + term
+    for s in range(CAP):
+        for nh in range(2):
+            for l in range(E):
+                at = (s * 8 + nh * 4 + l // 2) * 16
+                lanes = (l % 2) * 128
+                epilogue(pl.ds(s * 256 + nh * 128 + l * 16, 16), total[at : at + 16, lanes : lanes + 128])
 
 
 def logistic(v):
@@ -244,7 +251,8 @@
     weight_grad(x_ref, e_ref, p_ref)
 
 
-def w1_kernel(x_ref, e_ref, p_ref):
+def w1_kernel(x_ref, e_ref, second_ref, p_ref):
+    p_ref[pl.ds(PACKED, PACKED), :] = second_ref[...]
     weight_grad(x_ref, e_ref, p_ref)
 
 
@@ -271,17 +279,16 @@
 FIELD = jax.ShapeDtypeStruct((ROWS, 128), f32)
 PLANES = jax.ShapeDtypeStruct((PLANE, 128), bf16)
 WINDOWS = (CAP, 2, 10, 16, 768)
-WEIGHTS = jax.ShapeDtypeStruct((3, 768, 128), bf16)
+WEIGHTS = jax.ShapeDtypeStruct((4, 768, 256), bf16)
 CUBES = jax.ShapeDtypeStruct((1, CAP, C, E * E * E), f32)
 POOLS = [pltpu.VMEM((ROWS + 256, 128), f32), pltpu.VMEM((2, 2 * PLANE + 32, 128), f32)]
 TMP = pltpu.VMEM((16, C, 128), f32)
 
 
-def call(kernel, name, scalars, arrays, outs, scratch=(), flops=0, place=VMEM):
+def call(kernel, scalars, arrays, outs, scratch=(), flops=0, place=VMEM):
     moved = sum(x.size * x.dtype.itemsize for x in arrays) + sum(o.size * o.dtype.itemsize for o in outs)
     return pl.pallas_call(
         kernel,
-        name=name,
         out_shape=outs,
         in_specs=[SMEM] * len(scalars) + [place] * len(arrays),
         out_specs=[VMEM] * len(outs),
@@ -303,7 +310,7 @@
     return jnp.where(depth == 0, middle, outer).astype(jnp.int32)
 
 
-def body(features, cotangent, first_kernel, second_kernel, counts, neighbours):
+def step(features, cotangent, first_kernel, second_kernel, counts, neighbours):
     bricks = lax.axis_size("brick")
     up_pairs = [(i, (i + 1) % bricks) for i in range(bricks)]
     down_pairs = [(j, i) for i, j in up_pairs]
@@ -317,11 +324,10 @@
     scratch_x = pltpu.VMEM(WINDOWS, bf16)
     work = 2 * ROWS * 2304 * 128
 
-    inputs, up, down = call(pre_kernel, "pre", [counts], [features], [FIELD, PLANES, PLANES], [TMP])
+    inputs, up, down = call(pre_kernel, [counts], [features], [FIELD, PLANES, PLANES], [TMP])
     lo, hi = exchange(up, down)
     f1, f2, b1, b2, upstream = call(
         prep_kernel,
-        "prep",
         [counts],
         [pltpu.with_memory_space_constraint(v, pltpu.HBM) for v in (first_kernel, second_kernel, cotangent)],
         [WEIGHTS] * 4 + [FIELD],
@@ -335,23 +341,16 @@
         place=HBM,
     )
     x_in, hidden, slope1, up, down = call(
-        conv1_kernel, "conv1", [idx], [inputs, lo, hi, f1], [windows, FIELD, FIELD, PLANES, PLANES], POOLS, work
+        conv1_kernel, [idx], [inputs, lo, hi, f1], [windows, FIELD, FIELD, PLANES, PLANES], POOLS, work
     )
     lo, hi = exchange(up, down)
     x_hidden, out_rows, second_err, up, down = call(
-        conv2_kernel,
-        "conv2",
-        [idx],
-        [hidden, lo, hi, f2, upstream],
-        [windows, FIELD, FIELD, PLANES, PLANES],
-        POOLS,
-        work,
+        conv2_kernel, [idx], [hidden, lo, hi, f2, upstream], [windows, FIELD, FIELD, PLANES, PLANES], POOLS, work
     )
     lo, hi = exchange(up, down)
-    outputs, second_local = call(w2_kernel, "w2", [], [x_hidden, second_err, out_rows], [CUBES, packed], [TMP], work)
+    outputs, second_local = call(w2_kernel, [], [x_hidden, second_err, out_rows], [CUBES, packed], [TMP], work)
     hidden_grad, first_err, up, down = call(
         conv3_kernel,
-        "conv3",
         [idx],
         [second_err, lo, hi, b2, upstream, slope1],
         [FIELD, FIELD, PLANES, PLANES],
@@ -359,10 +358,11 @@
         work,
     )
     lo, hi = exchange(up, down)
-    (first_local,) = call(w1_kernel, "w1", [], [x_in, first_err], [packed], (), work)
+    (partial,) = call(
+        w1_kernel, [], [x_in, first_err, second_local], [jax.ShapeDtypeStruct((2 * PACKED, 128), bf16)], (), work
+    )
     (input_grad,) = call(
         conv4_kernel,
-        "conv4",
         [idx],
         [first_err, lo, hi, b1, hidden_grad],
         [CUBES],
@@ -390,21 +390,20 @@
     def spread(block, count):
         return jnp.broadcast_to(block[None], (count,) + block.shape)
 
-    partial = jnp.concatenate([first_local, second_local]).reshape(near, share, 128)
-    mine, input_grad = lax.optimization_barrier((total_of(near_exchange(partial)), input_grad))
+    mine = total_of(near_exchange(partial.reshape(near, share, 128)))
     mine = total_of(far_exchange(spread(mine, far)))
     total = near_exchange(spread(mine, near))
     scale = float((devices * CAP * E * E * E) ** -0.5)
     grads = jax.ShapeDtypeStruct((27, C, C), f32)
     first_grad, second_grad = call(
-        lambda *refs: finish_kernel(scale, *refs), "finish", [], [total.reshape(2 * PACKED, 128)], [grads, grads]
+        lambda *refs: finish_kernel(scale, *refs), [], [total.reshape(2 * PACKED, 128)], [grads, grads]
     )
     return (outputs, input_grad, first_grad, second_grad)
 
 
 def solution(mesh):
     return jax.shard_map(
-        body,
+        step,
         mesh=mesh,
         in_specs=(
             P("scene", "brick", None, None),

time: 95.1 us -> 89 us (0.936)
  starting transfers between devices: 33.8 us -> 28.3 us
  Pallas kernels: 20 us -> 16.6 us
  waiting for transfers between devices: 2.83 us -> 4.83 us
    pallas_call x9, Pallas kernels: 20 us -> 16.6 us  [call(): pl.pallas_call(kernel, out_shape=outs, in_specs=[SMEM] * len(scalars) + [...]
    ppermute x4, starting transfers between devices: 22.5 us -> 19.7 us  [exchange(): lax.ppermute(down, 'brick', down_pairs)]
    all_to_all x1, starting transfers between devices: 7.63 us -> 4.89 us  [near_exchange(): lax.all_to_all(blocks, axes, 0, 0, axis_index_groups=near_groups, tiled=T...]
    all_to_all x1, blocking collectives: 14.4 us -> 16.4 us  [far_exchange(): lax.all_to_all(blocks, 'brick', 0, 0, axis_index_groups=far_groups, tiled...]
    ppermute x4, waiting for transfers between devices: 0.01 us -> 1.33 us  [exchange(): lax.ppermute(down, 'brick', down_pairs)]
    all_to_all x1, blocking collectives: 19.6 us -> 18.4 us  [near_exchange(): lax.all_to_all(blocks, axes, 0, 0, axis_index_groups=near_groups, tiled=T...]
  transfers between devices with their start and end apart: 9 -> 9, of which waited for: 2 -> 4; matrix products, arithmetic and copies ran while one was open for 1% -> 1% of each run, Pallas kernels for 9% -> 8%
where the time goes in v4:
time: 89 us; the launch traced here: 88.6 us
  blocking collectives  34.8 us (39%)
  starting transfers between devices  28.3 us (32%)
  Pallas kernels  16.6 us (19%)
  waiting for transfers between devices  4.83 us (5%)
  local copies, waits for them, and re-layouts  1.88 us (2%)
  between operations  1.39 us (2%)
    ppermute x4, starting transfers between devices, exchange(): lax.ppermute(down, 'brick', down_pairs)  19.7 us
    all_to_all x1, blocking collectives, near_exchange(): lax.all_to_all(blocks, axes, 0, 0, axis_index_groups=near_groups, tiled=T...  18.4 us
    pallas_call x9, Pallas kernels, call(): pl.pallas_call(kernel, out_shape=outs, in_specs=[SMEM] * len(scalars) + [...  16.6 us
    all_to_all x1, blocking collectives, far_exchange(): lax.all_to_all(blocks, 'brick', 0, 0, axis_index_groups=far_groups, tiled...  16.4 us
    all_to_all x1, starting transfers between devices, near_exchange(): lax.all_to_all(blocks, axes, 0, 0, axis_index_groups=near_groups, tiled=T...  4.89 us
    ppermute x4, starting transfers between devices, exchange(): lax.ppermute(up, 'brick', up_pairs)  3.76 us
    ppermute x4, waiting for transfers between devices, exchange(): lax.ppermute(up, 'brick', up_pairs)  2.91 us
  transfers between devices with their start and end apart: 9, of which 4 were waited for; matrix products, arithmetic and copies ran while one was open for 1% of the time, Pallas kernels for 8%

profile of v4, /device:TPU:1, one launch (start us, length us, event | category | flops | bytes accessed | tf_op | source)
XLA Modules:
  0.0 88.6 jit_solution(5292872145018661317)
XLA Ops:
  1.3 0.0 copy-start
  1.3 1.0 %copy-done = f32[1,4,64,512]{3,2,1,0:T(8,128)S(1)} copy-done((f32[1,4,64,512]{3,2,1,0:T(8,128)S(1)}, f32[1,4,64,512]{3,2,1,0:T(8,128)}, u32[]{:S(2)}) %copy-start) | copy-done | bytes 524312
  2.3 0.5 shard_map.102
  2.9 2.1 %collective-permute-start = (bf16[128,128]{1,0:T(8,128)(2,1)S(1)}, bf16[128,128]{1,0:T(8,128)(2,1)S(1)}, u32[]{:S(2)}, u32[]{:S(2)}) collective-permute-start(bf16[128,128]{1,0:T(8,128)(2,1)S(1)} %get-tuple-element.31), channel_id=1, source_target_pairs={{0,8},{8,16},{16,24},{24,32},{32,40},{40,48},{48,56},{56,64},{64,7... | collective-permute-start | bytes 98312 | tf_op jit(solution)/shard_map/ppermute | solution.py:319
  5.0 6.6 %collective-permute-start.1 = (bf16[128,128]{1,0:T(8,128)(2,1)S(1)}, bf16[128,128]{1,0:T(8,128)(2,1)S(1)}, u32[]{:S(2)}, u32[]{:S(2)}) collective-permute-start(bf16[128,128]{1,0:T(8,128)(2,1)S(1)} %get-tuple-element.32), channel_id=1, source_target_pairs={{8,0},{16,8},{24,16},{32,24},{40,32},{48,40},{56,48},{64,56},{72,6... | collective-permute-start | bytes 98312 | tf_op jit(solution)/shard_map/ppermute | solution.py:319
  11.6 0.7 select_select_fusion.idx_ref
  12.3 2.8 %shard_map.103 = (bf16[4,768,256]{2,1,0:T(8,128)(2,1)S(1)}, bf16[4,768,256]{2,1,0:T(8,128)(2,1)S(1)}, bf16[4,768,256]{2,1,0:T(8,128)(2,1)S(1)}, bf16[4,768,256]{2,1,0:T(8,128)(2,1)S(1)}, f32[1024,128]{1,0:T(8,128)S(1)}) custom-call(s32[1]{0:T(128)S(6)} %copy.11.counts_ref, f32[27,64,64]{2,1,0:T(8,128)} %w1_hbm.1, f32[27,64,64]{2,1,0:T(8,128)} %w2_hbm.1, ...), custom_call_target="tpu_custom_call" | custom-call | bytes 8224768 | tf_op jit(solution)/shard_map/pallas_call | solution.py:290
  15.1 0.0 collective-permute-done.lo_ref
  15.1 0.0 collective-permute-done.1.hi_ref
  15.2 2.0 %shard_map.104 = (bf16[4,2,10,16,768]{4,3,2,1,0:T(8,128)(2,1)S(1)}, f32[1024,128]{1,0:T(8,128)S(1)}, f32[1024,128]{1,0:T(8,128)S(1)}, bf16[128,128]{1,0:T(8,128)(2,1)S(1)}, bf16[128,128]{1,0:T(8,128)(2,1)S(1)}) custom-call(s32[4,26]{1,0:T(4,128)S(1)} %select_select_fusion.idx_ref, f32[1024,128]{1,0:T(8,128)S(1)} %get-tuple-element.30.a_ref, ...), custom_call_target="tpu_custom_call" | custom-call | flops 603979776 | bytes 5242880 | tf_op jit(solution)/shard_map/pallas_call | solution.py:290
  17.2 0.1 collective-permute-start.2
  17.3 4.8 %collective-permute-start.3 = (bf16[128,128]{1,0:T(8,128)(2,1)S(1)}, bf16[128,128]{1,0:T(8,128)(2,1)S(1)}, u32[]{:S(2)}, u32[]{:S(2)}) collective-permute-start(bf16[128,128]{1,0:T(8,128)(2,1)S(1)} %get-tuple-element.36), channel_id=1, source_target_pairs={{8,0},{16,8},{24,16},{32,24},{40,32},{48,40},{56,48},{64,56},{72,6... | collective-permute-start | bytes 98312 | tf_op jit(solution)/shard_map/ppermute | solution.py:319
  22.0 1.3 %collective-permute-done.2.lo_ref = bf16[128,128]{1,0:T(8,128)(2,1)S(1)} collective-permute-done((bf16[128,128]{1,0:T(8,128)(2,1)S(1)}, bf16[128,128]{1,0:T(8,128)(2,1)S(1)}, u32[]{:S(2)}, u32[]{:S(2)}) %collective-permute-start.2) | collective-permute-done | bytes 32800 | tf_op jit(solution)/shard_map/ppermute | solution.py:319
  23.3 0.0 collective-permute-done.3.hi_ref
  23.4 2.0 %shard_map.105 = (bf16[4,2,10,16,768]{4,3,2,1,0:T(8,128)(2,1)S(1)}, f32[1024,128]{1,0:T(8,128)S(1)}, f32[1024,128]{1,0:T(8,128)S(1)}, bf16[128,128]{1,0:T(8,128)(2,1)S(1)}, bf16[128,128]{1,0:T(8,128)(2,1)S(1)}) custom-call(s32[4,26]{1,0:T(4,128)S(1)} %select_select_fusion.idx_ref, f32[1024,128]{1,0:T(8,128)S(1)} %get-tuple-element.34.a_ref, ...), custom_call_target="tpu_custom_call" | custom-call | flops 603979776 | bytes 5767168 | tf_op jit(solution)/shard_map/pallas_call | solution.py:290
  25.4 0.1 collective-permute-start.4
  25.5 4.9 %collective-permute-start.5 = (bf16[128,128]{1,0:T(8,128)(2,1)S(1)}, bf16[128,128]{1,0:T(8,128)(2,1)S(1)}, u32[]{:S(2)}, u32[]{:S(2)}) collective-permute-start(bf16[128,128]{1,0:T(8,128)(2,1)S(1)} %get-tuple-element.44), channel_id=1, source_target_pairs={{8,0},{16,8},{24,16},{32,24},{40,32},{48,40},{56,48},{64,56},{72,6... | collective-permute-start | bytes 98312 | tf_op jit(solution)/shard_map/ppermute | solution.py:319
  30.3 1.5 %shard_map.106 = (f32[1,4,64,512]{3,2,1,0:T(8,128)}, bf16[896,128]{1,0:T(8,128)(2,1)S(1)}) custom-call(bf16[4,2,10,16,768]{4,3,2,1,0:T(8,128)(2,1)S(1)} %get-tuple-element.39.x_ref, f32[1024,128]{1,0:T(8,128)S(1)} %get-tuple-element.40.e_ref.a_ref, f32[1024,128]{1,0:T(8,128)S(1)} %get-tuple-element.41.r_ref), custom_call_target="tpu_custom_call" | custom-call | flops 603979776 | bytes 3768320 | tf_op jit(solution)/shard_map/pallas_call | solution.py:290
  31.8 0.0 collective-permute-done.4.lo_ref
  31.8 0.0 collective-permute-done.5.hi_ref
  31.8 1.9 %shard_map.107 = (f32[1024,128]{1,0:T(8,128)S(1)}, f32[1024,128]{1,0:T(8,128)S(1)}, bf16[128,128]{1,0:T(8,128)(2,1)S(1)}, bf16[128,128]{1,0:T(8,128)(2,1)S(1)}) custom-call(s32[4,26]{1,0:T(4,128)S(1)} %select_select_fusion.idx_ref, f32[1024,128]{1,0:T(8,128)S(1)} %get-tuple-element.40.e_ref.a_ref, bf16[128,128]{1,0:T(8,128)(2,1)S(1)} %collective-permute-done.4.lo_ref, ...), custom_call_target="tpu_custom_call" | custom-call | flops 603979776 | bytes 4325376 | tf_op jit(solution)/shard_map/pallas_call | solution.py:290
  33.7 0.9 %shard_map.109 = bf16[1792,128]{1,0:T(8,128)(2,1)S(1)} custom-call(bf16[4,2,10,16,768]{4,3,2,1,0:T(8,128)(2,1)S(1)} %get-tuple-element.52.x_ref, f32[1024,128]{1,0:T(8,128)S(1)} %get-tuple-element.47.a_ref.e_ref, bf16[896,128]{1,0:T(8,128)(2,1)S(1)} %get-tuple-element.53.second_ref), custom_call_target="tpu_custom_call" | custom-call | flops 603979776 | bytes 3178496 | tf_op jit(solution)/shard_map/pallas_call | solution.py:290
  34.7 18.4 %all_to_all.15 = bf16[32,56,128]{2,1,0:T(8,128)(2,1)S(1)} all-to-all(bf16[32,56,128]{2,1,0:T(8,128)(2,1)S(1)} %bitcast.2), channel_id=1, replica_groups={{0,1,2,3,4,5,6,7,8,9,10,11,12,13,14,15,16,17,18,19,20,21,22,23,24,25,26..., dimensions={0} | all-to-all | bytes 917504 | tf_op jit(solution)/shard_map/all_to_all | solution.py:382
  53.1 0.1 reduce_sum.24
  53.2 16.4 %all_to_all.16 = bf16[8,56,128]{2,1,0:T(8,128)(2,1)S(1)} all-to-all(bf16[8,56,128]{2,1,0:T(8,128)(2,1)S(1)} %broadcast_in_dim.34), channel_id=1, replica_groups={{0,32,64,96,128,160,192,224},{8,40,72,104,136,168,200,232},{16,48,80,11..., dimensions={0} | all-to-all | bytes 229376 | tf_op jit(solution)/shard_map/all_to_all | solution.py:385
  69.6 0.8 broadcast_in_dim.35
  70.5 4.9 %all-to-all-start.2 = ((bf16[32,56,128]{2,1,0:T(8,128)(2,1)}), bf16[32,56,128]{2,1,0:T(8,128)(2,1)S(1)}, u32[]{:S(2)}, u32[]{:S(2)}) async-start(bf16[32,56,128]{2,1,0:T(8,128)(2,1)} %broadcast_in_dim.35), calls=%async_computation.2 | async-start | bytes 917504 | tf_op jit(solution)/shard_map/all_to_all | solution.py:382
  75.4 1.5 %collective-permute-start.6 = (bf16[128,128]{1,0:T(8,128)(2,1)S(1)}, bf16[128,128]{1,0:T(8,128)(2,1)S(1)}, u32[]{:S(2)}, u32[]{:S(2)}) collective-permute-start(bf16[128,128]{1,0:T(8,128)(2,1)S(1)} %get-tuple-element.48), channel_id=1, source_target_pairs={{0,8},{8,16},{16,24},{24,32},{32,40},{40,48},{48,56},{56,64},{64,7... | collective-permute-start | bytes 98312 | tf_op jit(solution)/shard_map/ppermute | solution.py:319
  76.8 3.4 %collective-permute-start.7 = (bf16[128,128]{1,0:T(8,128)(2,1)S(1)}, bf16[128,128]{1,0:T(8,128)(2,1)S(1)}, u32[]{:S(2)}, u32[]{:S(2)}) collective-permute-start(bf16[128,128]{1,0:T(8,128)(2,1)S(1)} %get-tuple-element.49), channel_id=1, source_target_pairs={{8,0},{16,8},{24,16},{32,24},{40,32},{48,40},{56,48},{64,56},{72,6... | collective-permute-start | bytes 98312 | tf_op jit(solution)/shard_map/ppermute | solution.py:319
  80.2 1.6 %collective-permute-done.6.lo_ref = bf16[128,128]{1,0:T(8,128)(2,1)S(1)} collective-permute-done((bf16[128,128]{1,0:T(8,128)(2,1)S(1)}, bf16[128,128]{1,0:T(8,128)(2,1)S(1)}, u32[]{:S(2)}, u32[]{:S(2)}) %collective-permute-start.6) | collective-permute-done | bytes 32800 | tf_op jit(solution)/shard_map/ppermute | solution.py:319
  81.8 1.3 %collective-permute-done.7.hi_ref = bf16[128,128]{1,0:T(8,128)(2,1)S(1)} collective-permute-done((bf16[128,128]{1,0:T(8,128)(2,1)S(1)}, bf16[128,128]{1,0:T(8,128)(2,1)S(1)}, u32[]{:S(2)}, u32[]{:S(2)}) %collective-permute-start.7) | collective-permute-done | bytes 32800 | tf_op jit(solution)/shard_map/ppermute | solution.py:319
  83.1 3.2 %shard_map.108 = f32[1,4,64,512]{3,2,1,0:T(8,128)} custom-call(s32[4,26]{1,0:T(4,128)S(1)} %select_select_fusion.idx_ref, f32[1024,128]{1,0:T(8,128)S(1)} %get-tuple-element.47.a_ref.e_ref, bf16[128,128]{1,0:T(8,128)(2,1)S(1)} %collective-permute-done.6.lo_ref, bf16[128,128]{1,0:T(8,128)(2,1)S(1)} %collective-permute-done.7.hi_ref, ...), custom_call_target="tpu_custom_call" | custom-call | flops 603979776 | bytes 3211264 | tf_op jit(solution)/shard_map/pallas_call | solution.py:290
  86.4 0.6 all-to-all-done.2
  87.0 1.6 %shard_map.110 = (f32[27,64,64]{2,1,0:T(8,128)}, f32[27,64,64]{2,1,0:T(8,128)}) custom-call(bf16[1792,128]{1,0:T(8,128)(2,1)S(1)} %bitcast.3), custom_call_target="tpu_custom_call" | custom-call | bytes 1343488 | tf_op jit(solution)/shard_map/pallas_call | solution.py:290
  (2 shorter events, 0.0 us)
Async XLA Ops:
  1.3 1.0 %copy-start = (f32[1,4,64,512]{3,2,1,0:T(8,128)S(1)}, f32[1,4,64,512]{3,2,1,0:T(8,128)}, u32[]{:S(2)}) copy-start(f32[1,4,64,512]{3,2,1,0:T(8,128)} %x_ref.1) | copy-start | bytes 1572868
  2.9 12.3 %collective-permute-start = (bf16[128,128]{1,0:T(8,128)(2,1)S(1)}, bf16[128,128]{1,0:T(8,128)(2,1)S(1)}, u32[]{:S(2)}, u32[]{:S(2)}) collective-permute-start(bf16[128,128]{1,0:T(8,128)(2,1)S(1)} %get-tuple-element.31), channel_id=1, source_target_pairs={{0,8},{8,16},{16,24},{24,32},{32,40},{40,48},{48,56},{56,64},{64,7... | collective-permute-start | bytes 98312 | tf_op jit(solution)/shard_map/ppermute | solution.py:319
  5.0 10.2 %collective-permute-start.1 = (bf16[128,128]{1,0:T(8,128)(2,1)S(1)}, bf16[128,128]{1,0:T(8,128)(2,1)S(1)}, u32[]{:S(2)}, u32[]{:S(2)}) collective-permute-start(bf16[128,128]{1,0:T(8,128)(2,1)S(1)} %get-tuple-element.32), channel_id=1, source_target_pairs={{8,0},{16,8},{24,16},{32,24},{40,32},{48,40},{56,48},{64,56},{72,6... | collective-permute-start | bytes 98312 | tf_op jit(solution)/shard_map/ppermute | solution.py:319
  17.2 6.2 %collective-permute-start.2 = (bf16[128,128]{1,0:T(8,128)(2,1)S(1)}, bf16[128,128]{1,0:T(8,128)(2,1)S(1)}, u32[]{:S(2)}, u32[]{:S(2)}) collective-permute-start(bf16[128,128]{1,0:T(8,128)(2,1)S(1)} %get-tuple-element.35), channel_id=1, source_target_pairs={{0,8},{8,16},{16,24},{24,32},{32,40},{40,48},{48,56},{56,64},{64,7... | collective-permute-start | bytes 98312 | tf_op jit(solution)/shard_map/ppermute | solution.py:319
  17.3 6.1 %collective-permute-start.3 = (bf16[128,128]{1,0:T(8,128)(2,1)S(1)}, bf16[128,128]{1,0:T(8,128)(2,1)S(1)}, u32[]{:S(2)}, u32[]{:S(2)}) collective-permute-start(bf16[128,128]{1,0:T(8,128)(2,1)S(1)} %get-tuple-element.36), channel_id=1, source_target_pairs={{8,0},{16,8},{24,16},{32,24},{40,32},{48,40},{56,48},{64,56},{72,6... | collective-permute-start | bytes 98312 | tf_op jit(solution)/shard_map/ppermute | solution.py:319
  25.4 6.4 %collective-permute-start.4 = (bf16[128,128]{1,0:T(8,128)(2,1)S(1)}, bf16[128,128]{1,0:T(8,128)(2,1)S(1)}, u32[]{:S(2)}, u32[]{:S(2)}) collective-permute-start(bf16[128,128]{1,0:T(8,128)(2,1)S(1)} %get-tuple-element.43), channel_id=1, source_target_pairs={{0,8},{8,16},{16,24},{24,32},{32,40},{40,48},{48,56},{56,64},{64,7... | collective-permute-start | bytes 98312 | tf_op jit(solution)/shard_map/ppermute | solution.py:319
  25.5 6.3 %collective-permute-start.5 = (bf16[128,128]{1,0:T(8,128)(2,1)S(1)}, bf16[128,128]{1,0:T(8,128)(2,1)S(1)}, u32[]{:S(2)}, u32[]{:S(2)}) collective-permute-start(bf16[128,128]{1,0:T(8,128)(2,1)S(1)} %get-tuple-element.44), channel_id=1, source_target_pairs={{8,0},{16,8},{24,16},{32,24},{40,32},{48,40},{56,48},{64,56},{72,6... | collective-permute-start | bytes 98312 | tf_op jit(solution)/shard_map/ppermute | solution.py:319
  70.5 16.5 %all-to-all-start.2 = ((bf16[32,56,128]{2,1,0:T(8,128)(2,1)}), bf16[32,56,128]{2,1,0:T(8,128)(2,1)S(1)}, u32[]{:S(2)}, u32[]{:S(2)}) async-start(bf16[32,56,128]{2,1,0:T(8,128)(2,1)} %broadcast_in_dim.35), calls=%async_computation.2 | async-start | bytes 917504 | tf_op jit(solution)/shard_map/all_to_all | solution.py:382
  75.4 6.5 %collective-permute-start.6 = (bf16[128,128]{1,0:T(8,128)(2,1)S(1)}, bf16[128,128]{1,0:T(8,128)(2,1)S(1)}, u32[]{:S(2)}, u32[]{:S(2)}) collective-permute-start(bf16[128,128]{1,0:T(8,128)(2,1)S(1)} %get-tuple-element.48), channel_id=1, source_target_pairs={{0,8},{8,16},{16,24},{24,32},{32,40},{40,48},{48,56},{56,64},{64,7... | collective-permute-start | bytes 98312 | tf_op jit(solution)/shard_map/ppermute | solution.py:319
  76.8 6.3 %collective-permute-start.7 = (bf16[128,128]{1,0:T(8,128)(2,1)S(1)}, bf16[128,128]{1,0:T(8,128)(2,1)S(1)}, u32[]{:S(2)}, u32[]{:S(2)}) collective-permute-start(bf16[128,128]{1,0:T(8,128)(2,1)S(1)} %get-tuple-element.49), channel_id=1, source_target_pairs={{8,0},{16,8},{24,16},{32,24},{40,32},{48,40},{56,48},{64,56},{72,6... | collective-permute-start | bytes 98312 | tf_op jit(solution)/shard_map/ppermute | solution.py:319

commit v5 on v4

v5 whole, which is shorter than its diff:
```python
import functools

import jax
import jax.numpy as jnp
from jax import lax
from jax.experimental import pallas as pl
from jax.experimental.pallas import tpu as pltpu
from jax.sharding import PartitionSpec as P


E = 8
C = 64
CAP = 4
f32 = jnp.float32
bf16 = jnp.bfloat16
offsets = [(a, b, c) for a in (-1, 0, 1) for b in (-1, 0, 1) for c in (-1, 0, 1)]
directions = [item for item in offsets if item != (0, 0, 0)]
number_of = {item: n for n, item in enumerate(directions)}

ROWS = CAP * 256
PLANE = CAP * 32
PACKED = 896


def row0(s, n, l):
    return s * 256 + (n // 2) * 128 + l * 16 + (n % 2) * 8


def flip(t):
    tt = t.T
    return jnp.concatenate([tt[:C], tt[C:]], axis=1)


def lane_low(shape):
    return lax.broadcasted_iota(jnp.int32, shape, 1) < C


def to_rows(x_ref, a_ref, tmp_ref, counts_ref, slots=range(CAP)):
    for s in slots:
        occupied = jnp.where(s < counts_ref[0], 1.0, 0.0).astype(f32)
        for n in range(4):
            t = x_ref[0, s, :, n * 128 : (n + 1) * 128] * occupied
            tmp_ref[s * 4 + n] = flip(t)
            for l in range(E):
                a_ref[pl.ds(row0(s, n, l), 8), :] = tmp_ref[s * 4 + n, pl.ds(l, 8, stride=8), :]


def from_rows(a_ref, o_ref, tmp_ref):
    for s in range(CAP):
        for n in range(4):
            for l in range(E):
                tmp_ref[s * 4 + n, pl.ds(l, 8, stride=8), :] = a_ref[pl.ds(row0(s, n, l), 8), :]
            o_ref[0, s, :, n * 128 : (n + 1) * 128] = flip(tmp_ref[s * 4 + n])


def planes_out(a_ref, up_ref, down_ref):
    for s in range(CAP):
        for nh in range(2):
            base = s * 256 + nh * 128
            to = pl.ds(s * 32 + nh * 16, 16)
            up_ref[to, :] = a_ref[pl.ds(base + 7 * 16, 16), :].astype(bf16)
            down_ref[to, :] = a_ref[pl.ds(base, 16), :].astype(bf16)


def pre_kernel(counts_ref, x_hbm, a_ref, up_ref, down_ref, tmp_ref, x_ref, sems):
    copies = [pltpu.make_async_copy(x_hbm.at[0, s], x_ref.at[0, s], sems.at[s]) for s in range(CAP)]
    for copy in copies:
        copy.start()
    for s in range(CAP):
        copies[s].wait()
        to_rows(x_ref, a_ref, tmp_ref, counts_ref, (s,))
    planes_out(a_ref, up_ref, down_ref)


def flat_weights(w_ref, o_ref, back):
    zero = jnp.zeros((C, C), f32)

    def block(a, b, c):
        k = 9 * (a + 1) + 3 * (b + 1) + (c + 1)
        return w_ref[26 - k].T if back else w_ref[k]

    blank = jnp.zeros((256, 128), bf16)
    for bi, b in enumerate((-1, 0, 1)):
        rows = pl.ds(bi * 256, 256)
        o_ref[0, rows, 128:] = blank
        o_ref[3, rows, :128] = blank
        for ci, c in enumerate((-1, 0, 1)):
            low, mid, high = (block(a, b, c) for a in (-1, 0, 1))
            left = jnp.concatenate([mid, high, zero, low], axis=0)
            right = jnp.concatenate([low, mid, high, zero], axis=0)
            joined = jnp.concatenate([left, right], axis=1).astype(bf16)
            o_ref[ci, rows, :128] = joined
            o_ref[ci + 1, rows, 128:] = joined


def prep1_kernel(w1_hbm, f1_ref, w1_ref, sem):
    copy = pltpu.make_async_copy(w1_hbm, w1_ref, sem)
    copy.start()
    copy.wait()
    flat_weights(w1_ref, f1_ref, False)


def prep2_kernel(counts_ref, w1_hbm, w2_hbm, x_hbm, f2_ref, b1_ref, b2_ref, u_ref, tmp_ref, w1_ref, w2_ref, x_ref, sems):
    pairs = ((w2_hbm, w2_ref), (w1_hbm, w1_ref), (x_hbm, x_ref))
    copies = [pltpu.make_async_copy(src, dst, sems.at[n]) for n, (src, dst) in enumerate(pairs)]
    for copy in copies:
        copy.start()
    copies[0].wait()
    flat_weights(w2_ref, f2_ref, False)
    flat_weights(w2_ref, b2_ref, True)
    copies[1].wait()
    flat_weights(w1_ref, b1_ref, True)
    copies[2].wait()
    to_rows(x_ref, u_ref, tmp_ref, counts_ref)


def build(idx_ref, source, x_ref, layers, c):
    row = lax.broadcasted_iota(jnp.int32, (8, 128), 0)
    low = lane_low((8, 128))

    def one_slot(s, carry):
        def tile(a, b, n, l):
            base = s * 256 if (a, b, c) == (0, 0, 0) else idx_ref[s, number_of[a, b, c]]
            return source(base, n, l)

        def pair(b, n, l):
            full = tile(0, b, n, l)
            after = tile(0, b, n + 1, l) if n < 3 else tile(1, b, 0, l)
            before = tile(0, b, n - 1, l) if n > 0 else tile(-1, b, 3, l)
            return full, jnp.where(low, after, before)

        for nh in range(2):
            for at, l in layers:
                parts = [[] for _ in range(6)]
                for nl in range(2):
                    n = 2 * nh + nl
                    own, left, right = pair(0, n, l), pair(-1, n, l), pair(1, n, l)
                    for h in range(2):
                        parts[h].append(pltpu.roll(jnp.where(row == 7, left[h], own[h]), 1, 0))
                        parts[2 + h].append(own[h])
                        parts[4 + h].append(pltpu.roll(jnp.where(row == 0, right[h], own[h]), 7, 0))
                for q in range(6):
                    x_ref[s, nh, at, :, q * 128 : (q + 1) * 128] = jnp.concatenate(parts[q], axis=0).astype(bf16)
        return carry

    lax.fori_loop(0, CAP, one_slot, 0)


def build_center(idx_ref, a_ref, g_ref, xc_ref):
    g_ref[pl.ds(0, ROWS), :] = a_ref[...]
    g_ref[pl.ds(ROWS, 256), :] = jnp.zeros((256, 128), f32)

    def source(base, n, l):
        return g_ref[pl.ds(pl.multiple_of(base + ((n // 2) * 128 + l * 16 + (n % 2) * 8), 8), 8), :]

    build(idx_ref, source, xc_ref, [(l, l) for l in range(E)], 0)


def build_outer(idx_ref, a_ref, lo_ref, hi_ref, pool_ref, xo_ref):
    for side, (ref, layer) in enumerate(((lo_ref, 7), (hi_ref, 0))):
        for s in range(CAP):
            for nh in range(2):
                pool_ref[side, pl.ds(s * 32 + nh * 16, 16), :] = a_ref[
                    pl.ds(s * 256 + nh * 128 + layer * 16, 16), :
                ]
        pool_ref[side, pl.ds(PLANE, PLANE), :] = ref[...].astype(f32)
        pool_ref[side, pl.ds(2 * PLANE, 32), :] = jnp.zeros((32, 128), f32)

        def source(base, n, l, side=side):
            return pool_ref[side, pl.ds(pl.multiple_of(base + ((n // 2) * 16 + (n % 2) * 8), 8), 8), :]

        build(idx_ref, source, xo_ref, [(side, 0)], -1 if side == 0 else 1)


def layers_of(xc_ref, xo_ref, first, count):
    parts = []
    if first == 0:
        parts.append(xo_ref[:, :, 0:1])
    low, high = max(first, 1), min(first + count, 9)
    if high > low:
        parts.append(xc_ref[:, :, low - 1 : high - 1])
    if first + count == 10:
        parts.append(xo_ref[:, :, 1:2])
    return parts[0] if len(parts) == 1 else jnp.concatenate(parts, axis=2)


def convolve(xc_ref, xo_ref, w_ref, pairs, epilogue):
    total = None
    count = len(pairs)
    for d in range(4):
        rows = jnp.concatenate([layers_of(xc_ref, xo_ref, d + 2 * m, 1) for m in pairs], axis=2)
        term = jnp.dot(rows.reshape(128 * count, 768), w_ref[d], preferred_element_type=f32)
        total = term if total is None else total + term
    for s in range(CAP):
        for nh in range(2):
            for i, m in enumerate(pairs):
                for h in range(2):
                    at = ((s * 2 + nh) * count + i) * 16
                    epilogue(s, nh, 2 * m + h, total[at : at + 16, h * 128 : h * 128 + 128])


CENTER = (1, 2)
OUTER = (0, 3)
ALL = (0, 1, 2, 3)


def full_rows(s, nh, l):
    return pl.ds(s * 256 + nh * 128 + l * 16, 16)


def center_rows(s, nh, l):
    return pl.ds((s * 2 + nh) * 64 + (l - 2) * 16, 16)


def take_center(part_ref, full_ref):
    for s in range(CAP):
        for nh in range(2):
            full_ref[pl.ds(s * 256 + nh * 128 + 32, 64), :] = part_ref[pl.ds((s * 2 + nh) * 64, 64), :]


def logistic(v):
    return 1.0 / (1.0 + jnp.exp(-v))


def first_layer(a, v):
    q = logistic(v)
    return a + v * q, q * (1.0 + v * (1.0 - q))


def second_layer(a, v, u):
    q = logistic(v)
    return a + v * q, u * (q * (1.0 + v * (1.0 - q)))


def second_back(v, u, slope):
    grad = u + v
    return grad, grad * slope


def center_kernel(formula, count, idx_ref, a_ref, w_ref, *refs):
    extra, (xc_ref, p_ref, q_ref, g_ref) = refs[:count], refs[count:]
    build_center(idx_ref, a_ref, g_ref, xc_ref)

    def epilogue(s, nh, l, v):
        full, part = full_rows(s, nh, l), center_rows(s, nh, l)
        p_ref[part, :], q_ref[part, :] = formula(v, a_ref[full, :], *[r[full, :] for r in extra])

    convolve(xc_ref, None, w_ref, CENTER, epilogue)


def outer_kernel(formula, count, send, idx_ref, a_ref, w_ref, lo_ref, hi_ref, xc_ref, pc_ref, qc_ref, *refs):
    extra, (xo_ref, p_ref, q_ref, up_ref, down_ref, pool_ref) = refs[:count], refs[count:]
    build_outer(idx_ref, a_ref, lo_ref, hi_ref, pool_ref, xo_ref)

    def epilogue(s, nh, l, v):
        full = full_rows(s, nh, l)
        p_ref[full, :], q_ref[full, :] = formula(v, a_ref[full, :], *[r[full, :] for r in extra])

    convolve(xc_ref, xo_ref, w_ref, OUTER, epilogue)
    planes_out((p_ref, q_ref)[send], up_ref, down_ref)
    take_center(pc_ref, p_ref)
    take_center(qc_ref, q_ref)


def last_kernel(idx_ref, a_ref, lo_ref, hi_ref, w_ref, hg_ref, o_ref, g_ref, pool_ref, xc_ref, xo_ref, r_ref, tmp_ref):
    build_center(idx_ref, a_ref, g_ref, xc_ref)
    build_outer(idx_ref, a_ref, lo_ref, hi_ref, pool_ref, xo_ref)

    def epilogue(s, nh, l, v):
        full = full_rows(s, nh, l)
        r_ref[full, :] = hg_ref[full, :] + v

    convolve(xc_ref, xo_ref, w_ref, ALL, epilogue)
    from_rows(r_ref, o_ref, tmp_ref)


def rows_kernel(r_ref, o_ref, tmp_ref):
    from_rows(r_ref, o_ref, tmp_ref)


def weight_grad(xc_ref, xo_ref, e_ref, p_ref):
    low = lane_low((C, 128))
    errors = e_ref[...].T.astype(bf16)
    held = None
    for c in range(3):
        rows = layers_of(xc_ref, xo_ref, c, E).reshape(ROWS, 768)
        m = jnp.dot(errors, rows, preferred_element_type=f32)
        for b in range(3):
            number = 3 * c + b
            z0, z1 = m[:C, b * 256 : b * 256 + 128], m[C:, b * 256 : b * 256 + 128]
            y0, y1 = m[:C, b * 256 + 128 : (b + 1) * 256], m[C:, b * 256 + 128 : (b + 1) * 256]
            p_ref[pl.ds(number * C, C), :] = (z0 + pltpu.roll(jnp.where(low, y1, z1), C, 1)).astype(p_ref.dtype)
            if number % 2 == 0:
                held = z1 + pltpu.roll(y0, C, 1)
                if number == 8:
                    p_ref[pl.ds((9 + number // 2) * C, C), :] = jnp.where(low, held, 0.0).astype(p_ref.dtype)
            else:
                odd = pltpu.roll(z1, C, 1) + y0
                p_ref[pl.ds((9 + number // 2) * C, C), :] = jnp.where(low, held, odd).astype(p_ref.dtype)


def w2_kernel(xc_ref, xo_ref, e_ref, p_ref):
    weight_grad(xc_ref, xo_ref, e_ref, p_ref)


def w1_kernel(xc_ref, xo_ref, e_ref, second_ref, p_ref):
    p_ref[pl.ds(PACKED, PACKED), :] = second_ref[...]
    weight_grad(xc_ref, xo_ref, e_ref, p_ref)


def finish_kernel(scale, r_ref, first_hbm, second_hbm, first_ref, second_ref, sems):
    copies = []
    for which, (ref, hbm) in enumerate(((first_ref, first_hbm), (second_ref, second_hbm))):
        for c in range(3):
            for b in range(3):
                number = 3 * c + b
                k = 3 * b + c
                t = (r_ref[pl.ds(which * PACKED + number * C, C), :].astype(f32) * scale).T
                ref[9 + k] = t[:C]
                ref[18 + k] = t[C:]
                if number % 2 == 0:
                    t = (r_ref[pl.ds(which * PACKED + (9 + number // 2) * C, C), :].astype(f32) * scale).T
                    held = t[C:]
                    ref[k] = t[:C]
                else:
                    ref[k] = held
        copy = pltpu.make_async_copy(ref, hbm, sems.at[which])
        copy.start()
        copies.append(copy)
    for copy in copies:
        copy.wait()


VMEM = pl.BlockSpec(memory_space=pltpu.VMEM)
SMEM = pl.BlockSpec(memory_space=pltpu.SMEM)
HBM = pl.BlockSpec(memory_space=pltpu.HBM)
FIELD = jax.ShapeDtypeStruct((ROWS, 128), f32)
PLANES = jax.ShapeDtypeStruct((PLANE, 128), bf16)
CENTERS = (CAP, 2, 8, 16, 768)
OUTERS = (CAP, 2, 2, 16, 768)
HALF = jax.ShapeDtypeStruct((ROWS // 2, 128), f32)
GRADS = jax.ShapeDtypeStruct((27, C, C), f32)
WEIGHTS = jax.ShapeDtypeStruct((4, 768, 256), bf16)
CUBES = jax.ShapeDtypeStruct((1, CAP, C, E * E * E), f32)
OWN = pltpu.VMEM((ROWS + 256, 128), f32)
POOL = pltpu.VMEM((2, 2 * PLANE + 32, 128), f32)
TMP = pltpu.VMEM((16, C, 128), f32)


def call(kernel, scalars, arrays, outs, scratch=(), flops=0, place=VMEM, result=VMEM):
    moved = sum(x.size * x.dtype.itemsize for x in arrays) + sum(o.size * o.dtype.itemsize for o in outs)
    return pl.pallas_call(
        kernel,
        out_shape=outs,
        in_specs=[SMEM] * len(scalars) + [place] * len(arrays),
        out_specs=[result] * len(outs),
        scratch_shapes=list(scratch),
        cost_estimate=pl.CostEstimate(flops=flops, bytes_accessed=moved, transcendentals=0),
        compiler_params=pltpu.CompilerParams(vmem_limit_bytes=24 << 20),
    )(*scalars, *arrays)


def slot_table(neighbours):
    own = neighbours - lax.axis_index("brick") * CAP
    depth = jnp.array([item[2] for item in directions], jnp.int32)[None, :]
    inside = jnp.clip(own, 0, CAP - 1)
    below = jnp.where(own >= 0, inside, jnp.clip(own + 2 * CAP, CAP, 2 * CAP - 1))
    above = jnp.clip(own, 0, 2 * CAP - 1)
    present = neighbours >= 0
    middle = jnp.where(present, inside * 256, ROWS)
    outer = jnp.where(present, jnp.where(depth < 0, below, above) * 32, 2 * PLANE)
    return jnp.where(depth == 0, middle, outer).astype(jnp.int32)


def step(features, cotangent, first_kernel, second_kernel, counts, neighbours):
    bricks = lax.axis_size("brick")
    up_pairs = [(i, (i + 1) % bricks) for i in range(bricks)]
    down_pairs = [(j, i) for i, j in up_pairs]

    def exchange(up, down):
        return lax.ppermute(up, "brick", up_pairs), lax.ppermute(down, "brick", down_pairs)

    idx = slot_table(neighbours)
    centers = jax.ShapeDtypeStruct(CENTERS, bf16)
    outers = jax.ShapeDtypeStruct(OUTERS, bf16)
    packed = jax.ShapeDtypeStruct((PACKED, 128), bf16)
    raw = pltpu.VMEM((27, C, C), f32)
    cubes = pltpu.VMEM((1, CAP, C, E * E * E), f32)
    work = 2 * ROWS * 2304 * 128
    features, cotangent, first_kernel, second_kernel = [
        pltpu.with_memory_space_constraint(v, pltpu.HBM) for v in (features, cotangent, first_kernel, second_kernel)
    ]

    def layer(formula, send, field, weights, extra, between):
        planes = between
        xc, pc, qc = call(
            functools.partial(center_kernel, formula, len(extra)),
            [idx],
            [field, weights] + extra,
            [centers, HALF, HALF],
            [OWN],
            work // 2,
        )
        xo, p, q, up, down = call(
            functools.partial(outer_kernel, formula, len(extra), send),
            [idx],
            [field, weights, *planes, xc, pc, qc] + extra,
            [outers, FIELD, FIELD, PLANES, PLANES],
            [POOL],
            work // 2,
        )
        return xc, xo, p, q, up, down

    inputs, up, down = call(
        pre_kernel,
        [counts],
        [features],
        [FIELD, PLANES, PLANES],
        [TMP, cubes, pltpu.SemaphoreType.DMA((CAP,))],
        place=HBM,
    )
    planes = exchange(up, down)
    (f1,) = call(prep1_kernel, [], [first_kernel], [WEIGHTS], [raw, pltpu.SemaphoreType.DMA], place=HBM)
    xc1, xo1, hidden, slope1, up, down = layer(lambda v, a: first_layer(a, v), 0, inputs, f1, [], planes)
    planes = exchange(up, down)
    f2, b1, b2, upstream = call(
        prep2_kernel,
        [counts],
        [first_kernel, second_kernel, cotangent],
        [WEIGHTS] * 3 + [FIELD],
        [TMP, raw, raw, cubes, pltpu.SemaphoreType.DMA((3,))],
        place=HBM,
    )
    xc2, xo2, out_rows, second_err, up, down = layer(
        lambda v, a, u: second_layer(a, v, u), 1, hidden, f2, [upstream], planes
    )
    planes = exchange(up, down)
    (second_local,) = call(w2_kernel, [], [xc2, xo2, second_err], [packed], (), work)
    _, _, hidden_grad, first_err, up, down = layer(
        lambda v, a, u, slope: second_back(v, u, slope), 1, second_err, b2, [upstream, slope1], planes
    )
    lo, hi = exchange(up, down)
    (partial,) = call(
        w1_kernel, [], [xc1, xo1, first_err, second_local], [jax.ShapeDtypeStruct((2 * PACKED, 128), bf16)], (), work
    )
    (input_grad,) = call(
        last_kernel,
        [idx],
        [first_err, lo, hi, b1, hidden_grad],
        [CUBES],
        [OWN, POOL, pltpu.VMEM(CENTERS, bf16), pltpu.VMEM(OUTERS, bf16), pltpu.VMEM((ROWS, 128), f32), TMP],
        work,
    )
    (outputs,) = call(rows_kernel, [], [out_rows], [CUBES], [TMP])
    axes = ("brick", "scene")
    scenes = lax.axis_size("scene")
    devices = bricks * scenes
    row = 4 if bricks % 4 == 0 else 1
    near, far = row * scenes, bricks // row
    near_groups = [list(range(z * near, (z + 1) * near)) for z in range(far)]
    far_groups = [[x + row * z for z in range(far)] for x in range(row)]
    share = 2 * PACKED // near

    def near_exchange(blocks):
        return lax.all_to_all(blocks, axes, 0, 0, axis_index_groups=near_groups, tiled=True)

    def far_exchange(blocks):
        return lax.all_to_all(blocks, "brick", 0, 0, axis_index_groups=far_groups, tiled=True)

    def total_of(blocks):
        return jnp.sum(blocks.astype(f32), axis=0).astype(bf16)

    def spread(block, count):
        return jnp.broadcast_to(block[None], (count,) + block.shape)

    scattered = near_exchange(partial.reshape(near, share, 128))
    mine = total_of(scattered)
    mine = total_of(far_exchange(spread(mine, far)))
    total = near_exchange(spread(mine, near))
    scale = float((devices * CAP * E * E * E) ** -0.5)
    first_grad, second_grad = call(
        functools.partial(finish_kernel, scale),
        [],
        [total.reshape(2 * PACKED, 128)],
        [GRADS, GRADS],
        [raw, raw, pltpu.SemaphoreType.DMA((2,))],
        result=HBM,
    )
    return (outputs, input_grad, first_grad, second_grad)


def solution(mesh):
    return jax.shard_map(
        step,
        mesh=mesh,
        in_specs=(
            P("scene", "brick", None, None),
            P("scene", "brick", None, None),
            P(),
            P(),
            P("brick"),
            P("brick", None),
        ),
        out_specs=(P("scene", "brick", None, None), P("scene", "brick", None, None), P(), P()),
        check_vma=False,
    )
```

time: 89 us -> 91 us (1.022)
  Pallas kernels: 16.6 us -> 23.4 us
  waiting for transfers between devices: 4.83 us -> 1.62 us
  blocking collectives: 34.8 us -> 33.3 us
    pallas_call x9 -> x14, Pallas kernels: 16.6 us -> 23.4 us  [call(): pl.pallas_call(kernel, out_shape=outs, in_specs=[SMEM] * len(scalars) + [...]
    ppermute x4, waiting for transfers between devices: 2.91 us -> 0.29 us  [exchange(): lax.ppermute(up, 'brick', up_pairs)]
    all_to_all x1, blocking collectives: 18.4 us -> 17.4 us  [near_exchange(): lax.all_to_all(blocks, axes, 0, 0, axis_index_groups=near_groups, tiled=T...]
  transfers between devices with their start and end apart: 9 -> 9, of which waited for: 4 -> 2; matrix products, arithmetic and copies ran while one was open for 1% -> 1% of each run, Pallas kernels for 8% -> 16%
where the time goes in v5:
time: 91 us; the launch traced here: 90.6 us
  blocking collectives  33.3 us (37%)
  starting transfers between devices  28 us (31%)
  Pallas kernels  23.4 us (26%)
  local copies, waits for them, and re-layouts  1.89 us (2%)
  waiting for transfers between devices  1.62 us (2%)
  between operations  1.61 us (2%)
    pallas_call x14, Pallas kernels, call(): pl.pallas_call(kernel, out_shape=outs, in_specs=[SMEM] * len(scalars) + [...  23.4 us
    ppermute x4, starting transfers between devices, exchange(): lax.ppermute(down, 'brick', down_pairs)  19.6 us
    all_to_all x1, blocking collectives, near_exchange(): lax.all_to_all(blocks, axes, 0, 0, axis_index_groups=near_groups, tiled=T...  17.4 us
    all_to_all x1, blocking collectives, far_exchange(): lax.all_to_all(blocks, 'brick', 0, 0, axis_index_groups=far_groups, tiled...  15.8 us
    all_to_all x1, starting transfers between devices, near_exchange(): lax.all_to_all(blocks, axes, 0, 0, axis_index_groups=near_groups, tiled=T...  4.71 us
    ppermute x4, starting transfers between devices, exchange(): lax.ppermute(up, 'brick', up_pairs)  3.76 us
  transfers between devices with their start and end apart: 9, of which 2 were waited for; matrix products, arithmetic and copies ran while one was open for 1% of the time, Pallas kernels for 16%

profile of v5, /device:TPU:1, one launch (start us, length us, event | category | flops | bytes accessed | tf_op | source)
XLA Modules:
  0.0 90.6 jit_solution(14991968569225432708)
XLA Ops:
  1.3 2.0 %shard_map.102 = (f32[1024,128]{1,0:T(8,128)S(1)}, bf16[128,128]{1,0:T(8,128)(2,1)S(1)}, bf16[128,128]{1,0:T(8,128)(2,1)S(1)}) custom-call(s32[1]{0:T(128)S(6)} %copy.11.counts_ref, f32[1,4,64,512]{3,2,1,0:T(8,128)} %x_hbm.2), custom_call_target="tpu_custom_call" | custom-call | bytes 1114112 | tf_op jit(solution)/shard_map/pallas_call | solution.py:352
  3.3 2.1 %collective-permute-start = (bf16[128,128]{1,0:T(8,128)(2,1)S(1)}, bf16[128,128]{1,0:T(8,128)(2,1)S(1)}, u32[]{:S(2)}, u32[]{:S(2)}) collective-permute-start(bf16[128,128]{1,0:T(8,128)(2,1)S(1)} %get-tuple-element.37), channel_id=1, source_target_pairs={{0,8},{8,16},{16,24},{24,32},{32,40},{40,48},{48,56},{56,64},{64,7... | collective-permute-start | bytes 98312 | tf_op jit(solution)/shard_map/ppermute | solution.py:381
  5.4 6.6 %collective-permute-start.1 = (bf16[128,128]{1,0:T(8,128)(2,1)S(1)}, bf16[128,128]{1,0:T(8,128)(2,1)S(1)}, u32[]{:S(2)}, u32[]{:S(2)}) collective-permute-start(bf16[128,128]{1,0:T(8,128)(2,1)S(1)} %get-tuple-element.38), channel_id=1, source_target_pairs={{8,0},{16,8},{24,16},{32,24},{40,32},{48,40},{56,48},{64,56},{72,6... | collective-permute-start | bytes 98312 | tf_op jit(solution)/shard_map/ppermute | solution.py:381
  12.0 0.7 select_select_fusion.idx_ref
  12.8 1.4 %shard_map.103.w_ref = bf16[4,768,256]{2,1,0:T(8,128)(2,1)S(1)} custom-call(f32[27,64,64]{2,1,0:T(8,128)} %w1_hbm.3), custom_call_target="tpu_custom_call" | custom-call | bytes 2015232 | tf_op jit(solution)/shard_map/pallas_call | solution.py:352
  14.2 1.5 %shard_map.104 = (bf16[4,2,8,16,768]{4,3,2,1,0:T(8,128)(2,1)S(1)}, f32[512,128]{1,0:T(8,128)S(1)}, f32[512,128]{1,0:T(8,128)S(1)}) custom-call(s32[4,26]{1,0:T(4,128)S(1)} %select_select_fusion.idx_ref, f32[1024,128]{1,0:T(8,128)S(1)} %get-tuple-element.36.a_ref, bf16[4,768,256]{2,1,0:T(8,128)(2,1)S(1)} %shard_map.103.w_ref), custom_call_target="tpu_custom_call" | custom-call | flops 301989888 | bytes 4194304 | tf_op jit(solution)/shard_map/pallas_call | solution.py:352
  15.7 0.0 collective-permute-done.lo_ref
  15.7 0.0 collective-permute-done.1.hi_ref
  15.7 1.4 %shard_map.105 = (bf16[4,2,2,16,768]{4,3,2,1,0:T(8,128)(2,1)S(1)}, f32[1024,128]{1,0:T(8,128)S(1)}, f32[1024,128]{1,0:T(8,128)S(1)}, bf16[128,128]{1,0:T(8,128)(2,1)S(1)}, bf16[128,128]{1,0:T(8,128)(2,1)S(1)}) custom-call(s32[4,26]{1,0:T(4,128)S(1)} %select_select_fusion.idx_ref, f32[1024,128]{1,0:T(8,128)S(1)} %get-tuple-element.36.a_ref, ...), custom_call_target="tpu_custom_call" | custom-call | flops 301989888 | bytes 5767168 | tf_op jit(solution)/shard_map/pallas_call | solution.py:352
  17.1 0.1 collective-permute-start.2
  17.2 4.8 %collective-permute-start.3 = (bf16[128,128]{1,0:T(8,128)(2,1)S(1)}, bf16[128,128]{1,0:T(8,128)(2,1)S(1)}, u32[]{:S(2)}, u32[]{:S(2)}) collective-permute-start(bf16[128,128]{1,0:T(8,128)(2,1)S(1)} %get-tuple-element.45), channel_id=1, source_target_pairs={{8,0},{16,8},{24,16},{32,24},{40,32},{48,40},{56,48},{64,56},{72,6... | collective-permute-start | bytes 98312 | tf_op jit(solution)/shard_map/ppermute | solution.py:381
  22.0 2.6 %shard_map.106 = (bf16[4,768,256]{2,1,0:T(8,128)(2,1)S(1)}, bf16[4,768,256]{2,1,0:T(8,128)(2,1)S(1)}, bf16[4,768,256]{2,1,0:T(8,128)(2,1)S(1)}, f32[1024,128]{1,0:T(8,128)S(1)}) custom-call(s32[1]{0:T(128)S(6)} %copy.11.counts_ref, f32[27,64,64]{2,1,0:T(8,128)} %w1_hbm.3, f32[27,64,64]{2,1,0:T(8,128)} %w2_hbm.1, f32[1,4,64,512]{3,2,1,0:T(8,128)} %x_hbm.3), custom_call_target="tpu_custom_call" | custom-call | bytes 6651904 | tf_op jit(solution)/shard_map/pallas_call | solution.py:352
  24.6 1.5 %shard_map.107 = (bf16[4,2,8,16,768]{4,3,2,1,0:T(8,128)(2,1)S(1)}, f32[512,128]{1,0:T(8,128)S(1)}, f32[512,128]{1,0:T(8,128)S(1)}) custom-call(s32[4,26]{1,0:T(4,128)S(1)} %select_select_fusion.idx_ref, f32[1024,128]{1,0:T(8,128)S(1)} %get-tuple-element.42.a_ref, bf16[4,768,256]{2,1,0:T(8,128)(2,1)S(1)} %get-tuple-element.43.w_ref, ...), custom_call_target="tpu_custom_call" | custom-call | flops 301989888 | bytes 4718592 | tf_op jit(solution)/shard_map/pallas_call | solution.py:352
  26.1 0.0 collective-permute-done.2.lo_ref
  26.1 0.0 collective-permute-done.3.hi_ref
  26.1 1.4 %shard_map.108 = (bf16[4,2,2,16,768]{4,3,2,1,0:T(8,128)(2,1)S(1)}, f32[1024,128]{1,0:T(8,128)S(1)}, f32[1024,128]{1,0:T(8,128)S(1)}, bf16[128,128]{1,0:T(8,128)(2,1)S(1)}, bf16[128,128]{1,0:T(8,128)(2,1)S(1)}) custom-call(s32[4,26]{1,0:T(4,128)S(1)} %select_select_fusion.idx_ref, f32[1024,128]{1,0:T(8,128)S(1)} %get-tuple-element.42.a_ref, ...), custom_call_target="tpu_custom_call" | custom-call | flops 301989888 | bytes 6291456 | tf_op jit(solution)/shard_map/pallas_call | solution.py:352
  27.5 0.1 collective-permute-start.4
  27.6 4.8 %collective-permute-start.5 = (bf16[128,128]{1,0:T(8,128)(2,1)S(1)}, bf16[128,128]{1,0:T(8,128)(2,1)S(1)}, u32[]{:S(2)}, u32[]{:S(2)}) collective-permute-start(bf16[128,128]{1,0:T(8,128)(2,1)S(1)} %get-tuple-element.54), channel_id=1, source_target_pairs={{8,0},{16,8},{24,16},{32,24},{40,32},{48,40},{56,48},{64,56},{72,6... | collective-permute-start | bytes 98312 | tf_op jit(solution)/shard_map/ppermute | solution.py:381
  32.3 0.9 %shard_map.113.second_ref = bf16[896,128]{1,0:T(8,128)(2,1)S(1)} custom-call(bf16[4,2,8,16,768]{4,3,2,1,0:T(8,128)(2,1)S(1)} %get-tuple-element.47.xc_ref, bf16[4,2,2,16,768]{4,3,2,1,0:T(8,128)(2,1)S(1)} %get-tuple-element.65.xo_ref, f32[1024,128]{1,0:T(8,128)S(1)} %get-tuple-element.51.a_ref.e_ref), custom_call_target="tpu_custom_call" | custom-call | flops 603979776 | bytes 2719744 | tf_op jit(solution)/shard_map/pallas_call | solution.py:352
  33.3 1.4 %shard_map.110 = (bf16[4,2,8,16,768]{4,3,2,1,0:T(8,128)(2,1)S(1)}, f32[512,128]{1,0:T(8,128)S(1)}, f32[512,128]{1,0:T(8,128)S(1)}) custom-call(s32[4,26]{1,0:T(4,128)S(1)} %select_select_fusion.idx_ref, f32[1024,128]{1,0:T(8,128)S(1)} %get-tuple-element.51.a_ref.e_ref, bf16[4,768,256]{2,1,0:T(8,128)(2,1)S(1)} %get-tuple-element.52.w_ref, ...), custom_call_target="tpu_custom_call" | custom-call | flops 301989888 | bytes 5242880 | tf_op jit(solution)/shard_map/pallas_call | solution.py:352
  34.7 0.0 collective-permute-done.4.lo_ref
  34.7 0.0 collective-permute-done.5.hi_ref
  34.7 2.0 %shard_map.111 = (bf16[4,2,2,16,768]{4,3,2,1,0:T(8,128)(2,1)}, f32[1024,128]{1,0:T(8,128)S(1)}, f32[1024,128]{1,0:T(8,128)S(1)}, bf16[128,128]{1,0:T(8,128)(2,1)S(1)}, bf16[128,128]{1,0:T(8,128)(2,1)S(1)}) custom-call(s32[4,26]{1,0:T(4,128)S(1)} %select_select_fusion.idx_ref, f32[1024,128]{1,0:T(8,128)S(1)} %get-tuple-element.51.a_ref.e_ref, ...), custom_call_target="tpu_custom_call" | custom-call | flops 301989888 | bytes 6815744 | tf_op jit(solution)/shard_map/pallas_call | solution.py:352
  36.8 0.0 copy-start
  36.8 0.9 %shard_map.114 = bf16[1792,128]{1,0:T(8,128)(2,1)S(1)} custom-call(bf16[4,2,8,16,768]{4,3,2,1,0:T(8,128)(2,1)S(1)} %get-tuple-element.39.xc_ref, bf16[4,2,2,16,768]{4,3,2,1,0:T(8,128)(2,1)S(1)} %get-tuple-element.64.xo_ref, f32[1024,128]{1,0:T(8,128)S(1)} %get-tuple-element.59.a_ref.e_ref, bf16[896,128]{1,0:T(8,128)(2,1)S(1)} %shard_map.113.second_ref), custom_call_target="tpu_custom_call" | custom-call | flops 603979776 | bytes 3178496 | tf_op jit(solution)/shard_map/pallas_call | solution.py:352
  37.7 0.0 copy-done
  37.7 17.4 %all_to_all.15 = bf16[32,56,128]{2,1,0:T(8,128)(2,1)S(1)} all-to-all(bf16[32,56,128]{2,1,0:T(8,128)(2,1)S(1)} %bitcast.2), channel_id=1, replica_groups={{0,1,2,3,4,5,6,7,8,9,10,11,12,13,14,15,16,17,18,19,20,21,22,23,24,25,26..., dimensions={0} | all-to-all | bytes 917504 | tf_op jit(solution)/shard_map/all_to_all | solution.py:465
  55.1 0.1 reduce_sum.24
  55.2 15.8 %all_to_all.16 = bf16[8,56,128]{2,1,0:T(8,128)(2,1)S(1)} all-to-all(bf16[8,56,128]{2,1,0:T(8,128)(2,1)S(1)} %broadcast_in_dim.34), channel_id=1, replica_groups={{0,32,64,96,128,160,192,224},{8,40,72,104,136,168,200,232},{16,48,80,11..., dimensions={0} | all-to-all | bytes 229376 | tf_op jit(solution)/shard_map/all_to_all | solution.py:468
  71.1 0.8 broadcast_in_dim.35
  71.9 4.7 %all-to-all-start.2 = ((bf16[32,56,128]{2,1,0:T(8,128)(2,1)}), bf16[32,56,128]{2,1,0:T(8,128)(2,1)S(1)}, u32[]{:S(2)}, u32[]{:S(2)}) async-start(bf16[32,56,128]{2,1,0:T(8,128)(2,1)} %broadcast_in_dim.35), calls=%async_computation.2 | async-start | bytes 917504 | tf_op jit(solution)/shard_map/all_to_all | solution.py:465
  76.6 1.5 %collective-permute-start.6 = (bf16[128,128]{1,0:T(8,128)(2,1)S(1)}, bf16[128,128]{1,0:T(8,128)(2,1)S(1)}, u32[]{:S(2)}, u32[]{:S(2)}) collective-permute-start(bf16[128,128]{1,0:T(8,128)(2,1)S(1)} %get-tuple-element.60), channel_id=1, source_target_pairs={{0,8},{8,16},{16,24},{24,32},{32,40},{40,48},{48,56},{56,64},{64,7... | collective-permute-start | bytes 98312 | tf_op jit(solution)/shard_map/ppermute | solution.py:381
  78.1 3.4 %collective-permute-start.7 = (bf16[128,128]{1,0:T(8,128)(2,1)S(1)}, bf16[128,128]{1,0:T(8,128)(2,1)S(1)}, u32[]{:S(2)}, u32[]{:S(2)}) collective-permute-start(bf16[128,128]{1,0:T(8,128)(2,1)S(1)} %get-tuple-element.61), channel_id=1, source_target_pairs={{8,0},{16,8},{24,16},{32,24},{40,32},{48,40},{56,48},{64,56},{72,6... | collective-permute-start | bytes 98312 | tf_op jit(solution)/shard_map/ppermute | solution.py:381
  81.5 1.3 %shard_map.109 = f32[1,4,64,512]{3,2,1,0:T(8,128)} custom-call(f32[1024,128]{1,0:T(8,128)S(1)} %get-tuple-element.50.r_ref), custom_call_target="tpu_custom_call" | custom-call | bytes 1048576 | tf_op jit(solution)/shard_map/pallas_call | solution.py:352
  82.8 0.3 collective-permute-done.6.lo_ref
  83.1 1.3 %collective-permute-done.7.hi_ref = bf16[128,128]{1,0:T(8,128)(2,1)S(1)} collective-permute-done((bf16[128,128]{1,0:T(8,128)(2,1)S(1)}, bf16[128,128]{1,0:T(8,128)(2,1)S(1)}, u32[]{:S(2)}, u32[]{:S(2)}) %collective-permute-start.7) | collective-permute-done | bytes 32800 | tf_op jit(solution)/shard_map/ppermute | solution.py:381
  84.4 0.0 copy-start.1
  84.4 1.0 %copy-done.1 = f32[1024,128]{1,0:T(8,128)S(1)} copy-done((f32[1024,128]{1,0:T(8,128)S(1)}, f32[1024,128]{1,0:T(8,128)}, u32[]{:S(2)}) %copy-start.1) | copy-done | bytes 524312
  85.5 3.3 %shard_map.112 = f32[1,4,64,512]{3,2,1,0:T(8,128)} custom-call(s32[4,26]{1,0:T(4,128)S(1)} %select_select_fusion.idx_ref, f32[1024,128]{1,0:T(8,128)S(1)} %get-tuple-element.59.a_ref.e_ref, bf16[128,128]{1,0:T(8,128)(2,1)S(1)} %collective-permute-done.6.lo_ref, bf16[128,128]{1,0:T(8,128)(2,1)S(1)} %collective-permute-done.7.hi_ref, ...), custom_call_target="tpu_custom_call" | custom-call | flops 603979776 | bytes 3211264 | tf_op jit(solution)/shard_map/pallas_call | solution.py:352
  88.8 0.0 all-to-all-done.2
  88.8 1.6 %shard_map.115 = (f32[27,64,64]{2,1,0:T(8,128)}, f32[27,64,64]{2,1,0:T(8,128)}) custom-call(bf16[1792,128]{1,0:T(8,128)(2,1)S(1)} %bitcast.3), custom_call_target="tpu_custom_call" | custom-call | bytes 1343488 | tf_op jit(solution)/shard_map/pallas_call | solution.py:352
  (2 shorter events, 0.0 us)
Async XLA Ops:
  3.3 12.4 %collective-permute-start = (bf16[128,128]{1,0:T(8,128)(2,1)S(1)}, bf16[128,128]{1,0:T(8,128)(2,1)S(1)}, u32[]{:S(2)}, u32[]{:S(2)}) collective-permute-start(bf16[128,128]{1,0:T(8,128)(2,1)S(1)} %get-tuple-element.37), channel_id=1, source_target_pairs={{0,8},{8,16},{16,24},{24,32},{32,40},{40,48},{48,56},{56,64},{64,7... | collective-permute-start | bytes 98312 | tf_op jit(solution)/shard_map/ppermute | solution.py:381
  5.4 10.3 %collective-permute-start.1 = (bf16[128,128]{1,0:T(8,128)(2,1)S(1)}, bf16[128,128]{1,0:T(8,128)(2,1)S(1)}, u32[]{:S(2)}, u32[]{:S(2)}) collective-permute-start(bf16[128,128]{1,0:T(8,128)(2,1)S(1)} %get-tuple-element.38), channel_id=1, source_target_pairs={{8,0},{16,8},{24,16},{32,24},{40,32},{48,40},{56,48},{64,56},{72,6... | collective-permute-start | bytes 98312 | tf_op jit(solution)/shard_map/ppermute | solution.py:381
  17.1 9.0 %collective-permute-start.2 = (bf16[128,128]{1,0:T(8,128)(2,1)S(1)}, bf16[128,128]{1,0:T(8,128)(2,1)S(1)}, u32[]{:S(2)}, u32[]{:S(2)}) collective-permute-start(bf16[128,128]{1,0:T(8,128)(2,1)S(1)} %get-tuple-element.44), channel_id=1, source_target_pairs={{0,8},{8,16},{16,24},{24,32},{32,40},{40,48},{48,56},{56,64},{64,7... | collective-permute-start | bytes 98312 | tf_op jit(solution)/shard_map/ppermute | solution.py:381
  17.2 8.9 %collective-permute-start.3 = (bf16[128,128]{1,0:T(8,128)(2,1)S(1)}, bf16[128,128]{1,0:T(8,128)(2,1)S(1)}, u32[]{:S(2)}, u32[]{:S(2)}) collective-permute-start(bf16[128,128]{1,0:T(8,128)(2,1)S(1)} %get-tuple-element.45), channel_id=1, source_target_pairs={{8,0},{16,8},{24,16},{32,24},{40,32},{48,40},{56,48},{64,56},{72,6... | collective-permute-start | bytes 98312 | tf_op jit(solution)/shard_map/ppermute | solution.py:381
  27.5 7.2 %collective-permute-start.4 = (bf16[128,128]{1,0:T(8,128)(2,1)S(1)}, bf16[128,128]{1,0:T(8,128)(2,1)S(1)}, u32[]{:S(2)}, u32[]{:S(2)}) collective-permute-start(bf16[128,128]{1,0:T(8,128)(2,1)S(1)} %get-tuple-element.53), channel_id=1, source_target_pairs={{0,8},{8,16},{16,24},{24,32},{32,40},{40,48},{48,56},{56,64},{64,7... | collective-permute-start | bytes 98312 | tf_op jit(solution)/shard_map/ppermute | solution.py:381
  27.6 7.2 %collective-permute-start.5 = (bf16[128,128]{1,0:T(8,128)(2,1)S(1)}, bf16[128,128]{1,0:T(8,128)(2,1)S(1)}, u32[]{:S(2)}, u32[]{:S(2)}) collective-permute-start(bf16[128,128]{1,0:T(8,128)(2,1)S(1)} %get-tuple-element.54), channel_id=1, source_target_pairs={{8,0},{16,8},{24,16},{32,24},{40,32},{48,40},{56,48},{64,56},{72,6... | collective-permute-start | bytes 98312 | tf_op jit(solution)/shard_map/ppermute | solution.py:381
  36.8 0.9 %copy-start = (f32[1024,128]{1,0:T(8,128)}, f32[1024,128]{1,0:T(8,128)S(1)}, u32[]{:S(2)}) copy-start(f32[1024,128]{1,0:T(8,128)S(1)} %get-tuple-element.63.hg_ref) | copy-start | bytes 1572868
  71.9 16.9 %all-to-all-start.2 = ((bf16[32,56,128]{2,1,0:T(8,128)(2,1)}), bf16[32,56,128]{2,1,0:T(8,128)(2,1)S(1)}, u32[]{:S(2)}, u32[]{:S(2)}) async-start(bf16[32,56,128]{2,1,0:T(8,128)(2,1)} %broadcast_in_dim.35), calls=%async_computation.2 | async-start | bytes 917504 | tf_op jit(solution)/shard_map/all_to_all | solution.py:465
  76.6 6.5 %collective-permute-start.6 = (bf16[128,128]{1,0:T(8,128)(2,1)S(1)}, bf16[128,128]{1,0:T(8,128)(2,1)S(1)}, u32[]{:S(2)}, u32[]{:S(2)}) collective-permute-start(bf16[128,128]{1,0:T(8,128)(2,1)S(1)} %get-tuple-element.60), channel_id=1, source_target_pairs={{0,8},{8,16},{16,24},{24,32},{32,40},{40,48},{48,56},{56,64},{64,7... | collective-permute-start | bytes 98312 | tf_op jit(solution)/shard_map/ppermute | solution.py:381
  78.1 6.3 %collective-permute-start.7 = (bf16[128,128]{1,0:T(8,128)(2,1)S(1)}, bf16[128,128]{1,0:T(8,128)(2,1)S(1)}, u32[]{:S(2)}, u32[]{:S(2)}) collective-permute-start(bf16[128,128]{1,0:T(8,128)(2,1)S(1)} %get-tuple-element.61), channel_id=1, source_target_pairs={{8,0},{16,8},{24,16},{32,24},{40,32},{48,40},{56,48},{64,56},{72,6... | collective-permute-start | bytes 98312 | tf_op jit(solution)/shard_map/ppermute | solution.py:381
  84.4 1.0 %copy-start.1 = (f32[1024,128]{1,0:T(8,128)S(1)}, f32[1024,128]{1,0:T(8,128)}, u32[]{:S(2)}) copy-start(f32[1024,128]{1,0:T(8,128)} %copy-done) | copy-start | bytes 1572868

commit v6 on v5

--- a/solution.py
+++ b/solution.py
@@ -35,8 +35,8 @@
     return lax.broadcasted_iota(jnp.int32, shape, 1) < C
 
 
-def to_rows(x_ref, a_ref, tmp_ref, counts_ref, slots=range(CAP)):
-    for s in slots:
+def to_rows(x_ref, a_ref, tmp_ref, counts_ref):
+    for s in range(CAP):
         occupied = jnp.where(s < counts_ref[0], 1.0, 0.0).astype(f32)
         for n in range(4):
             t = x_ref[0, s, :, n * 128 : (n + 1) * 128] * occupied
@@ -62,14 +62,18 @@
             down_ref[to, :] = a_ref[pl.ds(base, 16), :].astype(bf16)
 
 
-def pre_kernel(counts_ref, x_hbm, a_ref, up_ref, down_ref, tmp_ref, x_ref, sems):
-    copies = [pltpu.make_async_copy(x_hbm.at[0, s], x_ref.at[0, s], sems.at[s]) for s in range(CAP)]
+def pre_kernel(
+    counts_ref, x_hbm, w1_hbm, u_hbm, w2_hbm, a_ref, up_ref, down_ref, w1_ref, u_ref, w2_ref, tmp_ref, x_ref, sems
+):
+    pairs = ((x_hbm, x_ref), (w1_hbm, w1_ref), (w2_hbm, w2_ref), (u_hbm, u_ref))
+    copies = [pltpu.make_async_copy(src, dst, sems.at[n]) for n, (src, dst) in enumerate(pairs)]
     for copy in copies:
         copy.start()
-    for s in range(CAP):
-        copies[s].wait()
-        to_rows(x_ref, a_ref, tmp_ref, counts_ref, (s,))
+    copies[0].wait()
+    to_rows(x_ref, a_ref, tmp_ref, counts_ref)
     planes_out(a_ref, up_ref, down_ref)
+    for copy in copies[1:]:
+        copy.wait()
 
 
 def flat_weights(w_ref, o_ref, back):
@@ -93,25 +97,17 @@
             o_ref[ci + 1, rows, 128:] = joined
 
 
-def prep1_kernel(w1_hbm, f1_ref, w1_ref, sem):
-    copy = pltpu.make_async_copy(w1_hbm, w1_ref, sem)
-    copy.start()
-    copy.wait()
+def prep1_kernel(w1_ref, f1_ref):
     flat_weights(w1_ref, f1_ref, False)
 
 
-def prep2_kernel(counts_ref, w1_hbm, w2_hbm, x_hbm, f2_ref, b1_ref, b2_ref, u_ref, tmp_ref, w1_ref, w2_ref, x_ref, sems):
-    pairs = ((w2_hbm, w2_ref), (w1_hbm, w1_ref), (x_hbm, x_ref))
-    copies = [pltpu.make_async_copy(src, dst, sems.at[n]) for n, (src, dst) in enumerate(pairs)]
-    for copy in copies:
-        copy.start()
-    copies[0].wait()
+def prep2_kernel(counts_ref, w2_ref, x_ref, f2_ref, u_ref, tmp_ref):
     flat_weights(w2_ref, f2_ref, False)
-    flat_weights(w2_ref, b2_ref, True)
-    copies[1].wait()
-    flat_weights(w1_ref, b1_ref, True)
-    copies[2].wait()
     to_rows(x_ref, u_ref, tmp_ref, counts_ref)
+
+
+def back_kernel(w_ref, b_ref):
+    flat_weights(w_ref, b_ref, True)
 
 
 def build(idx_ref, source, x_ref, layers, c):
@@ -249,7 +245,7 @@
 
 
 def outer_kernel(formula, count, send, idx_ref, a_ref, w_ref, lo_ref, hi_ref, xc_ref, pc_ref, qc_ref, *refs):
-    extra, (xo_ref, p_ref, q_ref, up_ref, down_ref, pool_ref) = refs[:count], refs[count:]
+    extra, (p_ref, q_ref, up_ref, down_ref, xo_ref, pool_ref) = refs[:count], refs[count:]
     build_outer(idx_ref, a_ref, lo_ref, hi_ref, pool_ref, xo_ref)
 
     def epilogue(s, nh, l, v):
@@ -278,7 +274,7 @@
     from_rows(r_ref, o_ref, tmp_ref)
 
 
-def weight_grad(xc_ref, xo_ref, e_ref, p_ref):
+def weight_grad(xc_ref, xo_ref, e_ref, p_ref, ready=None):
     low = lane_low((C, 128))
     errors = e_ref[...].T.astype(bf16)
     held = None
@@ -297,15 +293,27 @@
             else:
                 odd = pltpu.roll(z1, C, 1) + y0
                 p_ref[pl.ds((9 + number // 2) * C, C), :] = jnp.where(low, held, odd).astype(p_ref.dtype)
+        if ready is not None:
+            ready(c)
 
 
 def w2_kernel(xc_ref, xo_ref, e_ref, p_ref):
     weight_grad(xc_ref, xo_ref, e_ref, p_ref)
 
 
-def w1_kernel(xc_ref, xo_ref, e_ref, second_ref, p_ref):
-    p_ref[pl.ds(PACKED, PACKED), :] = second_ref[...]
-    weight_grad(xc_ref, xo_ref, e_ref, p_ref)
+def w1_kernel(xc_ref, xo_ref, e_ref, second_ref, o_hbm, p_ref, sems):
+    copies = [pltpu.make_async_copy(second_ref, o_hbm.at[pl.ds(PACKED, PACKED)], sems.at[4])]
+    copies[0].start()
+
+    def send(n, start, size):
+        rows = pl.ds(start, size)
+        copies.append(pltpu.make_async_copy(p_ref.at[rows], o_hbm.at[rows], sems.at[n]))
+        copies[-1].start()
+
+    weight_grad(xc_ref, xo_ref, e_ref, p_ref, lambda c: send(c, c * 3 * C, 3 * C))
+    send(3, 9 * C, 5 * C)
+    for copy in copies:
+        copy.wait()
 
 
 def finish_kernel(scale, r_ref, first_hbm, second_hbm, first_ref, second_ref, sems):
@@ -391,7 +399,7 @@
         pltpu.with_memory_space_constraint(v, pltpu.HBM) for v in (features, cotangent, first_kernel, second_kernel)
     ]
 
-    def layer(formula, send, field, weights, extra, between):
+    def layer(formula, send, field, weights, extra, between, keep=True):
         planes = between
         xc, pc, qc = call(
             functools.partial(center_kernel, formula, len(extra)),
@@ -401,48 +409,51 @@
             [OWN],
             work // 2,
         )
-        xo, p, q, up, down = call(
+        made = call(
             functools.partial(outer_kernel, formula, len(extra), send),
             [idx],
             [field, weights, *planes, xc, pc, qc] + extra,
-            [outers, FIELD, FIELD, PLANES, PLANES],
-            [POOL],
+            [FIELD, FIELD, PLANES, PLANES] + ([outers] if keep else []),
+            [POOL] if keep else [pltpu.VMEM(OUTERS, bf16), POOL],
             work // 2,
         )
-        return xc, xo, p, q, up, down
-
-    inputs, up, down = call(
+        p, q, up, down = made[:4]
+        return xc, made[4] if keep else None, p, q, up, down
+
+    taps = jax.ShapeDtypeStruct((27, C, C), f32)
+    inputs, up, down, first_taps, raw_upstream, second_taps = call(
         pre_kernel,
         [counts],
-        [features],
-        [FIELD, PLANES, PLANES],
-        [TMP, cubes, pltpu.SemaphoreType.DMA((CAP,))],
+        [features, first_kernel, cotangent, second_kernel],
+        [FIELD, PLANES, PLANES, taps, CUBES, taps],
+        [TMP, cubes, pltpu.SemaphoreType.DMA((4,))],
         place=HBM,
     )
     planes = exchange(up, down)
-    (f1,) = call(prep1_kernel, [], [first_kernel], [WEIGHTS], [raw, pltpu.SemaphoreType.DMA], place=HBM)
+    (f1,) = call(prep1_kernel, [], [first_taps], [WEIGHTS])
     xc1, xo1, hidden, slope1, up, down = layer(lambda v, a: first_layer(a, v), 0, inputs, f1, [], planes)
     planes = exchange(up, down)
-    f2, b1, b2, upstream = call(
-        prep2_kernel,
-        [counts],
-        [first_kernel, second_kernel, cotangent],
-        [WEIGHTS] * 3 + [FIELD],
-        [TMP, raw, raw, cubes, pltpu.SemaphoreType.DMA((3,))],
-        place=HBM,
-    )
+    f2, upstream = call(prep2_kernel, [counts], [second_taps, raw_upstream], [WEIGHTS, FIELD], [TMP])
     xc2, xo2, out_rows, second_err, up, down = layer(
         lambda v, a, u: second_layer(a, v, u), 1, hidden, f2, [upstream], planes
     )
     planes = exchange(up, down)
+    (b2,) = call(back_kernel, [], [second_taps], [WEIGHTS])
     (second_local,) = call(w2_kernel, [], [xc2, xo2, second_err], [packed], (), work)
     _, _, hidden_grad, first_err, up, down = layer(
-        lambda v, a, u, slope: second_back(v, u, slope), 1, second_err, b2, [upstream, slope1], planes
+        lambda v, a, u, slope: second_back(v, u, slope), 1, second_err, b2, [upstream, slope1], planes, False
     )
     lo, hi = exchange(up, down)
     (partial,) = call(
-        w1_kernel, [], [xc1, xo1, first_err, second_local], [jax.ShapeDtypeStruct((2 * PACKED, 128), bf16)], (), work
-    )
+        w1_kernel,
+        [],
+        [xc1, xo1, first_err, second_local],
+        [jax.ShapeDtypeStruct((2 * PACKED, 128), bf16)],
+        [pltpu.VMEM((PACKED, 128), bf16), pltpu.SemaphoreType.DMA((5,))],
+        work,
+        result=HBM,
+    )
+    (b1,) = call(back_kernel, [], [first_taps], [WEIGHTS])
     (input_grad,) = call(
         last_kernel,
         [idx],

time: 91 us -> 87.5 us (0.962)
  Pallas kernels: 23.4 us -> 21.4 us
  local copies, waits for them, and re-layouts: 1.89 us -> 0.86 us
    pallas_call x14 -> x16, Pallas kernels: 23.4 us -> 21.4 us  [call(): pl.pallas_call(kernel, out_shape=outs, in_specs=[SMEM] * len(scalars) + [...]
    unnamed x4 -> x6, local copies, waits for them, and re-layouts: 1.05 us -> 0.02 us
  transfers between devices with their start and end apart: 9 -> 9, of which waited for: 2 -> 2; matrix products, arithmetic and copies ran while one was open for 1% -> 0% of each run, Pallas kernels for 16% -> 13%
where the time goes in v6:
time: 87.5 us; the launch traced here: 87.2 us
  blocking collectives  33.4 us (38%)
  starting transfers between devices  28 us (32%)
  Pallas kernels  21.4 us (24%)
  waiting for transfers between devices  1.75 us (2%)
  between operations  1.67 us (2%)
    pallas_call x16, Pallas kernels, call(): pl.pallas_call(kernel, out_shape=outs, in_specs=[SMEM] * len(scalars) + [...  21.4 us
    ppermute x4, starting transfers between devices, exchange(): lax.ppermute(down, 'brick', down_pairs)  19.6 us
    all_to_all x1, blocking collectives, near_exchange(): lax.all_to_all(blocks, axes, 0, 0, axis_index_groups=near_groups, tiled=T...  17.6 us
    all_to_all x1, blocking collectives, far_exchange(): lax.all_to_all(blocks, 'brick', 0, 0, axis_index_groups=far_groups, tiled...  15.8 us
    all_to_all x1, starting transfers between devices, near_exchange(): lax.all_to_all(blocks, axes, 0, 0, axis_index_groups=near_groups, tiled=T...  4.71 us
    ppermute x4, starting transfers between devices, exchange(): lax.ppermute(up, 'brick', up_pairs)  3.76 us
  transfers between devices with their start and end apart: 9, of which 2 were waited for; matrix products, arithmetic and copies ran while one was open for 0% of the time, Pallas kernels for 13%

profile of v6, /device:TPU:1, one launch (start us, length us, event | category | flops | bytes accessed | tf_op | source)
XLA Modules:
  0.0 87.2 jit_solution(10464271194167329101)
XLA Ops:
  0.6 0.0 copy-start.1
  0.6 0.0 copy-start.2
  0.7 0.0 copy-start
  1.3 1.8 %shard_map.102 = (f32[1024,128]{1,0:T(8,128)S(1)}, bf16[128,128]{1,0:T(8,128)(2,1)S(1)}, bf16[128,128]{1,0:T(8,128)(2,1)S(1)}, f32[27,64,64]{2,1,0:T(8,128)S(1)}...) custom-call(s32[1]{0:T(128)S(6)} %copy.11.counts_ref, f32[1,4,64,512]{3,2,1,0:T(8,128)} %x_hbm.1, ...), custom_call_target="tpu_custom_call" | custom-call | bytes 3932160 | tf_op jit(solution)/shard_map/pallas_call | solution.py:360
  3.1 2.1 %collective-permute-start = (bf16[128,128]{1,0:T(8,128)(2,1)S(1)}, bf16[128,128]{1,0:T(8,128)(2,1)S(1)}, u32[]{:S(2)}, u32[]{:S(2)}) collective-permute-start(bf16[128,128]{1,0:T(8,128)(2,1)S(1)} %get-tuple-element.39), channel_id=1, source_target_pairs={{0,8},{8,16},{16,24},{24,32},{32,40},{40,48},{48,56},{56,64},{64,7... | collective-permute-start | bytes 98312 | tf_op jit(solution)/shard_map/ppermute | solution.py:389
  5.2 6.6 %collective-permute-start.1 = (bf16[128,128]{1,0:T(8,128)(2,1)S(1)}, bf16[128,128]{1,0:T(8,128)(2,1)S(1)}, u32[]{:S(2)}, u32[]{:S(2)}) collective-permute-start(bf16[128,128]{1,0:T(8,128)(2,1)S(1)} %get-tuple-element.40), channel_id=1, source_target_pairs={{8,0},{16,8},{24,16},{32,24},{40,32},{48,40},{56,48},{64,56},{72,6... | collective-permute-start | bytes 98312 | tf_op jit(solution)/shard_map/ppermute | solution.py:389
  11.9 0.0 copy-done.1
  11.9 0.0 copy-done.2
  11.9 0.0 copy-done
  11.9 0.3 shard_map.103.w_ref
  12.2 1.5 %shard_map.104 = (bf16[4,2,8,16,768]{4,3,2,1,0:T(8,128)(2,1)S(1)}, f32[512,128]{1,0:T(8,128)S(1)}, f32[512,128]{1,0:T(8,128)S(1)}) custom-call(s32[4,26]{1,0:T(4,128)S(1)} %select_select_fusion.idx_ref, f32[1024,128]{1,0:T(8,128)S(1)} %get-tuple-element.37.a_ref, bf16[4,768,256]{2,1,0:T(8,128)(2,1)S(1)} %shard_map.103.w_ref), custom_call_target="tpu_custom_call" | custom-call | flops 301989888 | bytes 4194304 | tf_op jit(solution)/shard_map/pallas_call | solution.py:360
  13.7 0.0 collective-permute-done.lo_ref
  13.7 0.0 collective-permute-done.1.hi_ref
  13.7 1.4 %shard_map.105 = (f32[1024,128]{1,0:T(8,128)S(1)}, f32[1024,128]{1,0:T(8,128)S(1)}, bf16[128,128]{1,0:T(8,128)(2,1)S(1)}, bf16[128,128]{1,0:T(8,128)(2,1)S(1)}, bf16[4,2,2,16,768]{4,3,2,1,0:T(8,128)(2,1)S(1)}) custom-call(s32[4,26]{1,0:T(4,128)S(1)} %select_select_fusion.idx_ref, f32[1024,128]{1,0:T(8,128)S(1)} %get-tuple-element.37.a_ref, ...), custom_call_target="tpu_custom_call" | custom-call | flops 301989888 | bytes 5767168 | tf_op jit(solution)/shard_map/pallas_call | solution.py:360
  15.1 0.1 collective-permute-start.2
  15.2 4.8 %collective-permute-start.3 = (bf16[128,128]{1,0:T(8,128)(2,1)S(1)}, bf16[128,128]{1,0:T(8,128)(2,1)S(1)}, u32[]{:S(2)}, u32[]{:S(2)}) collective-permute-start(bf16[128,128]{1,0:T(8,128)(2,1)S(1)} %get-tuple-element.49), channel_id=1, source_target_pairs={{8,0},{16,8},{24,16},{32,24},{40,32},{48,40},{56,48},{64,56},{72,6... | collective-permute-start | bytes 98312 | tf_op jit(solution)/shard_map/ppermute | solution.py:389
  19.9 0.4 shard_map.110.w_ref
  20.3 0.7 shard_map.106
  21.1 1.5 %shard_map.107 = (bf16[4,2,8,16,768]{4,3,2,1,0:T(8,128)(2,1)S(1)}, f32[512,128]{1,0:T(8,128)S(1)}, f32[512,128]{1,0:T(8,128)S(1)}) custom-call(s32[4,26]{1,0:T(4,128)S(1)} %select_select_fusion.idx_ref, f32[1024,128]{1,0:T(8,128)S(1)} %get-tuple-element.44.a_ref, bf16[4,768,256]{2,1,0:T(8,128)(2,1)S(1)} %get-tuple-element.47.w_ref, ...), custom_call_target="tpu_custom_call" | custom-call | flops 301989888 | bytes 4718592 | tf_op jit(solution)/shard_map/pallas_call | solution.py:360
  22.6 0.0 collective-permute-done.2.lo_ref
  22.6 0.0 collective-permute-done.3.hi_ref
  22.6 1.4 %shard_map.108 = (f32[1024,128]{1,0:T(8,128)S(1)}, f32[1024,128]{1,0:T(8,128)S(1)}, bf16[128,128]{1,0:T(8,128)(2,1)S(1)}, bf16[128,128]{1,0:T(8,128)(2,1)S(1)}, bf16[4,2,2,16,768]{4,3,2,1,0:T(8,128)(2,1)S(1)}) custom-call(s32[4,26]{1,0:T(4,128)S(1)} %select_select_fusion.idx_ref, f32[1024,128]{1,0:T(8,128)S(1)} %get-tuple-element.44.a_ref, ...), custom_call_target="tpu_custom_call" | custom-call | flops 301989888 | bytes 6291456 | tf_op jit(solution)/shard_map/pallas_call | solution.py:360
  24.0 0.1 collective-permute-start.4
  24.0 4.8 %collective-permute-start.5 = (bf16[128,128]{1,0:T(8,128)(2,1)S(1)}, bf16[128,128]{1,0:T(8,128)(2,1)S(1)}, u32[]{:S(2)}, u32[]{:S(2)}) collective-permute-start(bf16[128,128]{1,0:T(8,128)(2,1)S(1)} %get-tuple-element.57), channel_id=1, source_target_pairs={{8,0},{16,8},{24,16},{32,24},{40,32},{48,40},{56,48},{64,56},{72,6... | collective-permute-start | bytes 98312 | tf_op jit(solution)/shard_map/ppermute | solution.py:389
  28.8 0.9 %shard_map.115.second_ref = bf16[896,128]{1,0:T(8,128)(2,1)S(1)} custom-call(bf16[4,2,8,16,768]{4,3,2,1,0:T(8,128)(2,1)S(1)} %get-tuple-element.51.xc_ref, bf16[4,2,2,16,768]{4,3,2,1,0:T(8,128)(2,1)S(1)} %get-tuple-element.67.xo_ref, f32[1024,128]{1,0:T(8,128)S(1)} %get-tuple-element.55.a_ref.e_ref), custom_call_target="tpu_custom_call" | custom-call | flops 603979776 | bytes 2719744 | tf_op jit(solution)/shard_map/pallas_call | solution.py:360
  29.8 1.4 %shard_map.111 = (bf16[4,2,8,16,768]{4,3,2,1,0:T(8,128)(2,1)S(1)}, f32[512,128]{1,0:T(8,128)S(1)}, f32[512,128]{1,0:T(8,128)S(1)}) custom-call(s32[4,26]{1,0:T(4,128)S(1)} %select_select_fusion.idx_ref, f32[1024,128]{1,0:T(8,128)S(1)} %get-tuple-element.55.a_ref.e_ref, bf16[4,768,256]{2,1,0:T(8,128)(2,1)S(1)} %shard_map.110.w_ref, ...), custom_call_target="tpu_custom_call" | custom-call | flops 301989888 | bytes 5242880 | tf_op jit(solution)/shard_map/pallas_call | solution.py:360
  31.2 0.0 collective-permute-done.4.lo_ref
  31.2 0.0 collective-permute-done.5.hi_ref
  31.2 1.3 %shard_map.112 = (f32[1024,128]{1,0:T(8,128)S(1)}, f32[1024,128]{1,0:T(8,128)S(1)}, bf16[128,128]{1,0:T(8,128)(2,1)S(1)}, bf16[128,128]{1,0:T(8,128)(2,1)S(1)}) custom-call(s32[4,26]{1,0:T(4,128)S(1)} %select_select_fusion.idx_ref, f32[1024,128]{1,0:T(8,128)S(1)} %get-tuple-element.55.a_ref.e_ref, bf16[4,768,256]{2,1,0:T(8,128)(2,1)S(1)} %shard_map.110.w_ref, ...), custom_call_target="tpu_custom_call" | custom-call | flops 301989888 | bytes 6422528 | tf_op jit(solution)/shard_map/pallas_call | solution.py:360
  32.5 2.2 %shard_map.116 = bf16[1792,128]{1,0:T(8,128)(2,1)S(1)} custom-call(bf16[4,2,8,16,768]{4,3,2,1,0:T(8,128)(2,1)S(1)} %get-tuple-element.41.xc_ref, bf16[4,2,2,16,768]{4,3,2,1,0:T(8,128)(2,1)S(1)} %get-tuple-element.66.xo_ref, f32[1024,128]{1,0:T(8,128)S(1)} %get-tuple-element.62.a_ref.e_ref, bf16[896,128]{1,0:T(8,128)(2,1)S(1)} %shard_map.115.second_ref), custom_call_target="tpu_custom_call" | custom-call | flops 603979776 | bytes 3178496 | tf_op jit(solution)/shard_map/pallas_call | solution.py:360
  34.7 17.6 %all_to_all.15 = bf16[32,56,128]{2,1,0:T(8,128)(2,1)S(1)} all-to-all(bf16[32,56,128]{2,1,0:T(8,128)(2,1)S(1)} %bitcast.2), channel_id=1, replica_groups={{0,1,2,3,4,5,6,7,8,9,10,11,12,13,14,15,16,17,18,19,20,21,22,23,24,25,26..., dimensions={0} | all-to-all | bytes 917504 | tf_op jit(solution)/shard_map/all_to_all | solution.py:476
  52.3 0.1 reduce_sum.24
  52.4 15.8 %all_to_all.16 = bf16[8,56,128]{2,1,0:T(8,128)(2,1)S(1)} all-to-all(bf16[8,56,128]{2,1,0:T(8,128)(2,1)S(1)} %broadcast_in_dim.34), channel_id=1, replica_groups={{0,32,64,96,128,160,192,224},{8,40,72,104,136,168,200,232},{16,48,80,11..., dimensions={0} | all-to-all | bytes 229376 | tf_op jit(solution)/shard_map/all_to_all | solution.py:479
  68.3 0.8 broadcast_in_dim.35
  69.1 4.7 %all-to-all-start.2 = ((bf16[32,56,128]{2,1,0:T(8,128)(2,1)}), bf16[32,56,128]{2,1,0:T(8,128)(2,1)S(1)}, u32[]{:S(2)}, u32[]{:S(2)}) async-start(bf16[32,56,128]{2,1,0:T(8,128)(2,1)} %broadcast_in_dim.35), calls=%async_computation.2 | async-start | bytes 917504 | tf_op jit(solution)/shard_map/all_to_all | solution.py:476
  73.8 1.5 %collective-permute-start.6 = (bf16[128,128]{1,0:T(8,128)(2,1)S(1)}, bf16[128,128]{1,0:T(8,128)(2,1)S(1)}, u32[]{:S(2)}, u32[]{:S(2)}) collective-permute-start(bf16[128,128]{1,0:T(8,128)(2,1)S(1)} %get-tuple-element.63), channel_id=1, source_target_pairs={{0,8},{8,16},{16,24},{24,32},{32,40},{40,48},{48,56},{56,64},{64,7... | collective-permute-start | bytes 98312 | tf_op jit(solution)/shard_map/ppermute | solution.py:389
  75.3 3.4 %collective-permute-start.7 = (bf16[128,128]{1,0:T(8,128)(2,1)S(1)}, bf16[128,128]{1,0:T(8,128)(2,1)S(1)}, u32[]{:S(2)}, u32[]{:S(2)}) collective-permute-start(bf16[128,128]{1,0:T(8,128)(2,1)S(1)} %get-tuple-element.64), channel_id=1, source_target_pairs={{8,0},{16,8},{24,16},{32,24},{40,32},{48,40},{56,48},{64,56},{72,6... | collective-permute-start | bytes 98312 | tf_op jit(solution)/shard_map/ppermute | solution.py:389
  78.7 0.4 shard_map.113.w_ref
  79.1 1.3 %shard_map.109 = f32[1,4,64,512]{3,2,1,0:T(8,128)} custom-call(f32[1024,128]{1,0:T(8,128)S(1)} %get-tuple-element.54.r_ref), custom_call_target="tpu_custom_call" | custom-call | bytes 1048576 | tf_op jit(solution)/shard_map/pallas_call | solution.py:360
  80.4 0.0 collective-permute-done.6.lo_ref
  80.4 1.2 %collective-permute-done.7.hi_ref = bf16[128,128]{1,0:T(8,128)(2,1)S(1)} collective-permute-done((bf16[128,128]{1,0:T(8,128)(2,1)S(1)}, bf16[128,128]{1,0:T(8,128)(2,1)S(1)}, u32[]{:S(2)}, u32[]{:S(2)}) %collective-permute-start.7) | collective-permute-done | bytes 32800 | tf_op jit(solution)/shard_map/ppermute | solution.py:389
  81.6 3.3 %shard_map.114 = f32[1,4,64,512]{3,2,1,0:T(8,128)} custom-call(s32[4,26]{1,0:T(4,128)S(1)} %select_select_fusion.idx_ref, f32[1024,128]{1,0:T(8,128)S(1)} %get-tuple-element.62.a_ref.e_ref, bf16[128,128]{1,0:T(8,128)(2,1)S(1)} %collective-permute-done.6.lo_ref, bf16[128,128]{1,0:T(8,128)(2,1)S(1)} %collective-permute-done.7.hi_ref, ...), custom_call_target="tpu_custom_call" | custom-call | flops 603979776 | bytes 3211264 | tf_op jit(solution)/shard_map/pallas_call | solution.py:360
  84.9 0.5 all-to-all-done.2
  85.4 1.6 %shard_map.117 = (f32[27,64,64]{2,1,0:T(8,128)}, f32[27,64,64]{2,1,0:T(8,128)}) custom-call(bf16[1792,128]{1,0:T(8,128)(2,1)S(1)} %bitcast.3), custom_call_target="tpu_custom_call" | custom-call | bytes 1343488 | tf_op jit(solution)/shard_map/pallas_call | solution.py:360
  (3 shorter events, 0.0 us)
Async XLA Ops:
  0.6 11.2 %copy-start.1 = (pred[26]{0:T(512)(128)(4,1)S(1)}, pred[26]{0:T(512)(128)(4,1)}, u32[]{:S(2)}) copy-start(pred[26]{0:T(512)(128)(4,1)} %constant.36) | copy-start | bytes 82
  0.6 11.2 %copy-start.2 = (pred[26]{0:T(512)(128)(4,1)S(1)}, pred[26]{0:T(512)(128)(4,1)}, u32[]{:S(2)}) copy-start(pred[26]{0:T(512)(128)(4,1)} %constant.37) | copy-start | bytes 82
  0.7 11.2 %copy-start = (s32[4,26]{1,0:T(4,128)S(1)}, s32[4,26]{1,0:T(4,128)}, u32[]{:S(2)}) copy-start(s32[4,26]{1,0:T(4,128)} %param.12) | copy-start | bytes 1252
  3.1 10.6 %collective-permute-start = (bf16[128,128]{1,0:T(8,128)(2,1)S(1)}, bf16[128,128]{1,0:T(8,128)(2,1)S(1)}, u32[]{:S(2)}, u32[]{:S(2)}) collective-permute-start(bf16[128,128]{1,0:T(8,128)(2,1)S(1)} %get-tuple-element.39), channel_id=1, source_target_pairs={{0,8},{8,16},{16,24},{24,32},{32,40},{40,48},{48,56},{56,64},{64,7... | collective-permute-start | bytes 98312 | tf_op jit(solution)/shard_map/ppermute | solution.py:389
  5.2 8.5 %collective-permute-start.1 = (bf16[128,128]{1,0:T(8,128)(2,1)S(1)}, bf16[128,128]{1,0:T(8,128)(2,1)S(1)}, u32[]{:S(2)}, u32[]{:S(2)}) collective-permute-start(bf16[128,128]{1,0:T(8,128)(2,1)S(1)} %get-tuple-element.40), channel_id=1, source_target_pairs={{8,0},{16,8},{24,16},{32,24},{40,32},{48,40},{56,48},{64,56},{72,6... | collective-permute-start | bytes 98312 | tf_op jit(solution)/shard_map/ppermute | solution.py:389
  15.1 7.5 %collective-permute-start.2 = (bf16[128,128]{1,0:T(8,128)(2,1)S(1)}, bf16[128,128]{1,0:T(8,128)(2,1)S(1)}, u32[]{:S(2)}, u32[]{:S(2)}) collective-permute-start(bf16[128,128]{1,0:T(8,128)(2,1)S(1)} %get-tuple-element.48), channel_id=1, source_target_pairs={{0,8},{8,16},{16,24},{24,32},{32,40},{40,48},{48,56},{56,64},{64,7... | collective-permute-start | bytes 98312 | tf_op jit(solution)/shard_map/ppermute | solution.py:389
  15.2 7.4 %collective-permute-start.3 = (bf16[128,128]{1,0:T(8,128)(2,1)S(1)}, bf16[128,128]{1,0:T(8,128)(2,1)S(1)}, u32[]{:S(2)}, u32[]{:S(2)}) collective-permute-start(bf16[128,128]{1,0:T(8,128)(2,1)S(1)} %get-tuple-element.49), channel_id=1, source_target_pairs={{8,0},{16,8},{24,16},{32,24},{40,32},{48,40},{56,48},{64,56},{72,6... | collective-permute-start | bytes 98312 | tf_op jit(solution)/shard_map/ppermute | solution.py:389
  24.0 7.3 %collective-permute-start.4 = (bf16[128,128]{1,0:T(8,128)(2,1)S(1)}, bf16[128,128]{1,0:T(8,128)(2,1)S(1)}, u32[]{:S(2)}, u32[]{:S(2)}) collective-permute-start(bf16[128,128]{1,0:T(8,128)(2,1)S(1)} %get-tuple-element.56), channel_id=1, source_target_pairs={{0,8},{8,16},{16,24},{24,32},{32,40},{40,48},{48,56},{56,64},{64,7... | collective-permute-start | bytes 98312 | tf_op jit(solution)/shard_map/ppermute | solution.py:389
  24.0 7.2 %collective-permute-start.5 = (bf16[128,128]{1,0:T(8,128)(2,1)S(1)}, bf16[128,128]{1,0:T(8,128)(2,1)S(1)}, u32[]{:S(2)}, u32[]{:S(2)}) collective-permute-start(bf16[128,128]{1,0:T(8,128)(2,1)S(1)} %get-tuple-element.57), channel_id=1, source_target_pairs={{8,0},{16,8},{24,16},{32,24},{40,32},{48,40},{56,48},{64,56},{72,6... | collective-permute-start | bytes 98312 | tf_op jit(solution)/shard_map/ppermute | solution.py:389
  69.1 16.3 %all-to-all-start.2 = ((bf16[32,56,128]{2,1,0:T(8,128)(2,1)}), bf16[32,56,128]{2,1,0:T(8,128)(2,1)S(1)}, u32[]{:S(2)}, u32[]{:S(2)}) async-start(bf16[32,56,128]{2,1,0:T(8,128)(2,1)} %broadcast_in_dim.35), calls=%async_computation.2 | async-start | bytes 917504 | tf_op jit(solution)/shard_map/all_to_all | solution.py:476
  73.8 6.6 %collective-permute-start.6 = (bf16[128,128]{1,0:T(8,128)(2,1)S(1)}, bf16[128,128]{1,0:T(8,128)(2,1)S(1)}, u32[]{:S(2)}, u32[]{:S(2)}) collective-permute-start(bf16[128,128]{1,0:T(8,128)(2,1)S(1)} %get-tuple-element.63), channel_id=1, source_target_pairs={{0,8},{8,16},{16,24},{24,32},{32,40},{40,48},{48,56},{56,64},{64,7... | collective-permute-start | bytes 98312 | tf_op jit(solution)/shard_map/ppermute | solution.py:389
  75.3 6.3 %collective-permute-start.7 = (bf16[128,128]{1,0:T(8,128)(2,1)S(1)}, bf16[128,128]{1,0:T(8,128)(2,1)S(1)}, u32[]{:S(2)}, u32[]{:S(2)}) collective-permute-start(bf16[128,128]{1,0:T(8,128)(2,1)S(1)} %get-tuple-element.64), channel_id=1, source_target_pairs={{8,0},{16,8},{24,16},{32,24},{40,32},{48,40},{56,48},{64,56},{72,6... | collective-permute-start | bytes 98312 | tf_op jit(solution)/shard_map/ppermute | solution.py:389

commit v7 on v6

--- a/solution.py
+++ b/solution.py
@@ -180,24 +180,36 @@
     return parts[0] if len(parts) == 1 else jnp.concatenate(parts, axis=2)
 
 
-def convolve(xc_ref, xo_ref, w_ref, pairs, epilogue):
+def convolve(xc_ref, xo_ref, w_ref, firsts, epilogue):
     total = None
-    count = len(pairs)
+    count = len(firsts)
     for d in range(4):
-        rows = jnp.concatenate([layers_of(xc_ref, xo_ref, d + 2 * m, 1) for m in pairs], axis=2)
+        rows = jnp.concatenate([layers_of(xc_ref, xo_ref, l + d, 1) for l in firsts], axis=2)
         term = jnp.dot(rows.reshape(128 * count, 768), w_ref[d], preferred_element_type=f32)
         total = term if total is None else total + term
     for s in range(CAP):
         for nh in range(2):
-            for i, m in enumerate(pairs):
+            for i, l in enumerate(firsts):
                 for h in range(2):
                     at = ((s * 2 + nh) * count + i) * 16
-                    epilogue(s, nh, 2 * m + h, total[at : at + 16, h * 128 : h * 128 + 128])
-
-
-CENTER = (1, 2)
-OUTER = (0, 3)
-ALL = (0, 1, 2, 3)
+                    epilogue(s, nh, l + h, total[at : at + 16, h * 128 : h * 128 + 128])
+
+
+def convolve_ends(xc_ref, xo_ref, w_ref, epilogue):
+    total = None
+    for c in range(3):
+        rows = jnp.concatenate([layers_of(xc_ref, xo_ref, l + c, 1) for l in (0, 7)], axis=2)
+        term = jnp.dot(rows.reshape(256, 768), w_ref[c, :, :128], preferred_element_type=f32)
+        total = term if total is None else total + term
+    for s in range(CAP):
+        for nh in range(2):
+            for i, l in enumerate((0, 7)):
+                at = ((s * 2 + nh) * 2 + i) * 16
+                epilogue(s, nh, l, total[at : at + 16])
+
+
+CENTER = (1, 3, 5)
+ALL = (0, 2, 4, 6)
 
 
 def full_rows(s, nh, l):
@@ -205,13 +217,13 @@
 
 
 def center_rows(s, nh, l):
-    return pl.ds((s * 2 + nh) * 64 + (l - 2) * 16, 16)
+    return pl.ds((s * 2 + nh) * 96 + (l - 1) * 16, 16)
 
 
 def take_center(part_ref, full_ref):
     for s in range(CAP):
         for nh in range(2):
-            full_ref[pl.ds(s * 256 + nh * 128 + 32, 64), :] = part_ref[pl.ds((s * 2 + nh) * 64, 64), :]
+            full_ref[pl.ds(s * 256 + nh * 128 + 16, 96), :] = part_ref[pl.ds((s * 2 + nh) * 96, 96), :]
 
 
 def logistic(v):
@@ -252,7 +264,7 @@
         full = full_rows(s, nh, l)
         p_ref[full, :], q_ref[full, :] = formula(v, a_ref[full, :], *[r[full, :] for r in extra])
 
-    convolve(xc_ref, xo_ref, w_ref, OUTER, epilogue)
+    convolve_ends(xc_ref, xo_ref, w_ref, epilogue)
     planes_out((p_ref, q_ref)[send], up_ref, down_ref)
     take_center(pc_ref, p_ref)
     take_center(qc_ref, q_ref)
@@ -346,7 +358,7 @@
 PLANES = jax.ShapeDtypeStruct((PLANE, 128), bf16)
 CENTERS = (CAP, 2, 8, 16, 768)
 OUTERS = (CAP, 2, 2, 16, 768)
-HALF = jax.ShapeDtypeStruct((ROWS // 2, 128), f32)
+MIDDLE = jax.ShapeDtypeStruct((ROWS * 3 // 4, 128), f32)
 GRADS = jax.ShapeDtypeStruct((27, C, C), f32)
 WEIGHTS = jax.ShapeDtypeStruct((4, 768, 256), bf16)
 CUBES = jax.ShapeDtypeStruct((1, CAP, C, E * E * E), f32)
@@ -405,7 +417,7 @@
             functools.partial(center_kernel, formula, len(extra)),
             [idx],
             [field, weights] + extra,
-            [centers, HALF, HALF],
+            [centers, MIDDLE, MIDDLE],
             [OWN],
             work // 2,
         )

time: 87.5 us -> 87.6 us (level)
  transfers between devices with their start and end apart: 9 -> 9, of which waited for: 2 -> 2; matrix products, arithmetic and copies ran while one was open for 0% -> 0% of each run, Pallas kernels for 13% -> 14%
where the time goes in v7:
time: 87.6 us; the launch traced here: 87.3 us
  blocking collectives  33.2 us (38%)
  starting transfers between devices  28 us (32%)
  Pallas kernels  21.6 us (25%)
  waiting for transfers between devices  1.75 us (2%)
  between operations  1.67 us (2%)
    pallas_call x16, Pallas kernels, call(): pl.pallas_call(kernel, out_shape=outs, in_specs=[SMEM] * len(scalars) + [...  21.6 us
    ppermute x4, starting transfers between devices, exchange(): lax.ppermute(down, 'brick', down_pairs)  19.6 us
    all_to_all x1, blocking collectives, near_exchange(): lax.all_to_all(blocks, axes, 0, 0, axis_index_groups=near_groups, tiled=T...  17.4 us
    all_to_all x1, blocking collectives, far_exchange(): lax.all_to_all(blocks, 'brick', 0, 0, axis_index_groups=far_groups, tiled...  15.8 us
    all_to_all x1, starting transfers between devices, near_exchange(): lax.all_to_all(blocks, axes, 0, 0, axis_index_groups=near_groups, tiled=T...  4.71 us
    ppermute x4, starting transfers between devices, exchange(): lax.ppermute(up, 'brick', up_pairs)  3.76 us
  transfers between devices with their start and end apart: 9, of which 2 were waited for; matrix products, arithmetic and copies ran while one was open for 0% of the time, Pallas kernels for 14%

profile of v7, /device:TPU:1, one launch (start us, length us, event | category | flops | bytes accessed | tf_op | source)
XLA Modules:
  0.0 87.3 jit_solution(11579718092982362819)
XLA Ops:
  0.6 0.0 copy-start.1
  0.6 0.0 copy-start.2
  0.7 0.0 copy-start
  1.3 1.8 %shard_map.102 = (f32[1024,128]{1,0:T(8,128)S(1)}, bf16[128,128]{1,0:T(8,128)(2,1)S(1)}, bf16[128,128]{1,0:T(8,128)(2,1)S(1)}, f32[27,64,64]{2,1,0:T(8,128)S(1)}...) custom-call(s32[1]{0:T(128)S(6)} %copy.11.counts_ref, f32[1,4,64,512]{3,2,1,0:T(8,128)} %x_hbm.1, ...), custom_call_target="tpu_custom_call" | custom-call | bytes 3932160 | tf_op jit(solution)/shard_map/pallas_call | solution.py:372
  3.1 2.1 %collective-permute-start = (bf16[128,128]{1,0:T(8,128)(2,1)S(1)}, bf16[128,128]{1,0:T(8,128)(2,1)S(1)}, u32[]{:S(2)}, u32[]{:S(2)}) collective-permute-start(bf16[128,128]{1,0:T(8,128)(2,1)S(1)} %get-tuple-element.39), channel_id=1, source_target_pairs={{0,8},{8,16},{16,24},{24,32},{32,40},{40,48},{48,56},{56,64},{64,7... | collective-permute-start | bytes 98312 | tf_op jit(solution)/shard_map/ppermute | solution.py:401
  5.2 6.6 %collective-permute-start.1 = (bf16[128,128]{1,0:T(8,128)(2,1)S(1)}, bf16[128,128]{1,0:T(8,128)(2,1)S(1)}, u32[]{:S(2)}, u32[]{:S(2)}) collective-permute-start(bf16[128,128]{1,0:T(8,128)(2,1)S(1)} %get-tuple-element.40), channel_id=1, source_target_pairs={{8,0},{16,8},{24,16},{32,24},{40,32},{48,40},{56,48},{64,56},{72,6... | collective-permute-start | bytes 98312 | tf_op jit(solution)/shard_map/ppermute | solution.py:401
  11.9 0.0 copy-done.1
  11.9 0.0 copy-done.2
  11.9 0.0 copy-done
  11.9 0.3 shard_map.103.w_ref
  12.2 1.7 %shard_map.104 = (bf16[4,2,8,16,768]{4,3,2,1,0:T(8,128)(2,1)S(1)}, f32[768,128]{1,0:T(8,128)S(1)}, f32[768,128]{1,0:T(8,128)S(1)}) custom-call(s32[4,26]{1,0:T(4,128)S(1)} %select_select_fusion.idx_ref, f32[1024,128]{1,0:T(8,128)S(1)} %get-tuple-element.37.a_ref, bf16[4,768,256]{2,1,0:T(8,128)(2,1)S(1)} %shard_map.103.w_ref), custom_call_target="tpu_custom_call" | custom-call | flops 301989888 | bytes 4456448 | tf_op jit(solution)/shard_map/pallas_call | solution.py:372
  13.9 0.0 collective-permute-done.lo_ref
  13.9 0.0 collective-permute-done.1.hi_ref
  13.9 1.2 %shard_map.105 = (f32[1024,128]{1,0:T(8,128)S(1)}, f32[1024,128]{1,0:T(8,128)S(1)}, bf16[128,128]{1,0:T(8,128)(2,1)S(1)}, bf16[128,128]{1,0:T(8,128)(2,1)S(1)}, bf16[4,2,2,16,768]{4,3,2,1,0:T(8,128)(2,1)S(1)}) custom-call(s32[4,26]{1,0:T(4,128)S(1)} %select_select_fusion.idx_ref, f32[1024,128]{1,0:T(8,128)S(1)} %get-tuple-element.37.a_ref, ...), custom_call_target="tpu_custom_call" | custom-call | flops 301989888 | bytes 6029312 | tf_op jit(solution)/shard_map/pallas_call | solution.py:372
  15.1 0.1 collective-permute-start.2
  15.2 4.8 %collective-permute-start.3 = (bf16[128,128]{1,0:T(8,128)(2,1)S(1)}, bf16[128,128]{1,0:T(8,128)(2,1)S(1)}, u32[]{:S(2)}, u32[]{:S(2)}) collective-permute-start(bf16[128,128]{1,0:T(8,128)(2,1)S(1)} %get-tuple-element.49), channel_id=1, source_target_pairs={{8,0},{16,8},{24,16},{32,24},{40,32},{48,40},{56,48},{64,56},{72,6... | collective-permute-start | bytes 98312 | tf_op jit(solution)/shard_map/ppermute | solution.py:401
  20.0 0.4 shard_map.110.w_ref
  20.4 0.7 shard_map.106
  21.1 1.7 %shard_map.107 = (bf16[4,2,8,16,768]{4,3,2,1,0:T(8,128)(2,1)S(1)}, f32[768,128]{1,0:T(8,128)S(1)}, f32[768,128]{1,0:T(8,128)S(1)}) custom-call(s32[4,26]{1,0:T(4,128)S(1)} %select_select_fusion.idx_ref, f32[1024,128]{1,0:T(8,128)S(1)} %get-tuple-element.44.a_ref, bf16[4,768,256]{2,1,0:T(8,128)(2,1)S(1)} %get-tuple-element.47.w_ref, ...), custom_call_target="tpu_custom_call" | custom-call | flops 301989888 | bytes 4980736 | tf_op jit(solution)/shard_map/pallas_call | solution.py:372
  22.9 0.0 collective-permute-done.2.lo_ref
  22.9 0.0 collective-permute-done.3.hi_ref
  22.9 1.2 %shard_map.108 = (f32[1024,128]{1,0:T(8,128)S(1)}, f32[1024,128]{1,0:T(8,128)S(1)}, bf16[128,128]{1,0:T(8,128)(2,1)S(1)}, bf16[128,128]{1,0:T(8,128)(2,1)S(1)}, bf16[4,2,2,16,768]{4,3,2,1,0:T(8,128)(2,1)S(1)}) custom-call(s32[4,26]{1,0:T(4,128)S(1)} %select_select_fusion.idx_ref, f32[1024,128]{1,0:T(8,128)S(1)} %get-tuple-element.44.a_ref, ...), custom_call_target="tpu_custom_call" | custom-call | flops 301989888 | bytes 6553600 | tf_op jit(solution)/shard_map/pallas_call | solution.py:372
  24.1 0.1 collective-permute-start.4
  24.2 4.8 %collective-permute-start.5 = (bf16[128,128]{1,0:T(8,128)(2,1)S(1)}, bf16[128,128]{1,0:T(8,128)(2,1)S(1)}, u32[]{:S(2)}, u32[]{:S(2)}) collective-permute-start(bf16[128,128]{1,0:T(8,128)(2,1)S(1)} %get-tuple-element.57), channel_id=1, source_target_pairs={{8,0},{16,8},{24,16},{32,24},{40,32},{48,40},{56,48},{64,56},{72,6... | collective-permute-start | bytes 98312 | tf_op jit(solution)/shard_map/ppermute | solution.py:401
  29.0 0.9 %shard_map.115.second_ref = bf16[896,128]{1,0:T(8,128)(2,1)S(1)} custom-call(bf16[4,2,8,16,768]{4,3,2,1,0:T(8,128)(2,1)S(1)} %get-tuple-element.51.xc_ref, bf16[4,2,2,16,768]{4,3,2,1,0:T(8,128)(2,1)S(1)} %get-tuple-element.67.xo_ref, f32[1024,128]{1,0:T(8,128)S(1)} %get-tuple-element.55.a_ref.e_ref), custom_call_target="tpu_custom_call" | custom-call | flops 603979776 | bytes 2719744 | tf_op jit(solution)/shard_map/pallas_call | solution.py:372
  29.9 1.6 %shard_map.111 = (bf16[4,2,8,16,768]{4,3,2,1,0:T(8,128)(2,1)S(1)}, f32[768,128]{1,0:T(8,128)S(1)}, f32[768,128]{1,0:T(8,128)S(1)}) custom-call(s32[4,26]{1,0:T(4,128)S(1)} %select_select_fusion.idx_ref, f32[1024,128]{1,0:T(8,128)S(1)} %get-tuple-element.55.a_ref.e_ref, bf16[4,768,256]{2,1,0:T(8,128)(2,1)S(1)} %shard_map.110.w_ref, ...), custom_call_target="tpu_custom_call" | custom-call | flops 301989888 | bytes 5505024 | tf_op jit(solution)/shard_map/pallas_call | solution.py:372
  31.6 0.0 collective-permute-done.4.lo_ref
  31.6 0.0 collective-permute-done.5.hi_ref
  31.6 1.2 %shard_map.112 = (f32[1024,128]{1,0:T(8,128)S(1)}, f32[1024,128]{1,0:T(8,128)S(1)}, bf16[128,128]{1,0:T(8,128)(2,1)S(1)}, bf16[128,128]{1,0:T(8,128)(2,1)S(1)}) custom-call(s32[4,26]{1,0:T(4,128)S(1)} %select_select_fusion.idx_ref, f32[1024,128]{1,0:T(8,128)S(1)} %get-tuple-element.55.a_ref.e_ref, bf16[4,768,256]{2,1,0:T(8,128)(2,1)S(1)} %shard_map.110.w_ref, ...), custom_call_target="tpu_custom_call" | custom-call | flops 301989888 | bytes 6684672 | tf_op jit(solution)/shard_map/pallas_call | solution.py:372
  32.8 2.2 %shard_map.116 = bf16[1792,128]{1,0:T(8,128)(2,1)S(1)} custom-call(bf16[4,2,8,16,768]{4,3,2,1,0:T(8,128)(2,1)S(1)} %get-tuple-element.41.xc_ref, bf16[4,2,2,16,768]{4,3,2,1,0:T(8,128)(2,1)S(1)} %get-tuple-element.66.xo_ref, f32[1024,128]{1,0:T(8,128)S(1)} %get-tuple-element.62.a_ref.e_ref, bf16[896,128]{1,0:T(8,128)(2,1)S(1)} %shard_map.115.second_ref), custom_call_target="tpu_custom_call" | custom-call | flops 603979776 | bytes 3178496 | tf_op jit(solution)/shard_map/pallas_call | solution.py:372
  35.0 17.4 %all_to_all.15 = bf16[32,56,128]{2,1,0:T(8,128)(2,1)S(1)} all-to-all(bf16[32,56,128]{2,1,0:T(8,128)(2,1)S(1)} %bitcast.2), channel_id=1, replica_groups={{0,1,2,3,4,5,6,7,8,9,10,11,12,13,14,15,16,17,18,19,20,21,22,23,24,25,26..., dimensions={0} | all-to-all | bytes 917504 | tf_op jit(solution)/shard_map/all_to_all | solution.py:488
  52.4 0.1 reduce_sum.24
  52.5 15.8 %all_to_all.16 = bf16[8,56,128]{2,1,0:T(8,128)(2,1)S(1)} all-to-all(bf16[8,56,128]{2,1,0:T(8,128)(2,1)S(1)} %broadcast_in_dim.34), channel_id=1, replica_groups={{0,32,64,96,128,160,192,224},{8,40,72,104,136,168,200,232},{16,48,80,11..., dimensions={0} | all-to-all | bytes 229376 | tf_op jit(solution)/shard_map/all_to_all | solution.py:491
  68.3 0.8 broadcast_in_dim.35
  69.2 4.7 %all-to-all-start.2 = ((bf16[32,56,128]{2,1,0:T(8,128)(2,1)}), bf16[32,56,128]{2,1,0:T(8,128)(2,1)S(1)}, u32[]{:S(2)}, u32[]{:S(2)}) async-start(bf16[32,56,128]{2,1,0:T(8,128)(2,1)} %broadcast_in_dim.35), calls=%async_computation.2 | async-start | bytes 917504 | tf_op jit(solution)/shard_map/all_to_all | solution.py:488
  73.9 1.5 %collective-permute-start.6 = (bf16[128,128]{1,0:T(8,128)(2,1)S(1)}, bf16[128,128]{1,0:T(8,128)(2,1)S(1)}, u32[]{:S(2)}, u32[]{:S(2)}) collective-permute-start(bf16[128,128]{1,0:T(8,128)(2,1)S(1)} %get-tuple-element.63), channel_id=1, source_target_pairs={{0,8},{8,16},{16,24},{24,32},{32,40},{40,48},{48,56},{56,64},{64,7... | collective-permute-start | bytes 98312 | tf_op jit(solution)/shard_map/ppermute | solution.py:401
  75.4 3.4 %collective-permute-start.7 = (bf16[128,128]{1,0:T(8,128)(2,1)S(1)}, bf16[128,128]{1,0:T(8,128)(2,1)S(1)}, u32[]{:S(2)}, u32[]{:S(2)}) collective-permute-start(bf16[128,128]{1,0:T(8,128)(2,1)S(1)} %get-tuple-element.64), channel_id=1, source_target_pairs={{8,0},{16,8},{24,16},{32,24},{40,32},{48,40},{56,48},{64,56},{72,6... | collective-permute-start | bytes 98312 | tf_op jit(solution)/shard_map/ppermute | solution.py:401
  78.8 0.4 shard_map.113.w_ref
  79.2 1.3 %shard_map.109 = f32[1,4,64,512]{3,2,1,0:T(8,128)} custom-call(f32[1024,128]{1,0:T(8,128)S(1)} %get-tuple-element.54.r_ref), custom_call_target="tpu_custom_call" | custom-call | bytes 1048576 | tf_op jit(solution)/shard_map/pallas_call | solution.py:372
  80.5 0.0 collective-permute-done.6.lo_ref
  80.5 1.2 %collective-permute-done.7.hi_ref = bf16[128,128]{1,0:T(8,128)(2,1)S(1)} collective-permute-done((bf16[128,128]{1,0:T(8,128)(2,1)S(1)}, bf16[128,128]{1,0:T(8,128)(2,1)S(1)}, u32[]{:S(2)}, u32[]{:S(2)}) %collective-permute-start.7) | collective-permute-done | bytes 32800 | tf_op jit(solution)/shard_map/ppermute | solution.py:401
  81.7 3.3 %shard_map.114 = f32[1,4,64,512]{3,2,1,0:T(8,128)} custom-call(s32[4,26]{1,0:T(4,128)S(1)} %select_select_fusion.idx_ref, f32[1024,128]{1,0:T(8,128)S(1)} %get-tuple-element.62.a_ref.e_ref, bf16[128,128]{1,0:T(8,128)(2,1)S(1)} %collective-permute-done.6.lo_ref, bf16[128,128]{1,0:T(8,128)(2,1)S(1)} %collective-permute-done.7.hi_ref, ...), custom_call_target="tpu_custom_call" | custom-call | flops 603979776 | bytes 3211264 | tf_op jit(solution)/shard_map/pallas_call | solution.py:372
  85.0 0.5 all-to-all-done.2
  85.5 1.6 %shard_map.117 = (f32[27,64,64]{2,1,0:T(8,128)}, f32[27,64,64]{2,1,0:T(8,128)}) custom-call(bf16[1792,128]{1,0:T(8,128)(2,1)S(1)} %bitcast.3), custom_call_target="tpu_custom_call" | custom-call | bytes 1343488 | tf_op jit(solution)/shard_map/pallas_call | solution.py:372
  (3 shorter events, 0.0 us)
Async XLA Ops:
  0.6 11.2 %copy-start.1 = (pred[26]{0:T(512)(128)(4,1)S(1)}, pred[26]{0:T(512)(128)(4,1)}, u32[]{:S(2)}) copy-start(pred[26]{0:T(512)(128)(4,1)} %constant.36) | copy-start | bytes 82
  0.6 11.2 %copy-start.2 = (pred[26]{0:T(512)(128)(4,1)S(1)}, pred[26]{0:T(512)(128)(4,1)}, u32[]{:S(2)}) copy-start(pred[26]{0:T(512)(128)(4,1)} %constant.37) | copy-start | bytes 82
  0.7 11.2 %copy-start = (s32[4,26]{1,0:T(4,128)S(1)}, s32[4,26]{1,0:T(4,128)}, u32[]{:S(2)}) copy-start(s32[4,26]{1,0:T(4,128)} %param.12) | copy-start | bytes 1252
  3.1 10.8 %collective-permute-start = (bf16[128,128]{1,0:T(8,128)(2,1)S(1)}, bf16[128,128]{1,0:T(8,128)(2,1)S(1)}, u32[]{:S(2)}, u32[]{:S(2)}) collective-permute-start(bf16[128,128]{1,0:T(8,128)(2,1)S(1)} %get-tuple-element.39), channel_id=1, source_target_pairs={{0,8},{8,16},{16,24},{24,32},{32,40},{40,48},{48,56},{56,64},{64,7... | collective-permute-start | bytes 98312 | tf_op jit(solution)/shard_map/ppermute | solution.py:401
  5.2 8.7 %collective-permute-start.1 = (bf16[128,128]{1,0:T(8,128)(2,1)S(1)}, bf16[128,128]{1,0:T(8,128)(2,1)S(1)}, u32[]{:S(2)}, u32[]{:S(2)}) collective-permute-start(bf16[128,128]{1,0:T(8,128)(2,1)S(1)} %get-tuple-element.40), channel_id=1, source_target_pairs={{8,0},{16,8},{24,16},{32,24},{40,32},{48,40},{56,48},{64,56},{72,6... | collective-permute-start | bytes 98312 | tf_op jit(solution)/shard_map/ppermute | solution.py:401
  15.1 7.7 %collective-permute-start.2 = (bf16[128,128]{1,0:T(8,128)(2,1)S(1)}, bf16[128,128]{1,0:T(8,128)(2,1)S(1)}, u32[]{:S(2)}, u32[]{:S(2)}) collective-permute-start(bf16[128,128]{1,0:T(8,128)(2,1)S(1)} %get-tuple-element.48), channel_id=1, source_target_pairs={{0,8},{8,16},{16,24},{24,32},{32,40},{40,48},{48,56},{56,64},{64,7... | collective-permute-start | bytes 98312 | tf_op jit(solution)/shard_map/ppermute | solution.py:401
  15.2 7.6 %collective-permute-start.3 = (bf16[128,128]{1,0:T(8,128)(2,1)S(1)}, bf16[128,128]{1,0:T(8,128)(2,1)S(1)}, u32[]{:S(2)}, u32[]{:S(2)}) collective-permute-start(bf16[128,128]{1,0:T(8,128)(2,1)S(1)} %get-tuple-element.49), channel_id=1, source_target_pairs={{8,0},{16,8},{24,16},{32,24},{40,32},{48,40},{56,48},{64,56},{72,6... | collective-permute-start | bytes 98312 | tf_op jit(solution)/shard_map/ppermute | solution.py:401
  24.1 7.5 %collective-permute-start.4 = (bf16[128,128]{1,0:T(8,128)(2,1)S(1)}, bf16[128,128]{1,0:T(8,128)(2,1)S(1)}, u32[]{:S(2)}, u32[]{:S(2)}) collective-permute-start(bf16[128,128]{1,0:T(8,128)(2,1)S(1)} %get-tuple-element.56), channel_id=1, source_target_pairs={{0,8},{8,16},{16,24},{24,32},{32,40},{40,48},{48,56},{56,64},{64,7... | collective-permute-start | bytes 98312 | tf_op jit(solution)/shard_map/ppermute | solution.py:401
  24.2 7.4 %collective-permute-start.5 = (bf16[128,128]{1,0:T(8,128)(2,1)S(1)}, bf16[128,128]{1,0:T(8,128)(2,1)S(1)}, u32[]{:S(2)}, u32[]{:S(2)}) collective-permute-start(bf16[128,128]{1,0:T(8,128)(2,1)S(1)} %get-tuple-element.57), channel_id=1, source_target_pairs={{8,0},{16,8},{24,16},{32,24},{40,32},{48,40},{56,48},{64,56},{72,6... | collective-permute-start | bytes 98312 | tf_op jit(solution)/shard_map/ppermute | solution.py:401
  69.2 16.3 %all-to-all-start.2 = ((bf16[32,56,128]{2,1,0:T(8,128)(2,1)}), bf16[32,56,128]{2,1,0:T(8,128)(2,1)S(1)}, u32[]{:S(2)}, u32[]{:S(2)}) async-start(bf16[32,56,128]{2,1,0:T(8,128)(2,1)} %broadcast_in_dim.35), calls=%async_computation.2 | async-start | bytes 917504 | tf_op jit(solution)/shard_map/all_to_all | solution.py:488
  73.9 6.6 %collective-permute-start.6 = (bf16[128,128]{1,0:T(8,128)(2,1)S(1)}, bf16[128,128]{1,0:T(8,128)(2,1)S(1)}, u32[]{:S(2)}, u32[]{:S(2)}) collective-permute-start(bf16[128,128]{1,0:T(8,128)(2,1)S(1)} %get-tuple-element.63), channel_id=1, source_target_pairs={{0,8},{8,16},{16,24},{24,32},{32,40},{40,48},{48,56},{56,64},{64,7... | collective-permute-start | bytes 98312 | tf_op jit(solution)/shard_map/ppermute | solution.py:401
  75.4 6.3 %collective-permute-start.7 = (bf16[128,128]{1,0:T(8,128)(2,1)S(1)}, bf16[128,128]{1,0:T(8,128)(2,1)S(1)}, u32[]{:S(2)}, u32[]{:S(2)}) collective-permute-start(bf16[128,128]{1,0:T(8,128)(2,1)S(1)} %get-tuple-element.64), channel_id=1, source_target_pairs={{8,0},{16,8},{24,16},{32,24},{40,32},{48,40},{56,48},{64,56},{72,6... | collective-permute-start | bytes 98312 | tf_op jit(solution)/shard_map/ppermute | solution.py:401

commit v8 on v7

--- a/solution.py
+++ b/solution.py
@@ -286,7 +286,7 @@
     from_rows(r_ref, o_ref, tmp_ref)
 
 
-def weight_grad(xc_ref, xo_ref, e_ref, p_ref, ready=None):
+def weight_grad(xc_ref, xo_ref, e_ref, p_ref):
     low = lane_low((C, 128))
     errors = e_ref[...].T.astype(bf16)
     held = None
@@ -305,41 +305,24 @@
             else:
                 odd = pltpu.roll(z1, C, 1) + y0
                 p_ref[pl.ds((9 + number // 2) * C, C), :] = jnp.where(low, held, odd).astype(p_ref.dtype)
-        if ready is not None:
-            ready(c)
-
-
-def w2_kernel(xc_ref, xo_ref, e_ref, p_ref):
+
+
+def terms_kernel(xc_ref, xo_ref, e_ref, p_ref):
     weight_grad(xc_ref, xo_ref, e_ref, p_ref)
 
 
-def w1_kernel(xc_ref, xo_ref, e_ref, second_ref, o_hbm, p_ref, sems):
-    copies = [pltpu.make_async_copy(second_ref, o_hbm.at[pl.ds(PACKED, PACKED)], sems.at[4])]
-    copies[0].start()
-
-    def send(n, start, size):
-        rows = pl.ds(start, size)
-        copies.append(pltpu.make_async_copy(p_ref.at[rows], o_hbm.at[rows], sems.at[n]))
-        copies[-1].start()
-
-    weight_grad(xc_ref, xo_ref, e_ref, p_ref, lambda c: send(c, c * 3 * C, 3 * C))
-    send(3, 9 * C, 5 * C)
-    for copy in copies:
-        copy.wait()
-
-
-def finish_kernel(scale, r_ref, first_hbm, second_hbm, first_ref, second_ref, sems):
+def finish_kernel(scale, r1_ref, r2_ref, first_hbm, second_hbm, first_ref, second_ref, sems):
     copies = []
-    for which, (ref, hbm) in enumerate(((first_ref, first_hbm), (second_ref, second_hbm))):
+    for which, (r_ref, ref, hbm) in enumerate(((r1_ref, first_ref, first_hbm), (r2_ref, second_ref, second_hbm))):
         for c in range(3):
             for b in range(3):
                 number = 3 * c + b
                 k = 3 * b + c
-                t = (r_ref[pl.ds(which * PACKED + number * C, C), :].astype(f32) * scale).T
+                t = (r_ref[pl.ds(number * C, C), :].astype(f32) * scale).T
                 ref[9 + k] = t[:C]
                 ref[18 + k] = t[C:]
                 if number % 2 == 0:
-                    t = (r_ref[pl.ds(which * PACKED + (9 + number // 2) * C, C), :].astype(f32) * scale).T
+                    t = (r_ref[pl.ds((9 + number // 2) * C, C), :].astype(f32) * scale).T
                     held = t[C:]
                     ref[k] = t[:C]
                 else:
@@ -451,20 +434,12 @@
     )
     planes = exchange(up, down)
     (b2,) = call(back_kernel, [], [second_taps], [WEIGHTS])
-    (second_local,) = call(w2_kernel, [], [xc2, xo2, second_err], [packed], (), work)
+    (second_local,) = call(terms_kernel, [], [xc2, xo2, second_err], [packed], (), work)
     _, _, hidden_grad, first_err, up, down = layer(
         lambda v, a, u, slope: second_back(v, u, slope), 1, second_err, b2, [upstream, slope1], planes, False
     )
     lo, hi = exchange(up, down)
-    (partial,) = call(
-        w1_kernel,
-        [],
-        [xc1, xo1, first_err, second_local],
-        [jax.ShapeDtypeStruct((2 * PACKED, 128), bf16)],
-        [pltpu.VMEM((PACKED, 128), bf16), pltpu.SemaphoreType.DMA((5,))],
-        work,
-        result=HBM,
-    )
+    (first_local,) = call(terms_kernel, [], [xc1, xo1, first_err], [packed], (), work)
     (b1,) = call(back_kernel, [], [first_taps], [WEIGHTS])
     (input_grad,) = call(
         last_kernel,
@@ -479,10 +454,20 @@
     scenes = lax.axis_size("scene")
     devices = bricks * scenes
     row = 4 if bricks % 4 == 0 else 1
-    near, far = row * scenes, bricks // row
-    near_groups = [list(range(z * near, (z + 1) * near)) for z in range(far)]
+    near, far = row * (scenes // 2), bricks // row
+    near_groups = [
+        [(row * z + x) * scenes + 2 * y + core for x in range(row) for y in range(scenes // 2)]
+        for z in range(far)
+        for core in range(2)
+    ]
     far_groups = [[x + row * z for z in range(far)] for x in range(row)]
-    share = 2 * PACKED // near
+    share = PACKED // near
+    pairs = [[i, i + 1] for i in range(0, scenes, 2)]
+    swap = [(i, i ^ 1) for i in range(scenes)]
+    even = lax.axis_index("scene") % 2 == 0
+
+    def core_exchange(blocks):
+        return lax.all_to_all(blocks, "scene", 0, 0, axis_index_groups=pairs, tiled=True)
 
     def near_exchange(blocks):
         return lax.all_to_all(blocks, axes, 0, 0, axis_index_groups=near_groups, tiled=True)
@@ -496,15 +481,19 @@
     def spread(block, count):
         return jnp.broadcast_to(block[None], (count,) + block.shape)
 
+    partial = total_of(core_exchange(jnp.stack([first_local, second_local])))
     scattered = near_exchange(partial.reshape(near, share, 128))
     mine = total_of(scattered)
     mine = total_of(far_exchange(spread(mine, far)))
-    total = near_exchange(spread(mine, near))
+    gathered = near_exchange(spread(mine, near))
+    half = gathered.reshape(PACKED, 128)
+    other = lax.ppermute(half, "scene", swap)
+    first_total, second_total = jnp.where(even, half, other), jnp.where(even, other, half)
     scale = float((devices * CAP * E * E * E) ** -0.5)
     first_grad, second_grad = call(
         functools.partial(finish_kernel, scale),
         [],
-        [total.reshape(2 * PACKED, 128)],
+        [first_total, second_total],
         [GRADS, GRADS],
         [raw, raw, pltpu.SemaphoreType.DMA((2,))],
         result=HBM,

time: 87.6 us -> 96.4 us (1.10)
  blocking collectives: 33.2 us -> 42.9 us
  waiting for transfers between devices: 1.75 us -> 0.02 us
  other arithmetic: 0.11 us -> 1.36 us
    all_to_all x0 -> x1, blocking collectives: none -> 5.8 us  [core_exchange(): lax.all_to_all(blocks, 'scene', 0, 0, axis_index_groups=pairs, tiled=True)]
    all_to_all x1 -> x2, blocking collectives: 17.4 us -> 22.2 us  [near_exchange(): lax.all_to_all(blocks, axes, 0, 0, axis_index_groups=near_groups, tiled=T...]
    all_to_all x1 -> x0, starting transfers between devices: 4.71 us -> none  [near_exchange(): lax.all_to_all(blocks, axes, 0, 0, axis_index_groups=near_groups, tiled=T...]
    ppermute x0 -> x1, starting transfers between devices: none -> 4.37 us  [step(): other = lax.ppermute(half, 'scene', swap)]
    ppermute x4, starting transfers between devices: 3.76 us -> 2.34 us  [exchange(): lax.ppermute(up, 'brick', up_pairs)]
    ppermute x4, starting transfers between devices: 19.6 us -> 20.9 us  [exchange(): lax.ppermute(down, 'brick', down_pairs)]
    ppermute x4, waiting for transfers between devices: 1.21 us -> 0.01 us  [exchange(): lax.ppermute(down, 'brick', down_pairs)]
    select_n x0 -> x1, other arithmetic: none -> 1.08 us  [step(): jnp.where(even, other, half)]
  transfers between devices with their start and end apart: 9 -> 9, of which waited for: 2 -> 0; matrix products, arithmetic and copies ran while one was open for 0% -> 0% of each run, Pallas kernels for 14% -> 13%
where the time goes in v8:
time: 96.4 us; the launch traced here: 96 us
  blocking collectives  42.9 us (45%)
  starting transfers between devices  27.6 us (29%)
  Pallas kernels  21.2 us (22%)
  between operations  1.71 us (2%)
  other arithmetic  1.36 us (1%)
  local copies, waits for them, and re-layouts  1.11 us (1%)
    all_to_all x2, blocking collectives, near_exchange(): lax.all_to_all(blocks, axes, 0, 0, axis_index_groups=near_groups, tiled=T...  22.2 us
    pallas_call x16, Pallas kernels, call(): pl.pallas_call(kernel, out_shape=outs, in_specs=[SMEM] * len(scalars) + [...  21.2 us
    ppermute x4, starting transfers between devices, exchange(): lax.ppermute(down, 'brick', down_pairs)  20.9 us
    all_to_all x1, blocking collectives, far_exchange(): lax.all_to_all(blocks, 'brick', 0, 0, axis_index_groups=far_groups, tiled...  15 us
    all_to_all x1, blocking collectives, core_exchange(): lax.all_to_all(blocks, 'scene', 0, 0, axis_index_groups=pairs, tiled=True)  5.8 us
    ppermute x1, starting transfers between devices, step(): other = lax.ppermute(half, 'scene', swap)  4.37 us
    ppermute x4, starting transfers between devices, exchange(): lax.ppermute(up, 'brick', up_pairs)  2.34 us
  transfers between devices with their start and end apart: 9, of which 0 were waited for; matrix products, arithmetic and copies ran while one was open for 0% of the time, Pallas kernels for 13%

profile of v8, /device:TPU:1, one launch (start us, length us, event | category | flops | bytes accessed | tf_op | source)
XLA Modules:
  0.0 96.0 jit_solution(379767992279060311)
XLA Ops:
  0.6 0.0 copy-start.3
  0.6 0.0 copy-start.4
  0.7 0.0 copy-start.2
  1.3 1.8 %shard_map.102 = (f32[1024,128]{1,0:T(8,128)S(1)}, bf16[128,128]{1,0:T(8,128)(2,1)S(1)}, bf16[128,128]{1,0:T(8,128)(2,1)S(1)}, f32[27,64,64]{2,1,0:T(8,128)S(1)}...) custom-call(s32[1]{0:T(128)S(6)} %copy.11.counts_ref, f32[1,4,64,512]{3,2,1,0:T(8,128)} %x_hbm.1, ...), custom_call_target="tpu_custom_call" | custom-call | bytes 3932160 | tf_op jit(solution)/shard_map/pallas_call | solution.py:355
  3.1 2.1 %collective-permute-start = (bf16[128,128]{1,0:T(8,128)(2,1)S(1)}, bf16[128,128]{1,0:T(8,128)(2,1)S(1)}, u32[]{:S(2)}, u32[]{:S(2)}) collective-permute-start(bf16[128,128]{1,0:T(8,128)(2,1)S(1)} %get-tuple-element.39), channel_id=1, source_target_pairs={{0,8},{8,16},{16,24},{24,32},{32,40},{40,48},{48,56},{56,64},{64,7... | collective-permute-start | bytes 98312 | tf_op jit(solution)/shard_map/ppermute | solution.py:384
  5.2 6.6 %collective-permute-start.1 = (bf16[128,128]{1,0:T(8,128)(2,1)S(1)}, bf16[128,128]{1,0:T(8,128)(2,1)S(1)}, u32[]{:S(2)}, u32[]{:S(2)}) collective-permute-start(bf16[128,128]{1,0:T(8,128)(2,1)S(1)} %get-tuple-element.40), channel_id=1, source_target_pairs={{8,0},{16,8},{24,16},{32,24},{40,32},{48,40},{56,48},{64,56},{72,6... | collective-permute-start | bytes 98312 | tf_op jit(solution)/shard_map/ppermute | solution.py:384
  11.9 0.0 copy-done.3
  11.9 0.0 copy-done.4
  11.9 0.0 copy-done.2
  11.9 0.3 shard_map.103.w_ref
  12.2 1.7 %shard_map.104 = (bf16[4,2,8,16,768]{4,3,2,1,0:T(8,128)(2,1)S(1)}, f32[768,128]{1,0:T(8,128)S(1)}, f32[768,128]{1,0:T(8,128)S(1)}) custom-call(s32[4,26]{1,0:T(4,128)S(1)} %select_select_fusion.idx_ref, f32[1024,128]{1,0:T(8,128)S(1)} %get-tuple-element.37.a_ref, bf16[4,768,256]{2,1,0:T(8,128)(2,1)S(1)} %shard_map.103.w_ref), custom_call_target="tpu_custom_call" | custom-call | flops 301989888 | bytes 4456448 | tf_op jit(solution)/shard_map/pallas_call | solution.py:355
  13.9 0.0 collective-permute-done.lo_ref
  13.9 0.0 collective-permute-done.1.hi_ref
  13.9 1.2 %shard_map.105 = (f32[1024,128]{1,0:T(8,128)S(1)}, f32[1024,128]{1,0:T(8,128)S(1)}, bf16[128,128]{1,0:T(8,128)(2,1)S(1)}, bf16[128,128]{1,0:T(8,128)(2,1)S(1)}, bf16[4,2,2,16,768]{4,3,2,1,0:T(8,128)(2,1)S(1)}) custom-call(s32[4,26]{1,0:T(4,128)S(1)} %select_select_fusion.idx_ref, f32[1024,128]{1,0:T(8,128)S(1)} %get-tuple-element.37.a_ref, ...), custom_call_target="tpu_custom_call" | custom-call | flops 301989888 | bytes 6029312 | tf_op jit(solution)/shard_map/pallas_call | solution.py:355
  15.1 0.1 collective-permute-start.2
  15.2 4.8 %collective-permute-start.3 = (bf16[128,128]{1,0:T(8,128)(2,1)S(1)}, bf16[128,128]{1,0:T(8,128)(2,1)S(1)}, u32[]{:S(2)}, u32[]{:S(2)}) collective-permute-start(bf16[128,128]{1,0:T(8,128)(2,1)S(1)} %get-tuple-element.49), channel_id=1, source_target_pairs={{8,0},{16,8},{24,16},{32,24},{40,32},{48,40},{56,48},{64,56},{72,6... | collective-permute-start | bytes 98312 | tf_op jit(solution)/shard_map/ppermute | solution.py:384
  20.0 0.4 shard_map.110.w_ref
  20.4 0.7 shard_map.106
  21.1 1.7 %shard_map.107 = (bf16[4,2,8,16,768]{4,3,2,1,0:T(8,128)(2,1)S(1)}, f32[768,128]{1,0:T(8,128)S(1)}, f32[768,128]{1,0:T(8,128)S(1)}) custom-call(s32[4,26]{1,0:T(4,128)S(1)} %select_select_fusion.idx_ref, f32[1024,128]{1,0:T(8,128)S(1)} %get-tuple-element.44.a_ref, bf16[4,768,256]{2,1,0:T(8,128)(2,1)S(1)} %get-tuple-element.47.w_ref, ...), custom_call_target="tpu_custom_call" | custom-call | flops 301989888 | bytes 4980736 | tf_op jit(solution)/shard_map/pallas_call | solution.py:355
  22.9 0.0 collective-permute-done.2.lo_ref
  22.9 0.0 collective-permute-done.3.hi_ref
  22.9 1.2 %shard_map.108 = (f32[1024,128]{1,0:T(8,128)S(1)}, f32[1024,128]{1,0:T(8,128)S(1)}, bf16[128,128]{1,0:T(8,128)(2,1)S(1)}, bf16[128,128]{1,0:T(8,128)(2,1)S(1)}, bf16[4,2,2,16,768]{4,3,2,1,0:T(8,128)(2,1)S(1)}) custom-call(s32[4,26]{1,0:T(4,128)S(1)} %select_select_fusion.idx_ref, f32[1024,128]{1,0:T(8,128)S(1)} %get-tuple-element.44.a_ref, ...), custom_call_target="tpu_custom_call" | custom-call | flops 301989888 | bytes 6553600 | tf_op jit(solution)/shard_map/pallas_call | solution.py:355
  24.1 0.1 collective-permute-start.4
  24.2 4.8 %collective-permute-start.5 = (bf16[128,128]{1,0:T(8,128)(2,1)S(1)}, bf16[128,128]{1,0:T(8,128)(2,1)S(1)}, u32[]{:S(2)}, u32[]{:S(2)}) collective-permute-start(bf16[128,128]{1,0:T(8,128)(2,1)S(1)} %get-tuple-element.57), channel_id=1, source_target_pairs={{8,0},{16,8},{24,16},{32,24},{40,32},{48,40},{56,48},{64,56},{72,6... | collective-permute-start | bytes 98312 | tf_op jit(solution)/shard_map/ppermute | solution.py:384
  29.0 0.9 shard_map.116
  29.9 1.6 %shard_map.111 = (bf16[4,2,8,16,768]{4,3,2,1,0:T(8,128)(2,1)S(1)}, f32[768,128]{1,0:T(8,128)S(1)}, f32[768,128]{1,0:T(8,128)S(1)}) custom-call(s32[4,26]{1,0:T(4,128)S(1)} %select_select_fusion.idx_ref, f32[1024,128]{1,0:T(8,128)S(1)} %get-tuple-element.55.a_ref.e_ref, bf16[4,768,256]{2,1,0:T(8,128)(2,1)S(1)} %shard_map.110.w_ref, ...), custom_call_target="tpu_custom_call" | custom-call | flops 301989888 | bytes 5505024 | tf_op jit(solution)/shard_map/pallas_call | solution.py:355
  31.6 0.0 collective-permute-done.4.lo_ref
  31.6 0.0 collective-permute-done.5.hi_ref
  31.6 1.8 %shard_map.112 = (f32[1024,128]{1,0:T(8,128)S(1)}, f32[1024,128]{1,0:T(8,128)S(1)}, bf16[128,128]{1,0:T(8,128)(2,1)}, bf16[128,128]{1,0:T(8,128)(2,1)}) custom-call(s32[4,26]{1,0:T(4,128)S(1)} %select_select_fusion.idx_ref, f32[1024,128]{1,0:T(8,128)S(1)} %get-tuple-element.55.a_ref.e_ref, bf16[4,768,256]{2,1,0:T(8,128)(2,1)S(1)} %shard_map.110.w_ref, ...), custom_call_target="tpu_custom_call" | custom-call | flops 301989888 | bytes 6684672 | tf_op jit(solution)/shard_map/pallas_call | solution.py:355
  33.4 0.9 shard_map.115
  34.4 0.0 copy-done
  34.4 5.8 %all_to_all.20 = bf16[2,896,128]{2,1,0:T(8,128)(2,1)S(1)} all-to-all(bf16[2,896,128]{2,1,0:T(8,128)(2,1)S(1)} %pad_maximum_fusion), channel_id=1, replica_groups={{0,1},{2,3},{4,5},{6,7},{8,9},{10,11},{12,13},{14,15},{16,17},{18,19},{..., dimensions={0} | all-to-all | bytes 917504 | tf_op jit(solution)/shard_map/all_to_all | solution.py:470
  40.2 0.2 reduce_sum.36
  40.4 11.5 %all_to_all.21 = bf16[16,56,128]{2,1,0:T(8,128)(2,1)S(1)} all-to-all(bf16[16,56,128]{2,1,0:T(8,128)(2,1)S(1)} %bitcast.8), channel_id=1, replica_groups={{0,2,4,6,8,10,12,14,16,18,20,22,24,26,28,30},{1,3,5,7,9,11,13,15,17,19,..., dimensions={0} | all-to-all | bytes 458752 | tf_op jit(solution)/shard_map/all_to_all | solution.py:473
  51.9 15.0 %all_to_all.22 = bf16[8,56,128]{2,1,0:T(8,128)(2,1)S(1)} all-to-all(bf16[8,56,128]{2,1,0:T(8,128)(2,1)S(1)} %broadcast_in_dim.34), channel_id=1, replica_groups={{0,32,64,96,128,160,192,224},{8,40,72,104,136,168,200,232},{16,48,80,11..., dimensions={0} | all-to-all | bytes 229376 | tf_op jit(solution)/shard_map/all_to_all | solution.py:476
  67.0 10.7 %all_to_all.23 = bf16[16,56,128]{2,1,0:T(8,128)(2,1)} all-to-all(bf16[16,56,128]{2,1,0:T(8,128)(2,1)S(1)} %broadcast_in_dim.35), channel_id=1, replica_groups={{0,2,4,6,8,10,12,14,16,18,20,22,24,26,28,30},{1,3,5,7,9,11,13,15,17,19,..., dimensions={0} | all-to-all | bytes 458752 | tf_op jit(solution)/shard_map/all_to_all | solution.py:473
  77.6 4.4 %collective-permute-start.8 = (bf16[896,128]{1,0:T(8,128)(2,1)}, bf16[896,128]{1,0:T(8,128)(2,1)}, u32[]{:S(2)}, u32[]{:S(2)}) collective-permute-start(bf16[896,128]{1,0:T(8,128)(2,1)} %bitcast.3), channel_id=1, source_target_pairs={{0,1},{1,0},{2,3},{3,2},{4,5},{5,4},{6,7},{7,6},{8,9},{9,8},{10,11... | collective-permute-start | bytes 688136 | tf_op jit(solution)/shard_map/ppermute | solution.py:490
  82.0 0.1 collective-permute-start.6
  82.1 4.7 %collective-permute-start.7 = (bf16[128,128]{1,0:T(8,128)(2,1)}, bf16[128,128]{1,0:T(8,128)(2,1)}, u32[]{:S(2)}, u32[]{:S(2)}) collective-permute-start(bf16[128,128]{1,0:T(8,128)(2,1)} %get-tuple-element.64), channel_id=1, source_target_pairs={{8,0},{16,8},{24,16},{32,24},{40,32},{48,40},{56,48},{64,56},{72,6... | collective-permute-start | bytes 98312 | tf_op jit(solution)/shard_map/ppermute | solution.py:384
  86.8 0.4 shard_map.113.w_ref
  87.2 1.3 %shard_map.109 = f32[1,4,64,512]{3,2,1,0:T(8,128)} custom-call(f32[1024,128]{1,0:T(8,128)S(1)} %get-tuple-element.54.r_ref), custom_call_target="tpu_custom_call" | custom-call | bytes 1048576 | tf_op jit(solution)/shard_map/pallas_call | solution.py:355
  88.5 0.0 collective-permute-done.6.lo_ref
  88.5 0.0 collective-permute-done.7.hi_ref
  88.6 1.0 %copy-done.1 = f32[1024,128]{1,0:T(8,128)S(1)} copy-done((f32[1024,128]{1,0:T(8,128)S(1)}, f32[1024,128]{1,0:T(8,128)}, u32[]{:S(2)}) %copy-start.1) | copy-done | bytes 524312
  89.6 3.5 %shard_map.114 = f32[1,4,64,512]{3,2,1,0:T(8,128)} custom-call(s32[4,26]{1,0:T(4,128)S(1)} %select_select_fusion.idx_ref, f32[1024,128]{1,0:T(8,128)S(1)} %get-tuple-element.62.a_ref.e_ref, bf16[128,128]{1,0:T(8,128)(2,1)S(1)} %collective-permute-done.6.lo_ref, bf16[128,128]{1,0:T(8,128)(2,1)} %collective-permute-done.7.hi_ref, ...), custom_call_target="tpu_custom_call" | custom-call | flops 603979776 | bytes 3211264 | tf_op jit(solution)/shard_map/pallas_call | solution.py:355
  93.1 0.0 collective-permute-done.8
  93.1 1.1 %broadcast_select_fusion = (bf16[896,128]{1,0:T(8,128)(2,1)S(1)}, bf16[896,128]{1,0:T(8,128)(2,1)S(1)}) fusion(bf16[896,128]{1,0:T(8,128)(2,1)} %collective-permute-done.8, pred[]{:T(512)S(6)} %eq.10, bf16[16,56,128]{2,1,0:T(8,128)(2,1)} %all_to_all.23), kind=kLoop, calls=%fused_computation.1 | loop fusion | flops 229376 | bytes 917505 | tf_op jit(solution)/shard_map/jit(_where)/select_n | solution.py:491
  94.2 1.6 %shard_map.117 = (f32[27,64,64]{2,1,0:T(8,128)}, f32[27,64,64]{2,1,0:T(8,128)}) custom-call(bf16[896,128]{1,0:T(8,128)(2,1)S(1)} %get-tuple-element.71.r1_ref, bf16[896,128]{1,0:T(8,128)(2,1)S(1)} %get-tuple-element.70.r2_ref), custom_call_target="tpu_custom_call" | custom-call | bytes 1343488 | tf_op jit(solution)/shard_map/pallas_call | solution.py:355
  (8 shorter events, 0.2 us)
Async XLA Ops:
  0.6 11.2 %copy-start.3 = (pred[26]{0:T(512)(128)(4,1)S(1)}, pred[26]{0:T(512)(128)(4,1)}, u32[]{:S(2)}) copy-start(pred[26]{0:T(512)(128)(4,1)} %constant.52) | copy-start | bytes 82
  0.6 11.2 %copy-start.4 = (pred[26]{0:T(512)(128)(4,1)S(1)}, pred[26]{0:T(512)(128)(4,1)}, u32[]{:S(2)}) copy-start(pred[26]{0:T(512)(128)(4,1)} %constant.53) | copy-start | bytes 82
  0.7 11.2 %copy-start.2 = (s32[4,26]{1,0:T(4,128)S(1)}, s32[4,26]{1,0:T(4,128)}, u32[]{:S(2)}) copy-start(s32[4,26]{1,0:T(4,128)} %param.12) | copy-start | bytes 1252
  3.1 10.8 %collective-permute-start = (bf16[128,128]{1,0:T(8,128)(2,1)S(1)}, bf16[128,128]{1,0:T(8,128)(2,1)S(1)}, u32[]{:S(2)}, u32[]{:S(2)}) collective-permute-start(bf16[128,128]{1,0:T(8,128)(2,1)S(1)} %get-tuple-element.39), channel_id=1, source_target_pairs={{0,8},{8,16},{16,24},{24,32},{32,40},{40,48},{48,56},{56,64},{64,7... | collective-permute-start | bytes 98312 | tf_op jit(solution)/shard_map/ppermute | solution.py:384
  5.2 8.7 %collective-permute-start.1 = (bf16[128,128]{1,0:T(8,128)(2,1)S(1)}, bf16[128,128]{1,0:T(8,128)(2,1)S(1)}, u32[]{:S(2)}, u32[]{:S(2)}) collective-permute-start(bf16[128,128]{1,0:T(8,128)(2,1)S(1)} %get-tuple-element.40), channel_id=1, source_target_pairs={{8,0},{16,8},{24,16},{32,24},{40,32},{48,40},{56,48},{64,56},{72,6... | collective-permute-start | bytes 98312 | tf_op jit(solution)/shard_map/ppermute | solution.py:384
  15.1 7.7 %collective-permute-start.2 = (bf16[128,128]{1,0:T(8,128)(2,1)S(1)}, bf16[128,128]{1,0:T(8,128)(2,1)S(1)}, u32[]{:S(2)}, u32[]{:S(2)}) collective-permute-start(bf16[128,128]{1,0:T(8,128)(2,1)S(1)} %get-tuple-element.48), channel_id=1, source_target_pairs={{0,8},{8,16},{16,24},{24,32},{32,40},{40,48},{48,56},{56,64},{64,7... | collective-permute-start | bytes 98312 | tf_op jit(solution)/shard_map/ppermute | solution.py:384
  15.2 7.6 %collective-permute-start.3 = (bf16[128,128]{1,0:T(8,128)(2,1)S(1)}, bf16[128,128]{1,0:T(8,128)(2,1)S(1)}, u32[]{:S(2)}, u32[]{:S(2)}) collective-permute-start(bf16[128,128]{1,0:T(8,128)(2,1)S(1)} %get-tuple-element.49), channel_id=1, source_target_pairs={{8,0},{16,8},{24,16},{32,24},{40,32},{48,40},{56,48},{64,56},{72,6... | collective-permute-start | bytes 98312 | tf_op jit(solution)/shard_map/ppermute | solution.py:384
  24.1 7.5 %collective-permute-start.4 = (bf16[128,128]{1,0:T(8,128)(2,1)S(1)}, bf16[128,128]{1,0:T(8,128)(2,1)S(1)}, u32[]{:S(2)}, u32[]{:S(2)}) collective-permute-start(bf16[128,128]{1,0:T(8,128)(2,1)S(1)} %get-tuple-element.56), channel_id=1, source_target_pairs={{0,8},{8,16},{16,24},{24,32},{32,40},{40,48},{48,56},{56,64},{64,7... | collective-permute-start | bytes 98312 | tf_op jit(solution)/shard_map/ppermute | solution.py:384
  24.2 7.4 %collective-permute-start.5 = (bf16[128,128]{1,0:T(8,128)(2,1)S(1)}, bf16[128,128]{1,0:T(8,128)(2,1)S(1)}, u32[]{:S(2)}, u32[]{:S(2)}) collective-permute-start(bf16[128,128]{1,0:T(8,128)(2,1)S(1)} %get-tuple-element.57), channel_id=1, source_target_pairs={{8,0},{16,8},{24,16},{32,24},{40,32},{48,40},{56,48},{64,56},{72,6... | collective-permute-start | bytes 98312 | tf_op jit(solution)/shard_map/ppermute | solution.py:384
  33.4 1.0 %copy-start = (f32[1024,128]{1,0:T(8,128)}, f32[1024,128]{1,0:T(8,128)S(1)}, u32[]{:S(2)}) copy-start(f32[1024,128]{1,0:T(8,128)S(1)} %get-tuple-element.65.hg_ref) | copy-start | bytes 1572868
  77.6 15.5 %collective-permute-start.8 = (bf16[896,128]{1,0:T(8,128)(2,1)}, bf16[896,128]{1,0:T(8,128)(2,1)}, u32[]{:S(2)}, u32[]{:S(2)}) collective-permute-start(bf16[896,128]{1,0:T(8,128)(2,1)} %bitcast.3), channel_id=1, source_target_pairs={{0,1},{1,0},{2,3},{3,2},{4,5},{5,4},{6,7},{7,6},{8,9},{9,8},{10,11... | collective-permute-start | bytes 688136 | tf_op jit(solution)/shard_map/ppermute | solution.py:490
  82.0 6.5 %collective-permute-start.6 = (bf16[128,128]{1,0:T(8,128)(2,1)}, bf16[128,128]{1,0:T(8,128)(2,1)S(1)}, u32[]{:S(2)}, u32[]{:S(2)}) collective-permute-start(bf16[128,128]{1,0:T(8,128)(2,1)} %get-tuple-element.63), channel_id=1, source_target_pairs={{0,8},{8,16},{16,24},{24,32},{32,40},{40,48},{48,56},{56,64},{64,7... | collective-permute-start | bytes 98312 | tf_op jit(solution)/shard_map/ppermute | solution.py:384
  82.1 6.5 %collective-permute-start.7 = (bf16[128,128]{1,0:T(8,128)(2,1)}, bf16[128,128]{1,0:T(8,128)(2,1)}, u32[]{:S(2)}, u32[]{:S(2)}) collective-permute-start(bf16[128,128]{1,0:T(8,128)(2,1)} %get-tuple-element.64), channel_id=1, source_target_pairs={{8,0},{16,8},{24,16},{32,24},{40,32},{48,40},{56,48},{64,56},{72,6... | collective-permute-start | bytes 98312 | tf_op jit(solution)/shard_map/ppermute | solution.py:384
  88.5 1.0 %copy-start.1 = (f32[1024,128]{1,0:T(8,128)S(1)}, f32[1024,128]{1,0:T(8,128)}, u32[]{:S(2)}) copy-start(f32[1024,128]{1,0:T(8,128)} %copy-done) | copy-start | bytes 1572868

commit v9 on v7

--- a/solution.py
+++ b/solution.py
@@ -330,23 +330,25 @@
 
 def finish_kernel(scale, r_ref, first_hbm, second_hbm, first_ref, second_ref, sems):
     copies = []
+
+    def send(ref, hbm, start, size):
+        part = pl.ds(start, size)
+        copies.append(pltpu.make_async_copy(ref.at[part], hbm.at[part], sems.at[len(copies)]))
+        copies[-1].start()
+
     for which, (ref, hbm) in enumerate(((first_ref, first_hbm), (second_ref, second_hbm))):
-        for c in range(3):
-            for b in range(3):
-                number = 3 * c + b
-                k = 3 * b + c
-                t = (r_ref[pl.ds(which * PACKED + number * C, C), :].astype(f32) * scale).T
-                ref[9 + k] = t[:C]
-                ref[18 + k] = t[C:]
-                if number % 2 == 0:
-                    t = (r_ref[pl.ds(which * PACKED + (9 + number // 2) * C, C), :].astype(f32) * scale).T
-                    held = t[C:]
-                    ref[k] = t[:C]
-                else:
-                    ref[k] = held
-        copy = pltpu.make_async_copy(ref, hbm, sems.at[which])
-        copy.start()
-        copies.append(copy)
+        for number in range(9):
+            k = 3 * (number % 3) + number // 3
+            t = (r_ref[pl.ds(which * PACKED + number * C, C), :].astype(f32) * scale).T
+            ref[9 + k] = t[:C]
+            ref[18 + k] = t[C:]
+        send(ref, hbm, 9, 18)
+        for number in range(0, 9, 2):
+            t = (r_ref[pl.ds(which * PACKED + (9 + number // 2) * C, C), :].astype(f32) * scale).T
+            ref[3 * (number % 3) + number // 3] = t[:C]
+            if number < 8:
+                ref[3 * ((number + 1) % 3) + (number + 1) // 3] = t[C:]
+        send(ref, hbm, 0, 9)
     for copy in copies:
         copy.wait()
 
@@ -506,7 +508,7 @@
         [],
         [total.reshape(2 * PACKED, 128)],
         [GRADS, GRADS],
-        [raw, raw, pltpu.SemaphoreType.DMA((2,))],
+        [raw, raw, pltpu.SemaphoreType.DMA((4,))],
         result=HBM,
     )
     return (outputs, input_grad, first_grad, second_grad)

time: 87.6 us -> 87.4 us (level)
  no operation moved by 1% of the time
where the time goes in v9:
time: 87.4 us; the launch traced here: 87.1 us
  blocking collectives  33.2 us (38%)
  starting transfers between devices  28 us (32%)
  Pallas kernels  21.5 us (25%)
  waiting for transfers between devices  1.75 us (2%)
  between operations  1.67 us (2%)
    pallas_call x16, Pallas kernels, call(): pl.pallas_call(kernel, out_shape=outs, in_specs=[SMEM] * len(scalars) + [...  21.5 us
    ppermute x4, starting transfers between devices, exchange(): lax.ppermute(down, 'brick', down_pairs)  19.6 us
    all_to_all x1, blocking collectives, near_exchange(): lax.all_to_all(blocks, axes, 0, 0, axis_index_groups=near_groups, tiled=T...  17.4 us
    all_to_all x1, blocking collectives, far_exchange(): lax.all_to_all(blocks, 'brick', 0, 0, axis_index_groups=far_groups, tiled...  15.8 us
    all_to_all x1, starting transfers between devices, near_exchange(): lax.all_to_all(blocks, axes, 0, 0, axis_index_groups=near_groups, tiled=T...  4.71 us
    ppermute x4, starting transfers between devices, exchange(): lax.ppermute(up, 'brick', up_pairs)  3.76 us
  transfers between devices with their start and end apart: 9, of which 2 were waited for; matrix products, arithmetic and copies ran while one was open for 0% of the time, Pallas kernels for 14%

profile of v9, /device:TPU:1, one launch (start us, length us, event | category | flops | bytes accessed | tf_op | source)
XLA Modules:
  0.0 87.1 jit_solution(59915315440144250)
XLA Ops:
  0.6 0.0 copy-start.1
  0.6 0.0 copy-start.2
  0.7 0.0 copy-start
  1.3 1.8 %shard_map.102 = (f32[1024,128]{1,0:T(8,128)S(1)}, bf16[128,128]{1,0:T(8,128)(2,1)S(1)}, bf16[128,128]{1,0:T(8,128)(2,1)S(1)}, f32[27,64,64]{2,1,0:T(8,128)S(1)}...) custom-call(s32[1]{0:T(128)S(6)} %copy.11.counts_ref, f32[1,4,64,512]{3,2,1,0:T(8,128)} %x_hbm.1, ...), custom_call_target="tpu_custom_call" | custom-call | bytes 3932160 | tf_op jit(solution)/shard_map/pallas_call | solution.py:374
  3.1 2.1 %collective-permute-start = (bf16[128,128]{1,0:T(8,128)(2,1)S(1)}, bf16[128,128]{1,0:T(8,128)(2,1)S(1)}, u32[]{:S(2)}, u32[]{:S(2)}) collective-permute-start(bf16[128,128]{1,0:T(8,128)(2,1)S(1)} %get-tuple-element.39), channel_id=1, source_target_pairs={{0,8},{8,16},{16,24},{24,32},{32,40},{40,48},{48,56},{56,64},{64,7... | collective-permute-start | bytes 98312 | tf_op jit(solution)/shard_map/ppermute | solution.py:403
  5.2 6.6 %collective-permute-start.1 = (bf16[128,128]{1,0:T(8,128)(2,1)S(1)}, bf16[128,128]{1,0:T(8,128)(2,1)S(1)}, u32[]{:S(2)}, u32[]{:S(2)}) collective-permute-start(bf16[128,128]{1,0:T(8,128)(2,1)S(1)} %get-tuple-element.40), channel_id=1, source_target_pairs={{8,0},{16,8},{24,16},{32,24},{40,32},{48,40},{56,48},{64,56},{72,6... | collective-permute-start | bytes 98312 | tf_op jit(solution)/shard_map/ppermute | solution.py:403
  11.9 0.0 copy-done.1
  11.9 0.0 copy-done.2
  11.9 0.0 copy-done
  11.9 0.3 shard_map.103.w_ref
  12.2 1.7 %shard_map.104 = (bf16[4,2,8,16,768]{4,3,2,1,0:T(8,128)(2,1)S(1)}, f32[768,128]{1,0:T(8,128)S(1)}, f32[768,128]{1,0:T(8,128)S(1)}) custom-call(s32[4,26]{1,0:T(4,128)S(1)} %select_select_fusion.idx_ref, f32[1024,128]{1,0:T(8,128)S(1)} %get-tuple-element.37.a_ref, bf16[4,768,256]{2,1,0:T(8,128)(2,1)S(1)} %shard_map.103.w_ref), custom_call_target="tpu_custom_call" | custom-call | flops 301989888 | bytes 4456448 | tf_op jit(solution)/shard_map/pallas_call | solution.py:374
  13.9 0.0 collective-permute-done.lo_ref
  13.9 0.0 collective-permute-done.1.hi_ref
  13.9 1.2 %shard_map.105 = (f32[1024,128]{1,0:T(8,128)S(1)}, f32[1024,128]{1,0:T(8,128)S(1)}, bf16[128,128]{1,0:T(8,128)(2,1)S(1)}, bf16[128,128]{1,0:T(8,128)(2,1)S(1)}, bf16[4,2,2,16,768]{4,3,2,1,0:T(8,128)(2,1)S(1)}) custom-call(s32[4,26]{1,0:T(4,128)S(1)} %select_select_fusion.idx_ref, f32[1024,128]{1,0:T(8,128)S(1)} %get-tuple-element.37.a_ref, ...), custom_call_target="tpu_custom_call" | custom-call | flops 301989888 | bytes 6029312 | tf_op jit(solution)/shard_map/pallas_call | solution.py:374
  15.1 0.1 collective-permute-start.2
  15.2 4.8 %collective-permute-start.3 = (bf16[128,128]{1,0:T(8,128)(2,1)S(1)}, bf16[128,128]{1,0:T(8,128)(2,1)S(1)}, u32[]{:S(2)}, u32[]{:S(2)}) collective-permute-start(bf16[128,128]{1,0:T(8,128)(2,1)S(1)} %get-tuple-element.49), channel_id=1, source_target_pairs={{8,0},{16,8},{24,16},{32,24},{40,32},{48,40},{56,48},{64,56},{72,6... | collective-permute-start | bytes 98312 | tf_op jit(solution)/shard_map/ppermute | solution.py:403
  20.0 0.4 shard_map.110.w_ref
  20.4 0.7 shard_map.106
  21.1 1.7 %shard_map.107 = (bf16[4,2,8,16,768]{4,3,2,1,0:T(8,128)(2,1)S(1)}, f32[768,128]{1,0:T(8,128)S(1)}, f32[768,128]{1,0:T(8,128)S(1)}) custom-call(s32[4,26]{1,0:T(4,128)S(1)} %select_select_fusion.idx_ref, f32[1024,128]{1,0:T(8,128)S(1)} %get-tuple-element.44.a_ref, bf16[4,768,256]{2,1,0:T(8,128)(2,1)S(1)} %get-tuple-element.47.w_ref, ...), custom_call_target="tpu_custom_call" | custom-call | flops 301989888 | bytes 4980736 | tf_op jit(solution)/shard_map/pallas_call | solution.py:374
  22.9 0.0 collective-permute-done.2.lo_ref
  22.9 0.0 collective-permute-done.3.hi_ref
  22.9 1.2 %shard_map.108 = (f32[1024,128]{1,0:T(8,128)S(1)}, f32[1024,128]{1,0:T(8,128)S(1)}, bf16[128,128]{1,0:T(8,128)(2,1)S(1)}, bf16[128,128]{1,0:T(8,128)(2,1)S(1)}, bf16[4,2,2,16,768]{4,3,2,1,0:T(8,128)(2,1)S(1)}) custom-call(s32[4,26]{1,0:T(4,128)S(1)} %select_select_fusion.idx_ref, f32[1024,128]{1,0:T(8,128)S(1)} %get-tuple-element.44.a_ref, ...), custom_call_target="tpu_custom_call" | custom-call | flops 301989888 | bytes 6553600 | tf_op jit(solution)/shard_map/pallas_call | solution.py:374
  24.1 0.1 collective-permute-start.4
  24.2 4.8 %collective-permute-start.5 = (bf16[128,128]{1,0:T(8,128)(2,1)S(1)}, bf16[128,128]{1,0:T(8,128)(2,1)S(1)}, u32[]{:S(2)}, u32[]{:S(2)}) collective-permute-start(bf16[128,128]{1,0:T(8,128)(2,1)S(1)} %get-tuple-element.57), channel_id=1, source_target_pairs={{8,0},{16,8},{24,16},{32,24},{40,32},{48,40},{56,48},{64,56},{72,6... | collective-permute-start | bytes 98312 | tf_op jit(solution)/shard_map/ppermute | solution.py:403
  29.0 0.9 %shard_map.115.second_ref = bf16[896,128]{1,0:T(8,128)(2,1)S(1)} custom-call(bf16[4,2,8,16,768]{4,3,2,1,0:T(8,128)(2,1)S(1)} %get-tuple-element.51.xc_ref, bf16[4,2,2,16,768]{4,3,2,1,0:T(8,128)(2,1)S(1)} %get-tuple-element.67.xo_ref, f32[1024,128]{1,0:T(8,128)S(1)} %get-tuple-element.55.a_ref.e_ref), custom_call_target="tpu_custom_call" | custom-call | flops 603979776 | bytes 2719744 | tf_op jit(solution)/shard_map/pallas_call | solution.py:374
  29.9 1.6 %shard_map.111 = (bf16[4,2,8,16,768]{4,3,2,1,0:T(8,128)(2,1)S(1)}, f32[768,128]{1,0:T(8,128)S(1)}, f32[768,128]{1,0:T(8,128)S(1)}) custom-call(s32[4,26]{1,0:T(4,128)S(1)} %select_select_fusion.idx_ref, f32[1024,128]{1,0:T(8,128)S(1)} %get-tuple-element.55.a_ref.e_ref, bf16[4,768,256]{2,1,0:T(8,128)(2,1)S(1)} %shard_map.110.w_ref, ...), custom_call_target="tpu_custom_call" | custom-call | flops 301989888 | bytes 5505024 | tf_op jit(solution)/shard_map/pallas_call | solution.py:374
  31.6 0.0 collective-permute-done.4.lo_ref
  31.6 0.0 collective-permute-done.5.hi_ref
  31.6 1.2 %shard_map.112 = (f32[1024,128]{1,0:T(8,128)S(1)}, f32[1024,128]{1,0:T(8,128)S(1)}, bf16[128,128]{1,0:T(8,128)(2,1)S(1)}, bf16[128,128]{1,0:T(8,128)(2,1)S(1)}) custom-call(s32[4,26]{1,0:T(4,128)S(1)} %select_select_fusion.idx_ref, f32[1024,128]{1,0:T(8,128)S(1)} %get-tuple-element.55.a_ref.e_ref, bf16[4,768,256]{2,1,0:T(8,128)(2,1)S(1)} %shard_map.110.w_ref, ...), custom_call_target="tpu_custom_call" | custom-call | flops 301989888 | bytes 6684672 | tf_op jit(solution)/shard_map/pallas_call | solution.py:374
  32.8 2.2 %shard_map.116 = bf16[1792,128]{1,0:T(8,128)(2,1)S(1)} custom-call(bf16[4,2,8,16,768]{4,3,2,1,0:T(8,128)(2,1)S(1)} %get-tuple-element.41.xc_ref, bf16[4,2,2,16,768]{4,3,2,1,0:T(8,128)(2,1)S(1)} %get-tuple-element.66.xo_ref, f32[1024,128]{1,0:T(8,128)S(1)} %get-tuple-element.62.a_ref.e_ref, bf16[896,128]{1,0:T(8,128)(2,1)S(1)} %shard_map.115.second_ref), custom_call_target="tpu_custom_call" | custom-call | flops 603979776 | bytes 3178496 | tf_op jit(solution)/shard_map/pallas_call | solution.py:374
  35.0 17.4 %all_to_all.15 = bf16[32,56,128]{2,1,0:T(8,128)(2,1)S(1)} all-to-all(bf16[32,56,128]{2,1,0:T(8,128)(2,1)S(1)} %bitcast.2), channel_id=1, replica_groups={{0,1,2,3,4,5,6,7,8,9,10,11,12,13,14,15,16,17,18,19,20,21,22,23,24,25,26..., dimensions={0} | all-to-all | bytes 917504 | tf_op jit(solution)/shard_map/all_to_all | solution.py:490
  52.4 0.1 reduce_sum.24
  52.5 15.8 %all_to_all.16 = bf16[8,56,128]{2,1,0:T(8,128)(2,1)S(1)} all-to-all(bf16[8,56,128]{2,1,0:T(8,128)(2,1)S(1)} %broadcast_in_dim.34), channel_id=1, replica_groups={{0,32,64,96,128,160,192,224},{8,40,72,104,136,168,200,232},{16,48,80,11..., dimensions={0} | all-to-all | bytes 229376 | tf_op jit(solution)/shard_map/all_to_all | solution.py:493
  68.3 0.8 broadcast_in_dim.35
  69.2 4.7 %all-to-all-start.2 = ((bf16[32,56,128]{2,1,0:T(8,128)(2,1)}), bf16[32,56,128]{2,1,0:T(8,128)(2,1)S(1)}, u32[]{:S(2)}, u32[]{:S(2)}) async-start(bf16[32,56,128]{2,1,0:T(8,128)(2,1)} %broadcast_in_dim.35), calls=%async_computation.2 | async-start | bytes 917504 | tf_op jit(solution)/shard_map/all_to_all | solution.py:490
  73.9 1.5 %collective-permute-start.6 = (bf16[128,128]{1,0:T(8,128)(2,1)S(1)}, bf16[128,128]{1,0:T(8,128)(2,1)S(1)}, u32[]{:S(2)}, u32[]{:S(2)}) collective-permute-start(bf16[128,128]{1,0:T(8,128)(2,1)S(1)} %get-tuple-element.63), channel_id=1, source_target_pairs={{0,8},{8,16},{16,24},{24,32},{32,40},{40,48},{48,56},{56,64},{64,7... | collective-permute-start | bytes 98312 | tf_op jit(solution)/shard_map/ppermute | solution.py:403
  75.4 3.4 %collective-permute-start.7 = (bf16[128,128]{1,0:T(8,128)(2,1)S(1)}, bf16[128,128]{1,0:T(8,128)(2,1)S(1)}, u32[]{:S(2)}, u32[]{:S(2)}) collective-permute-start(bf16[128,128]{1,0:T(8,128)(2,1)S(1)} %get-tuple-element.64), channel_id=1, source_target_pairs={{8,0},{16,8},{24,16},{32,24},{40,32},{48,40},{56,48},{64,56},{72,6... | collective-permute-start | bytes 98312 | tf_op jit(solution)/shard_map/ppermute | solution.py:403
  78.8 0.4 shard_map.113.w_ref
  79.2 1.3 %shard_map.109 = f32[1,4,64,512]{3,2,1,0:T(8,128)} custom-call(f32[1024,128]{1,0:T(8,128)S(1)} %get-tuple-element.54.r_ref), custom_call_target="tpu_custom_call" | custom-call | bytes 1048576 | tf_op jit(solution)/shard_map/pallas_call | solution.py:374
  80.5 0.0 collective-permute-done.6.lo_ref
  80.5 1.2 %collective-permute-done.7.hi_ref = bf16[128,128]{1,0:T(8,128)(2,1)S(1)} collective-permute-done((bf16[128,128]{1,0:T(8,128)(2,1)S(1)}, bf16[128,128]{1,0:T(8,128)(2,1)S(1)}, u32[]{:S(2)}, u32[]{:S(2)}) %collective-permute-start.7) | collective-permute-done | bytes 32800 | tf_op jit(solution)/shard_map/ppermute | solution.py:403
  81.7 3.3 %shard_map.114 = f32[1,4,64,512]{3,2,1,0:T(8,128)} custom-call(s32[4,26]{1,0:T(4,128)S(1)} %select_select_fusion.idx_ref, f32[1024,128]{1,0:T(8,128)S(1)} %get-tuple-element.62.a_ref.e_ref, bf16[128,128]{1,0:T(8,128)(2,1)S(1)} %collective-permute-done.6.lo_ref, bf16[128,128]{1,0:T(8,128)(2,1)S(1)} %collective-permute-done.7.hi_ref, ...), custom_call_target="tpu_custom_call" | custom-call | flops 603979776 | bytes 3211264 | tf_op jit(solution)/shard_map/pallas_call | solution.py:374
  85.0 0.5 all-to-all-done.2
  85.5 1.5 %shard_map.117 = (f32[27,64,64]{2,1,0:T(8,128)}, f32[27,64,64]{2,1,0:T(8,128)}) custom-call(bf16[1792,128]{1,0:T(8,128)(2,1)S(1)} %bitcast.3), custom_call_target="tpu_custom_call" | custom-call | bytes 1343488 | tf_op jit(solution)/shard_map/pallas_call | solution.py:374
  (3 shorter events, 0.0 us)
Async XLA Ops:
  0.6 11.2 %copy-start.1 = (pred[26]{0:T(512)(128)(4,1)S(1)}, pred[26]{0:T(512)(128)(4,1)}, u32[]{:S(2)}) copy-start(pred[26]{0:T(512)(128)(4,1)} %constant.36) | copy-start | bytes 82
  0.6 11.2 %copy-start.2 = (pred[26]{0:T(512)(128)(4,1)S(1)}, pred[26]{0:T(512)(128)(4,1)}, u32[]{:S(2)}) copy-start(pred[26]{0:T(512)(128)(4,1)} %constant.37) | copy-start | bytes 82
  0.7 11.2 %copy-start = (s32[4,26]{1,0:T(4,128)S(1)}, s32[4,26]{1,0:T(4,128)}, u32[]{:S(2)}) copy-start(s32[4,26]{1,0:T(4,128)} %param.12) | copy-start | bytes 1252
  3.1 10.8 %collective-permute-start = (bf16[128,128]{1,0:T(8,128)(2,1)S(1)}, bf16[128,128]{1,0:T(8,128)(2,1)S(1)}, u32[]{:S(2)}, u32[]{:S(2)}) collective-permute-start(bf16[128,128]{1,0:T(8,128)(2,1)S(1)} %get-tuple-element.39), channel_id=1, source_target_pairs={{0,8},{8,16},{16,24},{24,32},{32,40},{40,48},{48,56},{56,64},{64,7... | collective-permute-start | bytes 98312 | tf_op jit(solution)/shard_map/ppermute | solution.py:403
  5.2 8.7 %collective-permute-start.1 = (bf16[128,128]{1,0:T(8,128)(2,1)S(1)}, bf16[128,128]{1,0:T(8,128)(2,1)S(1)}, u32[]{:S(2)}, u32[]{:S(2)}) collective-permute-start(bf16[128,128]{1,0:T(8,128)(2,1)S(1)} %get-tuple-element.40), channel_id=1, source_target_pairs={{8,0},{16,8},{24,16},{32,24},{40,32},{48,40},{56,48},{64,56},{72,6... | collective-permute-start | bytes 98312 | tf_op jit(solution)/shard_map/ppermute | solution.py:403
  15.1 7.7 %collective-permute-start.2 = (bf16[128,128]{1,0:T(8,128)(2,1)S(1)}, bf16[128,128]{1,0:T(8,128)(2,1)S(1)}, u32[]{:S(2)}, u32[]{:S(2)}) collective-permute-start(bf16[128,128]{1,0:T(8,128)(2,1)S(1)} %get-tuple-element.48), channel_id=1, source_target_pairs={{0,8},{8,16},{16,24},{24,32},{32,40},{40,48},{48,56},{56,64},{64,7... | collective-permute-start | bytes 98312 | tf_op jit(solution)/shard_map/ppermute | solution.py:403
  15.2 7.6 %collective-permute-start.3 = (bf16[128,128]{1,0:T(8,128)(2,1)S(1)}, bf16[128,128]{1,0:T(8,128)(2,1)S(1)}, u32[]{:S(2)}, u32[]{:S(2)}) collective-permute-start(bf16[128,128]{1,0:T(8,128)(2,1)S(1)} %get-tuple-element.49), channel_id=1, source_target_pairs={{8,0},{16,8},{24,16},{32,24},{40,32},{48,40},{56,48},{64,56},{72,6... | collective-permute-start | bytes 98312 | tf_op jit(solution)/shard_map/ppermute | solution.py:403
  24.1 7.5 %collective-permute-start.4 = (bf16[128,128]{1,0:T(8,128)(2,1)S(1)}, bf16[128,128]{1,0:T(8,128)(2,1)S(1)}, u32[]{:S(2)}, u32[]{:S(2)}) collective-permute-start(bf16[128,128]{1,0:T(8,128)(2,1)S(1)} %get-tuple-element.56), channel_id=1, source_target_pairs={{0,8},{8,16},{16,24},{24,32},{32,40},{40,48},{48,56},{56,64},{64,7... | collective-permute-start | bytes 98312 | tf_op jit(solution)/shard_map/ppermute | solution.py:403
  24.2 7.4 %collective-permute-start.5 = (bf16[128,128]{1,0:T(8,128)(2,1)S(1)}, bf16[128,128]{1,0:T(8,128)(2,1)S(1)}, u32[]{:S(2)}, u32[]{:S(2)}) collective-permute-start(bf16[128,128]{1,0:T(8,128)(2,1)S(1)} %get-tuple-element.57), channel_id=1, source_target_pairs={{8,0},{16,8},{24,16},{32,24},{40,32},{48,40},{56,48},{64,56},{72,6... | collective-permute-start | bytes 98312 | tf_op jit(solution)/shard_map/ppermute | solution.py:403
  69.2 16.3 %all-to-all-start.2 = ((bf16[32,56,128]{2,1,0:T(8,128)(2,1)}), bf16[32,56,128]{2,1,0:T(8,128)(2,1)S(1)}, u32[]{:S(2)}, u32[]{:S(2)}) async-start(bf16[32,56,128]{2,1,0:T(8,128)(2,1)} %broadcast_in_dim.35), calls=%async_computation.2 | async-start | bytes 917504 | tf_op jit(solution)/shard_map/all_to_all | solution.py:490
  73.9 6.6 %collective-permute-start.6 = (bf16[128,128]{1,0:T(8,128)(2,1)S(1)}, bf16[128,128]{1,0:T(8,128)(2,1)S(1)}, u32[]{:S(2)}, u32[]{:S(2)}) collective-permute-start(bf16[128,128]{1,0:T(8,128)(2,1)S(1)} %get-tuple-element.63), channel_id=1, source_target_pairs={{0,8},{8,16},{16,24},{24,32},{32,40},{40,48},{48,56},{56,64},{64,7... | collective-permute-start | bytes 98312 | tf_op jit(solution)/shard_map/ppermute | solution.py:403
  75.4 6.3 %collective-permute-start.7 = (bf16[128,128]{1,0:T(8,128)(2,1)S(1)}, bf16[128,128]{1,0:T(8,128)(2,1)S(1)}, u32[]{:S(2)}, u32[]{:S(2)}) collective-permute-start(bf16[128,128]{1,0:T(8,128)(2,1)S(1)} %get-tuple-element.64), channel_id=1, source_target_pairs={{8,0},{16,8},{24,16},{32,24},{40,32},{48,40},{56,48},{64,56},{72,6... | collective-permute-start | bytes 98312 | tf_op jit(solution)/shard_map/ppermute | solution.py:403
